TPU v7x, 32 devices: a whole 2x2x4 slice. The times are simulated.
32 devices in a mesh: wide: 8 (over y, x, core), narrow: 4 (over z).
Axes of the slice: x: 2, y: 2, z: 4, core: 2. Of those that a mesh axis runs over, the one named last changes fastest.
Arguments:
- tokens: bfloat16 [2048, 2048], P('wide', 'narrow'), may hold values from -6 to 6
- gain_attn: bfloat16 [2048], P('narrow'), may hold values from 0.5 to 1.5
- w_query: bfloat16 [2048, 2048], P('wide', 'narrow'), may hold values from -0.1875 to 0.1875
- w_key: bfloat16 [2048, 2048], P('wide', 'narrow'), may hold values from -0.1875 to 0.1875
- w_value: bfloat16 [2048, 2048], P('wide', 'narrow'), may hold values from -0.125 to 0.125
- w_out: bfloat16 [2048, 2048], P('wide', 'narrow'), may hold values from -0.5 to 0.5
- gain_ffn: bfloat16 [2048], P('narrow'), may hold values from 0.5 to 1.5
- w_router: bfloat16 [2048, 4], P('wide'), may hold values from -0.09375 to 0.09375
- w_gate: bfloat16 [2048, 4, 5632], P('wide', None, 'narrow'), may hold values from -0.125 to 0.125
- w_up: bfloat16 [2048, 4, 5632], P('wide', None, 'narrow'), may hold values from -0.125 to 0.125
- w_down: bfloat16 [2048, 4, 5632], P('wide', None, 'narrow'), may hold values from -0.109375 to 0.109375
- segment: int32 [8, 256], P('wide'), may hold values from 0 to 12, never falling along the last dimension, each value on 1 to 102 neighbouring positions
- parents: int32 [8, 13], P('wide'), may hold values from 0 to 4, as said below
- expert_ids: int32 [2048, 2], P('wide'), may hold values from 0 to 3, all different within a row
- slot_order: int32 [8, 256], P('wide'), may hold values from 0 to 255, each once within a row
- cotangent: bfloat16 [2048, 2048], P('wide', 'narrow'), may hold values from -6 to 6
Outputs:
- output: bfloat16 [2048, 2048], P('wide', 'narrow')
- grad_tokens: float32 [2048, 2048], P('wide', 'narrow')
- grad_gain_attn: float32 [2048], P('narrow')
- grad_w_query: float32 [2048, 2048], P('wide', 'narrow')
- grad_w_key: float32 [2048, 2048], P('wide', 'narrow')
- grad_w_value: float32 [2048, 2048], P('wide', 'narrow')
- grad_w_out: float32 [2048, 2048], P('wide', 'narrow')
- grad_gain_ffn: float32 [2048], P('narrow')
- grad_w_router: float32 [2048, 4], P('wide')
- grad_w_gate: float32 [2048, 4, 5632], P('wide', None, 'narrow')
- grad_w_up: float32 [2048, 4, 5632], P('wide', None, 'narrow')
- grad_w_down: float32 [2048, 4, 5632], P('wide', None, 'narrow')
Inputs may be any that keep to these rules, and one draw needn't show every extreme that they name: In every tree, segment 0 is the trunk and has entry 0; segments 1 to 4 have parent 0; segments 5 to 12 have parents among 1 to 4, two on each. `segment`: segment numbers never fall within a tree; all 13 segments are present. `expert_ids`: the two experts of a token differ. `slot_order`: each row is a permutation of the numbers below 256.
All inputs are finite; a program needn't handle non-finite values.
Results may differ from a plain program's by a relative error of at most 0.03.
Values may be sent and summed in bfloat16 or wider, within the bound.
A program may use at most 448 MiB of HBM per device.

v0:
```python
import jax
import jax.numpy as jnp
from jax import lax
from jax.sharding import PartitionSpec as P

HEAD_DIM = 128
EXPERTS = 4
SEGS = 13
CAP = 144


HIGH_PREC = lax.Precision.HIGHEST
NORM_EPS = 1e-05
NEG_FILL = -1e30
ROPE_BASE = 10000.0


def take_cols(full_rows, narrow_at, part_width):
    return lax.dynamic_slice_in_dim(full_rows, narrow_at * part_width, part_width, 1)


def tree_layout(segment_row, parent_row):
    seg_ids = jnp.arange(SEGS, dtype=jnp.int32)
    member = (segment_row[:, None] == seg_ids[None, :]).astype(jnp.int32)
    parent_of = (parent_row[:, None] == seg_ids[None, :]) & (seg_ids[:, None] != 0)
    itself = seg_ids[:, None] == seg_ids[None, :]
    reach = itself
    for _ in range(3):
        reach = itself | jnp.any(parent_of[:, :, None] & reach[None, :, :], axis=1)
    lengths = jnp.sum(member, 0)
    starts = jnp.sum(jnp.where(seg_ids[None, :] < seg_ids[:, None], lengths[None, :], 0), 1)
    before = jnp.sum(jnp.where(reach, lengths[None, :], 0), 1) - lengths
    places = jnp.sum(member * (before - starts)[None, :], 1) + jnp.arange(
        segment_row.shape[0], dtype=jnp.int32
    )
    return (member.astype(jnp.float32), reach.astype(jnp.float32), places.astype(jnp.float32))


def visible(member, reach, first_row, block_rows):
    lineage = jnp.dot(member, reach, precision=HIGH_PREC)
    shared = jnp.dot(lineage, member.T, precision=HIGH_PREC) > 0.5
    row_at = first_row + jnp.arange(block_rows, dtype=jnp.int32)
    col_at = jnp.arange(member.shape[0], dtype=jnp.int32)
    return shared & (col_at[None, :] <= row_at[:, None])


def rotate(vectors, places, direction):
    half_dim = vectors.shape[-1] // 2
    freqs = ROPE_BASE ** (-2.0 * jnp.arange(half_dim, dtype=jnp.float32) / vectors.shape[-1])
    angles = places[:, None] * freqs[None, :]
    cosines = jnp.cos(angles)[:, None, :]
    sine_vals = direction * jnp.sin(angles)[:, None, :]
    first_half = vectors[..., :half_dim]
    second_half = vectors[..., half_dim:]
    return jnp.concatenate(
        [
            first_half * cosines - second_half * sine_vals,
            second_half * cosines + first_half * sine_vals,
        ],
        -1,
    )


def gate_pair(logits, hot_first, hot_second):
    chances = jax.nn.softmax(logits, axis=-1)
    first_share = jnp.sum(chances * hot_first, 1)
    second_share = jnp.sum(chances * hot_second, 1)
    pair_total = first_share + second_share
    return (first_share / pair_total, second_share / pair_total)


def route(expert_row, slot_rank):
    token_count = expert_row.shape[0]
    expert_range = jnp.arange(EXPERTS, dtype=jnp.int32)
    hot_first = (expert_row[:, 0:1] == expert_range[None, :]).astype(jnp.float32)
    hot_second = (expert_row[:, 1:2] == expert_range[None, :]).astype(jnp.float32)
    earlier = (slot_rank[None, :] < slot_rank[:, None]).astype(jnp.float32)
    ahead_first = jnp.sum(jnp.dot(earlier, hot_first, precision=HIGH_PREC) * hot_first, 1)
    ahead_second = jnp.sum(
        (jnp.dot(earlier, hot_second, precision=HIGH_PREC) + jnp.sum(hot_first, 0)[None, :])
        * hot_second,
        1,
    )
    slot_index = jnp.stack([ahead_first, ahead_second], 1).astype(jnp.int32)
    kept_mask = slot_index < CAP
    flat_slot = jnp.where(kept_mask, expert_row * CAP + slot_index, EXPERTS * CAP)
    token_index = jnp.broadcast_to(
        jnp.arange(token_count, dtype=jnp.int32)[:, None], (token_count, 2)
    )
    slot_table = (
        jnp.full((EXPERTS * CAP + 1,), token_count, jnp.int32)
        .at[flat_slot.reshape(-1)]
        .set(token_index.reshape(-1))[: EXPERTS * CAP]
    )
    return (hot_first, hot_second, kept_mask.astype(jnp.float32), flat_slot, slot_table)


def attend(queries, keys_all, values_all, member, reach):
    token_count = queries.shape[0]
    block_rows = min(512, token_count)
    scale_factor = queries.shape[-1] ** (-0.5)

    def one_block(block_id):
        first_row = block_id * block_rows
        scores = (
            jnp.einsum("bhd,thd->hbt", queries, keys_all, preferred_element_type=jnp.float32)
            * scale_factor
        )
        scores = jnp.where(visible(member, reach, first_row, block_rows)[None], scores, NEG_FILL)
        row_peak = jnp.max(scores, -1, keepdims=True)
        exp_scores = jnp.exp(scores - row_peak)
        row_total = jnp.sum(exp_scores, -1, keepdims=True)
        weights_low = (exp_scores / row_total).astype(jnp.bfloat16)
        mixed = jnp.einsum(
            "hbt,thd->bhd", weights_low, values_all, preferred_element_type=jnp.float32
        )
        return (mixed.astype(jnp.bfloat16), (row_peak + jnp.log(row_total))[..., 0])

    block_outs, log_totals = lax.map(
        one_block, jnp.arange(token_count // block_rows, dtype=jnp.int32)
    )
    return (block_outs.reshape(token_count, -1), log_totals)


def attend_back(queries, keys_all, values_all, grad_out, log_totals, member, reach):
    token_count = queries.shape[0]
    block_rows = min(512, token_count)
    scale_factor = queries.shape[-1] ** (-0.5)

    def one_block(carry, items):
        grad_keys, grad_values = carry
        block_id, log_block = items
        first_row = block_id * block_rows
        scores = (
            jnp.einsum("bhd,thd->hbt", queries, keys_all, preferred_element_type=jnp.float32)
            * scale_factor
        )
        scores = jnp.where(visible(member, reach, first_row, block_rows)[None], scores, NEG_FILL)
        weights_full = jnp.exp(scores - log_block[..., None])
        weights_low = weights_full.astype(jnp.bfloat16)
        grad_weights = jnp.einsum(
            "bhd,thd->hbt", grad_out, values_all, preferred_element_type=jnp.float32
        )
        grad_scores = (
            weights_full * (grad_weights - jnp.sum(weights_full * grad_weights, -1, keepdims=True))
        ).astype(jnp.bfloat16)
        grad_query_block = (
            jnp.einsum("hbt,thd->bhd", grad_scores, keys_all, preferred_element_type=jnp.float32)
            * scale_factor
        )
        grad_keys = (
            grad_keys
            + jnp.einsum("hbt,bhd->thd", grad_scores, queries, preferred_element_type=jnp.float32)
            * scale_factor
        )
        grad_values = grad_values + jnp.einsum(
            "hbt,bhd->thd", weights_low, grad_out, preferred_element_type=jnp.float32
        )
        return ((grad_keys, grad_values), grad_query_block)

    zero_grad = jnp.zeros(keys_all.shape, jnp.float32)
    block_ids = jnp.arange(token_count // block_rows, dtype=jnp.int32)
    (grad_keys, grad_values), grad_blocks = lax.scan(
        one_block, (zero_grad, zero_grad), (block_ids, log_totals)
    )
    return (grad_blocks.reshape(queries.shape), grad_keys, grad_values)


def per_device(
    tokens,
    gain_attn,
    w_query,
    w_key,
    w_value,
    w_out,
    gain_ffn,
    w_router,
    w_gate,
    w_up,
    w_down,
    segment,
    parents,
    expert_ids,
    slot_order,
    cotangent,
):
    narrow_count = lax.axis_size("narrow")
    wide_count = lax.axis_size("wide")
    narrow_at = lax.axis_index("narrow")
    token_count, part_width = tokens.shape
    full_width = part_width * narrow_count
    gains_local = jnp.stack([gain_attn, gain_ffn])
    tokens_full, grad_full, gains_full = (
        lax.all_gather(tokens, "narrow", axis=1, tiled=True),
        lax.all_gather(cotangent, "narrow", axis=1, tiled=True),
        lax.all_gather(gains_local, "narrow", axis=1, tiled=True),
    )
    weight_set = (w_query, w_key, w_value, w_out, w_router, w_gate, w_up, w_down)
    query_w, key_w, value_w, out_w, router_w, gate_w, up_w, down_w = (
        lax.all_gather(weight_set[0], "wide", axis=0, tiled=True),
        lax.all_gather(weight_set[1], "wide", axis=0, tiled=True),
        lax.all_gather(weight_set[2], "wide", axis=0, tiled=True),
        lax.all_gather(weight_set[3], "wide", axis=0, tiled=True),
        lax.all_gather(weight_set[4], "wide", axis=0, tiled=True),
        lax.all_gather(weight_set[5], "wide", axis=0, tiled=True),
        lax.all_gather(weight_set[6], "wide", axis=0, tiled=True),
        lax.all_gather(weight_set[7], "wide", axis=0, tiled=True),
    )
    gain_first = gains_full[0].astype(jnp.float32)
    gain_second = gains_full[1].astype(jnp.float32)
    gain_first_loc = gain_attn.astype(jnp.float32)
    gain_second_loc = gain_ffn.astype(jnp.float32)
    member, reach, places = tree_layout(segment[0], parents[0])
    hot_first, hot_second, kept_mask, flat_slot, slot_table = route(expert_ids, slot_order[0])
    inputs_full = tokens_full.astype(jnp.float32)
    scale_first = lax.rsqrt(jnp.mean(inputs_full * inputs_full, -1, keepdims=True) + NORM_EPS)
    normed_first = inputs_full * scale_first
    hidden_first = (normed_first * gain_first).astype(jnp.bfloat16)
    heads_local = query_w.shape[1] // HEAD_DIM
    query_raw = jnp.dot(hidden_first, query_w, preferred_element_type=jnp.float32)
    key_raw = jnp.dot(hidden_first, key_w, preferred_element_type=jnp.float32)
    queries = rotate(query_raw.reshape(token_count, heads_local, HEAD_DIM), places, 1.0).astype(
        jnp.bfloat16
    )
    keys_all = rotate(key_raw.reshape(token_count, heads_local, HEAD_DIM), places, 1.0).astype(
        jnp.bfloat16
    )
    values_all = (
        jnp.dot(hidden_first, value_w, preferred_element_type=jnp.float32)
        .astype(jnp.bfloat16)
        .reshape(token_count, heads_local, HEAD_DIM)
    )
    attended, log_totals = attend(queries, keys_all, values_all, member, reach)
    branch_part = jnp.dot(attended, out_w.T, preferred_element_type=jnp.float32)
    branch_local = lax.psum_scatter(
        branch_part.astype(jnp.bfloat16), "narrow", scatter_dimension=1, tiled=True
    ).astype(jnp.float32)
    middle = tokens.astype(jnp.float32) + branch_local
    middle_full = lax.all_gather(middle.astype(jnp.bfloat16), "narrow", axis=1, tiled=True).astype(
        middle.dtype
    )
    scale_second = lax.rsqrt(jnp.mean(middle_full * middle_full, -1, keepdims=True) + NORM_EPS)
    normed_second = middle_full * scale_second
    hidden_second = (normed_second * gain_second).astype(jnp.bfloat16)
    logits = jnp.dot(hidden_second, router_w, preferred_element_type=jnp.float32)
    share_first, share_second = gate_pair(logits, hot_first, hot_second)
    weight_first = kept_mask[:, 0] * share_first
    weight_second = kept_mask[:, 1] * share_second
    padded_hidden = jnp.concatenate([hidden_second, jnp.zeros((1, full_width), jnp.bfloat16)], 0)
    dispatched = jnp.take(padded_hidden, slot_table, axis=0).reshape(EXPERTS, CAP, full_width)
    gate_pre = jnp.einsum("ecd,def->ecf", dispatched, gate_w, preferred_element_type=jnp.float32)
    up_pre = jnp.einsum("ecd,def->ecf", dispatched, up_w, preferred_element_type=jnp.float32)
    sigmoid_gate = jax.nn.sigmoid(gate_pre)
    silu_gate = gate_pre * sigmoid_gate
    activated = (silu_gate * up_pre).astype(jnp.bfloat16)
    expert_part = jnp.einsum("ecf,def->ecd", activated, down_w, preferred_element_type=jnp.float32)
    expert_local = (
        lax.psum_scatter(
            expert_part.astype(jnp.bfloat16), "narrow", scatter_dimension=2, tiled=True
        )
        .astype(jnp.float32)
        .reshape(EXPERTS * CAP, part_width)
    )
    padded_expert = jnp.concatenate([expert_local, jnp.zeros((1, part_width), jnp.float32)], 0)
    picked_first = jnp.take(padded_expert, flat_slot[:, 0], axis=0)
    picked_second = jnp.take(padded_expert, flat_slot[:, 1], axis=0)
    output = (
        middle + weight_first[:, None] * picked_first + weight_second[:, None] * picked_second
    ).astype(jnp.bfloat16)
    query_w, key_w, value_w, out_w, router_w, gate_w, up_w, down_w = (
        lax.all_gather(weight_set[0], "wide", axis=0, tiled=True),
        lax.all_gather(weight_set[1], "wide", axis=0, tiled=True),
        lax.all_gather(weight_set[2], "wide", axis=0, tiled=True),
        lax.all_gather(weight_set[3], "wide", axis=0, tiled=True),
        lax.all_gather(weight_set[4], "wide", axis=0, tiled=True),
        lax.all_gather(weight_set[5], "wide", axis=0, tiled=True),
        lax.all_gather(weight_set[6], "wide", axis=0, tiled=True),
        lax.all_gather(weight_set[7], "wide", axis=0, tiled=True),
    )
    grad_local = cotangent.astype(jnp.float32)
    grad_rows = grad_full.astype(jnp.float32)
    entry_weights = jnp.stack([weight_first, weight_second], 1).reshape(-1)
    table_weight = (
        jnp.zeros((EXPERTS * CAP + 1,), jnp.float32)
        .at[flat_slot.reshape(-1)]
        .set(entry_weights)[: EXPERTS * CAP]
    )
    padded_grad = jnp.concatenate([grad_rows, jnp.zeros((1, full_width), jnp.float32)], 0)
    grad_expert = (
        (table_weight[:, None] * jnp.take(padded_grad, slot_table, axis=0))
        .astype(jnp.bfloat16)
        .reshape(EXPERTS, CAP, full_width)
    )
    grad_act = jnp.einsum("ecd,def->ecf", grad_expert, down_w, preferred_element_type=jnp.float32)
    grad_gate_pre = (
        grad_act * up_pre * sigmoid_gate * (1.0 + gate_pre * (1.0 - sigmoid_gate))
    ).astype(jnp.bfloat16)
    grad_up_pre = (grad_act * silu_gate).astype(jnp.bfloat16)
    grad_dispatched = jnp.einsum(
        "ecf,def->ecd", grad_gate_pre, gate_w, preferred_element_type=jnp.float32
    ) + jnp.einsum("ecf,def->ecd", grad_up_pre, up_w, preferred_element_type=jnp.float32)
    grad_hidden_part = (
        jnp.zeros((token_count + 1, full_width), jnp.float32)
        .at[slot_table]
        .add(grad_dispatched.reshape(EXPERTS * CAP, full_width))[:token_count]
    )
    grad_share_first = jnp.sum(grad_local * picked_first, 1)
    grad_share_second = jnp.sum(grad_local * picked_second, 1)
    stat_second = jnp.sum(normed_second * gain_second * grad_hidden_part, 1)
    stat_tiles = jnp.tile(stat_second[:, None], (1, narrow_count))
    share_tiles = jnp.tile(jnp.stack([grad_share_first, grad_share_second], 1), (1, narrow_count))
    grad_hidden_loc, stat_copies, share_copies = (
        lax.psum_scatter(
            grad_hidden_part.astype(jnp.bfloat16), "narrow", scatter_dimension=1, tiled=True
        ).astype(jnp.float32),
        lax.psum_scatter(
            stat_tiles.astype(jnp.bfloat16), "narrow", scatter_dimension=1, tiled=True
        ).astype(jnp.float32),
        lax.psum_scatter(
            share_tiles.astype(jnp.bfloat16), "narrow", scatter_dimension=1, tiled=True
        ).astype(jnp.float32),
    )
    _, pull_gates = jax.vjp(lambda logit_in: gate_pair(logit_in, hot_first, hot_second), logits)
    (grad_logits,) = pull_gates(
        (kept_mask[:, 0] * share_copies[:, 0], kept_mask[:, 1] * share_copies[:, 1])
    )
    grad_logits_low = grad_logits.astype(jnp.bfloat16)
    grad_router_rows = jnp.dot(grad_logits_low, router_w.T, preferred_element_type=jnp.float32)
    stat_total = stat_copies[:, 0] + jnp.sum(normed_second * gain_second * grad_router_rows, 1)
    grad_hidden_loc = grad_hidden_loc + take_cols(grad_router_rows, narrow_at, part_width)
    normed_second_loc = take_cols(normed_second, narrow_at, part_width)
    grad_gain_second = jnp.sum(grad_hidden_loc * normed_second_loc, 0)
    grad_middle = grad_local + scale_second * (
        gain_second_loc * grad_hidden_loc - normed_second_loc * stat_total[:, None] / full_width
    )
    grad_router_w = jnp.dot(hidden_second.T, grad_logits_low, preferred_element_type=jnp.float32)
    grad_branch = lax.all_gather(grad_middle.astype(jnp.bfloat16), "narrow", axis=1, tiled=True)
    grad_attended = jnp.dot(grad_branch, out_w, preferred_element_type=jnp.float32).astype(
        jnp.bfloat16
    )
    grad_out_w = jnp.dot(grad_branch.T, attended, preferred_element_type=jnp.float32)
    grad_queries, grad_keys, grad_values = attend_back(
        queries,
        keys_all,
        values_all,
        grad_attended.reshape(token_count, heads_local, HEAD_DIM),
        log_totals,
        member,
        reach,
    )
    grad_query_raw = (
        rotate(grad_queries, places, -1.0).reshape(token_count, -1).astype(jnp.bfloat16)
    )
    grad_key_raw = rotate(grad_keys, places, -1.0).reshape(token_count, -1).astype(jnp.bfloat16)
    grad_value_raw = grad_values.reshape(token_count, -1).astype(jnp.bfloat16)
    grad_query_w = jnp.dot(hidden_first.T, grad_query_raw, preferred_element_type=jnp.float32)
    grad_key_w = jnp.dot(hidden_first.T, grad_key_raw, preferred_element_type=jnp.float32)
    grad_value_w = jnp.dot(hidden_first.T, grad_value_raw, preferred_element_type=jnp.float32)
    grad_hidden_first = (
        jnp.dot(grad_query_raw, query_w.T, preferred_element_type=jnp.float32)
        + jnp.dot(grad_key_raw, key_w.T, preferred_element_type=jnp.float32)
        + jnp.dot(grad_value_raw, value_w.T, preferred_element_type=jnp.float32)
    )
    stat_first = jnp.sum(normed_first * gain_first * grad_hidden_first, 1)
    grad_first_loc, stat_first_copies = (
        lax.psum_scatter(
            grad_hidden_first.astype(jnp.bfloat16), "narrow", scatter_dimension=1, tiled=True
        ).astype(jnp.float32),
        lax.psum_scatter(
            jnp.tile(stat_first[:, None], (1, narrow_count)).astype(jnp.bfloat16),
            "narrow",
            scatter_dimension=1,
            tiled=True,
        ).astype(jnp.float32),
    )
    normed_first_loc = take_cols(normed_first, narrow_at, part_width)
    grad_gain_first = jnp.sum(grad_first_loc * normed_first_loc, 0)
    grad_tokens = grad_middle + scale_first * (
        gain_first_loc * grad_first_loc - normed_first_loc * stat_first_copies / full_width
    )
    gain_copies = jnp.broadcast_to(
        jnp.stack([grad_gain_first, grad_gain_second])[None], (wide_count, 2, part_width)
    )
    gate_term = jnp.einsum(
        "ecd,ecf->def", dispatched, grad_gate_pre, preferred_element_type=jnp.float32
    )
    up_term = jnp.einsum(
        "ecd,ecf->def", dispatched, grad_up_pre, preferred_element_type=jnp.float32
    )
    down_term = jnp.einsum(
        "ecd,ecf->def", grad_expert, activated, preferred_element_type=jnp.float32
    )
    expert_summed = lax.psum_scatter(
        jnp.stack([gate_term, up_term, down_term], 1), "wide", scatter_dimension=0, tiled=True
    )
    summed = (
        lax.psum_scatter(grad_query_w, "wide", scatter_dimension=0, tiled=True),
        lax.psum_scatter(grad_key_w, "wide", scatter_dimension=0, tiled=True),
        lax.psum_scatter(grad_value_w, "wide", scatter_dimension=0, tiled=True),
        lax.psum_scatter(grad_out_w, "wide", scatter_dimension=0, tiled=True),
        lax.psum_scatter(grad_router_w, "wide", scatter_dimension=0, tiled=True),
        lax.psum_scatter(gain_copies, "wide", scatter_dimension=0, tiled=True),
    )
    return (
        output,
        grad_tokens,
        summed[5][0, 0],
        summed[0],
        summed[1],
        summed[2],
        summed[3],
        summed[5][0, 1],
        summed[4],
        expert_summed[:, 0],
        expert_summed[:, 1],
        expert_summed[:, 2],
    )


def solution(mesh):
    return jax.shard_map(
        per_device,
        mesh=mesh,
        in_specs=(
            P("wide", "narrow"),
            P("narrow"),
            P("wide", "narrow"),
            P("wide", "narrow"),
            P("wide", "narrow"),
            P("wide", "narrow"),
            P("narrow"),
            P("wide", None),
            P("wide", None, "narrow"),
            P("wide", None, "narrow"),
            P("wide", None, "narrow"),
            P("wide", None),
            P("wide", None),
            P("wide", None),
            P("wide", None),
            P("wide", "narrow"),
        ),
        out_specs=(
            P("wide", "narrow"),
            P("wide", "narrow"),
            P("narrow"),
            P("wide", "narrow"),
            P("wide", "narrow"),
            P("wide", "narrow"),
            P("wide", "narrow"),
            P("narrow"),
            P("wide", None),
            P("wide", None, "narrow"),
            P("wide", None, "narrow"),
            P("wide", None, "narrow"),
        ),
        check_vma=False,
    )
```

profile of v0, /device:TPU:0, one launch (start us, length us, event | category | flops | bytes accessed | tf_op | source)
XLA Modules:
  0.0 1888.5 jit_solution(1243104091451810518)
XLA Ops:
  17.0 13.8 all_gather.48
  32.0 8.2 all-gather.12.cloned.1.call-done
  41.8 28.0 %all-gather.16.cloned.1.call-done = bf16[2048,512]{1,0:T(8,128)(2,1)} async-done(((bf16[256,512]{1,0:T(8,128)(2,1)}), bf16[2048,512]{1,0:T(8,128)(2,1)}) %all-gather.16.cloned.1.call-update) | async-done | bytes 2097168 | tf_op jit(solution)/shard_map/all_gather | solution.py:200
  69.8 2.7 fusion.79
  72.7 26.9 %all-gather.18.cloned.1.call-done = bf16[2048,512]{1,0:T(8,128)(2,1)} async-done(((bf16[256,512]{1,0:T(8,128)(2,1)}), bf16[2048,512]{1,0:T(8,128)(2,1)}) %all-gather.18.cloned.1.call-update) | async-done | bytes 2097168 | tf_op jit(solution)/shard_map/all_gather | solution.py:201
  104.5 24.8 %all-gather.14.cloned.1.call-done = bf16[2048,512]{1,0:T(8,128)(2,1)} async-done(((bf16[256,512]{1,0:T(8,128)(2,1)}), bf16[2048,512]{1,0:T(8,128)(2,1)}) %all-gather.14.cloned.1.call-update) | async-done | bytes 2097168 | tf_op jit(solution)/shard_map/all_gather | solution.py:202
  132.4 26.6 %all-gather.20.cloned.1.call-done = bf16[2048,512]{1,0:T(8,128)(2,1)} async-done(((bf16[256,512]{1,0:T(8,128)(2,1)}), bf16[2048,512]{1,0:T(8,128)(2,1)}) %all-gather.20.cloned.1.call-update) | async-done | bytes 2097168 | tf_op jit(solution)/shard_map/all_gather | solution.py:203
  158.9 3.5 convolution_convert_fusion.1
  163.2 26.5 %reduce-scatter.13.cloned.1.call-done = bf16[256,512]{1,0:T(8,128)(2,1)} async-done(((bf16[256,2048]{1,0:T(8,128)(2,1)}), bf16[256,512]{1,0:T(8,128)(2,1)}) %reduce-scatter.13.cloned.1.call-update) | async-done | bytes 262160 | tf_op jit(solution)/shard_map/reduce_scatter | solution.py:235
  203.8 8.9 all_gather.54
  212.9 5.1 all-gather.30.cloned.1.call-done
  219.5 28.2 %all-gather.22.cloned.1.call-done = bf16[256,2048]{1,0:T(8,128)(2,1)} async-done(((bf16[256,512]{1,0:T(8,128)(2,1)}), bf16[256,2048]{1,0:T(8,128)(2,1)}) %all-gather.22.cloned.1.call-update) | async-done | bytes 1048592 | tf_op jit(solution)/shard_map/all_gather | solution.py:239
  249.2 2.9 convert_multiply_fusion
  263.0 3.9 gather_fusion
  266.9 4.4 gather_fusion.1
  271.3 95.0 %all-gather.26.cloned.1.call-done = bf16[2048,4,1408]{2,0,1:T(8,128)(2,1)} async-done(((bf16[256,4,1408]{2,0,1:T(8,128)(2,1)}), bf16[2048,4,1408]{2,0,1:T(8,128)(2,1)}) %all-gather.26.cloned.1.call-update) | async-done | bytes 23068688 | tf_op jit(solution)/shard_map/all_gather | solution.py:206
  366.3 14.0 fusion.3
  380.4 104.9 %all-gather.24.cloned.1.call-done = bf16[2048,4,1408]{2,0,1:T(8,128)(2,1)} async-done(((bf16[256,4,1408]{2,0,1:T(8,128)(2,1)}), bf16[2048,4,1408]{2,0,1:T(8,128)(2,1)}) %all-gather.24.cloned.1.call-update) | async-done | bytes 23068688 | tf_op jit(solution)/shard_map/all_gather | solution.py:205
  485.3 13.2 fusion.4
  498.5 105.4 %all-gather.28.cloned.1.call-done = bf16[2048,4,1408]{2,0,1:T(8,128)(2,1)} async-done(((bf16[256,4,1408]{2,0,1:T(8,128)(2,1)}), bf16[2048,4,1408]{2,0,1:T(8,128)(2,1)}) %all-gather.28.cloned.1.call-update) | async-done | bytes 23068688 | tf_op jit(solution)/shard_map/all_gather | solution.py:207
  603.9 17.6 multiply_convert_fusion.1
  621.5 22.6 %convolution_convert_fusion = bf16[4,144,2048]{2,1,0:T(8,128)(2,1)} fusion(bf16[4,144,1408]{2,1,0:T(8,128)(2,1)} %get-tuple-element.134, bf16[2048,4,1408]{2,0,1:T(8,128)(2,1)} %all-gather.28.cloned.1.call-done), kind=kOutput, calls=%fused_computation.21 | convolution fusion | flops 3323068416 | bytes 27049984 | tf_op jit(solution)/shard_map/ecf,def->ecd/dot_general | solution.py:256
  647.7 14.3 fusion.88
  662.0 14.8 convolution_add_fusion
  676.8 16.2 scatter_custom_fusion.2
  695.8 20.0 %convolution_bitcast_fusion.1 = f32[2048,1,4,1408]{0,3,2,1:T(8,128)} fusion(bf16[4,144,1408]{2,1,0:T(8,128)(2,1)} %get-tuple-element.132, bf16[4,144,2048]{2,1,0:T(8,128)(2,1)S(1)} %bitcast.118, pred[4,144]{1,0:T(4,128)(4,1)S(1)} %compare_and_fusion), kind=kOutput, calls=%fused_computation.9 | convolution fusion | flops 3323068416 | bytes 50119232 | tf_op jit(solution)/shard_map/ecd,ecf->def/dot_general | solution.py:387
  723.5 11.7 all-reduce.3
  736.8 3.7 multiply_reduce_fusion.2
  740.5 8.4 all-reduce.4
  749.5 3.0 fusion.80
  752.7 19.6 %convolution_bitcast_fusion.2 = f32[2048,1,4,1408]{0,3,2,1:T(8,128)} fusion(bf16[4,144,1408]{2,1,0:T(8,128)(2,1)} %get-tuple-element.133, bf16[4,144,2048]{2,1,0:T(8,128)(2,1)S(1)} %bitcast.119, pred[4,144]{1,0:T(4,128)(4,1)S(1)} %copy-done.33), kind=kOutput, calls=%fused_computation.10 | convolution fusion | flops 3323068416 | bytes 50119232 | tf_op jit(solution)/shard_map/ecd,ecf->def/dot_general | solution.py:384
  772.4 20.2 %convolution_bitcast_fusion = f32[2048,1,4,1408]{0,3,2,1:T(8,128)} fusion(bf16[4,144,1408]{2,1,0:T(8,128)(2,1)} %get-tuple-element.134, f32[4,144,2048]{2,1,0:T(8,128)} %bitcast.121, f32[4,144]{1,0:T(4,128)S(1)} %copy-done.42, pred[4,144]{1,0:T(4,128)(4,1)S(1)} %copy-done.33), kind=kOutput, calls=%fused_computation.8 | convolution fusion | flops 3325427712 | bytes 52480832 | tf_op jit(solution)/shard_map/ecd,ecf->def/dot_general | solution.py:390
  809.1 89.4 %pad_maximum_fusion = f32[2048,3,4,1408]{0,3,2,1:T(8,128)} fusion(f32[2048,1,4,1408]{0,3,2,1:T(8,128)} %convolution_bitcast_fusion, f32[2048,1,4,1408]{0,3,2,1:T(8,128)} %convolution_bitcast_fusion.1, f32[2048,1,4,1408]{0,3,2,1:T(8,128)} %convolution_bitcast_fusion.2), kind=kLoop, calls=%fused_computation.7 | loop fusion | flops 69206016 | bytes 276824064 | tf_op jit(solution)/shard_map/stack | solution.py:394
  898.6 4.1 fusion.90
  902.7 4.2 fusion.75
  907.0 4.1 fusion.76
  911.2 3.1 fusion.77
  917.3 11.3 all-reduce.5
  931.2 22.4 %all-reduce.6 = f32[8,2,512]{2,1,0:T(2,128)S(1)} all-reduce(f32[8,2,512]{2,1,0:T(2,128)S(1)} %broadcast_in_dim.134), channel_id=9, replica_groups=mesh['wide'=8,'narrow'=4] {'wide'}, use_global_device_ids=true, to_apply=%region_37.39.clone | all-reduce | flops 8192 | bytes 65536
  954.8 705.1 %reduce-scatter.29.cloned.1.call-done = f32[256,3,4,1408]{0,3,2,1:T(8,128)} async-done(((f32[2048,3,4,1408]{0,3,2,1:T(8,128)}), f32[256,3,4,1408]{0,3,2,1:T(8,128)}) %reduce-scatter.29.cloned.1.call-update) | async-done | bytes 17301520 | tf_op jit(solution)/shard_map/reduce_scatter | solution.py:393
  1659.9 12.7 slice_bitcast_fusion
  1672.6 7.7 copy.131
  1680.4 7.4 copy.130
  1687.8 7.4 copy.129
  1695.2 20.2 %reduce-scatter.27.cloned.1.call-done = f32[256,512]{1,0:T(8,128)} async-done(((f32[2048,512]{1,0:T(8,128)}), f32[256,512]{1,0:T(8,128)}) %reduce-scatter.27.cloned.1.call-update) | async-done | bytes 524304 | tf_op jit(solution)/shard_map/reduce_scatter | solution.py:400
  1715.4 55.3 %reduce-scatter.25.cloned.1.call-done = f32[256,512]{1,0:T(8,128)} async-done(((f32[2048,512]{1,0:T(8,128)}), f32[256,512]{1,0:T(8,128)}) %reduce-scatter.25.cloned.1.call-update) | async-done | bytes 524304 | tf_op jit(solution)/shard_map/reduce_scatter | solution.py:399
  1770.7 55.5 %reduce-scatter.23.cloned.1.call-done = f32[256,512]{1,0:T(8,128)} async-done(((f32[2048,512]{1,0:T(8,128)}), f32[256,512]{1,0:T(8,128)}) %reduce-scatter.23.cloned.1.call-update) | async-done | bytes 524304 | tf_op jit(solution)/shard_map/reduce_scatter | solution.py:398
  1826.2 55.3 %reduce-scatter.21.cloned.1.call-done = f32[256,512]{1,0:T(8,128)} async-done(((f32[2048,512]{1,0:T(8,128)}), f32[256,512]{1,0:T(8,128)}) %reduce-scatter.21.cloned.1.call-update) | async-done | bytes 524304 | tf_op jit(solution)/shard_map/reduce_scatter | solution.py:397
  (346 shorter events, 87.9 us)
Async XLA Ops:
  7.2 33.1 %all-gather.12.cloned.1.call-start = ((), (), s32[]{:S(2)}) async-start(), calls=%async_computation.10 | async-start | bytes 1310720 | tf_op jit(solution)/shard_map/all_gather | solution.py:194
  7.9 61.9 %all-gather.16.cloned.1.call-start = ((), (), s32[]{:S(2)}) async-start(), calls=%async_computation.12 | async-start | bytes 2359296 | tf_op jit(solution)/shard_map/all_gather | solution.py:200
  8.7 90.9 %all-gather.18.cloned.1.call-start = ((), (), s32[]{:S(2)}) async-start(), calls=%async_computation.13 | async-start | bytes 2359296 | tf_op jit(solution)/shard_map/all_gather | solution.py:201
  9.4 119.9 %all-gather.14.cloned.1.call-start = ((), (), s32[]{:S(2)}) async-start(), calls=%async_computation.11 | async-start | bytes 2359296 | tf_op jit(solution)/shard_map/all_gather | solution.py:202
  10.0 149.0 %all-gather.20.cloned.1.call-start = ((), (), s32[]{:S(2)}) async-start(), calls=%async_computation.14 | async-start | bytes 2359296 | tf_op jit(solution)/shard_map/all_gather | solution.py:203
  10.6 179.2 %reduce-scatter.13.cloned.1.call-start = ((), (), s32[]{:S(2)}) async-start(), calls=%async_computation.15 | async-start | bytes 1310720 | tf_op jit(solution)/shard_map/reduce_scatter | solution.py:235
  32.0 70.8 %copy-start.26 = (f32[256,64]{1,0:T(8,128)}, f32[256,64]{1,0:T(8,128)S(1)}, u32[]{:S(2)}) copy-start(f32[256,64]{1,0:T(8,128)S(1)} %get-tuple-element.178) | copy-start | bytes 196612
  32.0 97.3 %copy-start.29 = (f32[1,2048]{1,0:T(1,128)}, f32[1,2048]{1,0:T(1,128)S(1)}, u32[]{:S(2)}) copy-start(f32[1,2048]{1,0:T(1,128)S(1)} %get-tuple-element.163) | copy-start | bytes 24580
  32.0 217.2 %copy-start.45 = (f32[1,2048]{1,0:T(1,128)}, f32[1,2048]{1,0:T(1,128)S(1)}, u32[]{:S(2)}) copy-start(f32[1,2048]{1,0:T(1,128)S(1)} %get-tuple-element.162) | copy-start | bytes 24580
  41.8 87.5 %copy-start.43 = (f32[256]{0:T(256)}, f32[256]{0:T(256)S(1)}, u32[]{:S(2)}) copy-start(f32[256]{0:T(256)S(1)} %add_rsqrt_fusion.1) | copy-start | bytes 3076
  69.8 29.8 %copy-start = (bf16[256,2048]{1,0:T(8,128)(2,1)S(1)}, bf16[256,2048]{1,0:T(8,128)(2,1)}, u32[]{:S(2)}) copy-start(bf16[256,2048]{1,0:T(8,128)(2,1)} %all-gather.12.cloned.1.call-done) | copy-start | bytes 3145732
  104.3 27.3 %copy-start.3 = (f32[4,256,256]{1,2,0:T(8,128)}, f32[4,256,256]{1,2,0:T(8,128)S(1)}, u32[]{:S(2)}) copy-start(f32[4,256,256]{1,2,0:T(8,128)S(1)} %get-tuple-element.180) | copy-start | bytes 3145732
  104.3 27.3 %copy-start.48 = (f32[4,256]{1,0:T(4,128)}, f32[4,256]{1,0:T(4,128)S(1)}, u32[]{:S(2)}) copy-start(f32[4,256]{1,0:T(4,128)S(1)} %get-tuple-element.179) | copy-start | bytes 12292
  104.5 27.2 %copy-start.66 = (f32[4,256]{1,0:T(4,128)}, f32[4,256]{1,0:T(4,128)S(1)}, u32[]{:S(2)}) copy-start(f32[4,256]{1,0:T(4,128)S(1)} %fusion.19) | copy-start | bytes 12292
  132.4 30.1 %copy-start.28 = (bf16[4,128,256]{2,1,0:T(8,128)(2,1)}, bf16[4,128,256]{2,1,0:T(8,128)(2,1)S(1)}, u32[]{:S(2)}) copy-start(bf16[4,128,256]{2,1,0:T(8,128)(2,1)S(1)} %convolution_convert_fusion.4) | copy-start | bytes 786436
  158.9 30.8 %copy-start.13 = (bf16[256,512]{1,0:T(8,128)(2,1)S(1)}, bf16[256,512]{1,0:T(8,128)(2,1)}, u32[]{:S(2)}) copy-start(bf16[256,512]{1,0:T(8,128)(2,1)} %param.18) | copy-start | bytes 786436
  158.9 32.6 %copy-start.8 = (bf16[256,4,1408]{2,1,0:T(4,128)(2,1)S(1)}, bf16[256,4,1408]{2,1,0:T(4,128)(2,1)}, u32[]{:S(2)}) copy-start(bf16[256,4,1408]{2,1,0:T(4,128)(2,1)} %param.27) | copy-start | bytes 8650756
  162.4 55.5 %all-gather.30.cloned.1.call-start = ((), (), s32[]{:S(2)}) async-start(), calls=%async_computation.21 | async-start | bytes 1310720 | tf_op jit(solution)/shard_map/all_gather | solution.py:195
  163.2 84.5 %all-gather.22.cloned.1.call-start = ((), (), s32[]{:S(2)}) async-start(), calls=%async_computation.16 | async-start | bytes 1310720 | tf_op jit(solution)/shard_map/all_gather | solution.py:239
  191.5 174.8 %all-gather.26.cloned.1.call-start = ((), (), s32[]{:S(2)}) async-start(), calls=%async_computation.18 | async-start | bytes 25952256 | tf_op jit(solution)/shard_map/all_gather | solution.py:206
  193.5 291.8 %all-gather.24.cloned.1.call-start = ((), (), s32[]{:S(2)}) async-start(), calls=%async_computation.17 | async-start | bytes 25952256 | tf_op jit(solution)/shard_map/all_gather | solution.py:205
  197.2 406.6 %all-gather.28.cloned.1.call-start = ((), (), s32[]{:S(2)}) async-start(), calls=%async_computation.19 | async-start | bytes 25952256 | tf_op jit(solution)/shard_map/all_gather | solution.py:207
  201.1 514.7 %reduce-scatter.15.cloned.1.call-start = ((), (), s32[]{:S(2)}) async-start(), calls=%async_computation.20 | async-start | bytes 2949120 | tf_op jit(solution)/shard_map/reduce_scatter | solution.py:258
  212.6 39.5 %copy-start.36 = (bf16[2048,4]{0,1:T(4,128)(2,1)}, bf16[2048,4]{0,1:T(4,128)(2,1)S(1)}, u32[]{:S(2)}) copy-start(bf16[2048,4]{0,1:T(4,128)(2,1)S(1)} %all_gather.54) | copy-start | bytes 49156
  212.6 40.9 %copy-start.60 = (s32[256,1]{0,1:T(1,128)}, s32[256,1]{0,1:T(1,128)S(1)}, u32[]{:S(2)}) copy-start(s32[256,1]{0,1:T(1,128)S(1)} %get-tuple-element.175) | copy-start | bytes 3076
  212.7 41.1 %copy-start.57 = (s32[256,1]{0,1:T(1,128)}, s32[256,1]{0,1:T(1,128)S(1)}, u32[]{:S(2)}) copy-start(s32[256,1]{0,1:T(1,128)S(1)} %get-tuple-element.174) | copy-start | bytes 3076
  271.3 424.5 %copy-start.32 = (pred[4,144]{1,0:T(4,128)(4,1)}, pred[4,144]{1,0:T(4,128)(4,1)S(1)}, u32[]{:S(2)}) copy-start(pred[4,144]{1,0:T(4,128)(4,1)S(1)} %compare_and_fusion) | copy-start | bytes 1732
  366.3 119.0 %copy-start.2 = (bf16[576,2048]{1,0:T(8,128)(2,1)S(1)}, bf16[576,2048]{1,0:T(8,128)(2,1)}, u32[]{:S(2)}) copy-start(bf16[576,2048]{1,0:T(8,128)(2,1)} %gather_fusion) | copy-start | bytes 7077892
  380.4 223.5 %copy-start.41 = (f32[4,144]{1,0:T(4,128)S(1)}, f32[4,144]{1,0:T(4,128)}, u32[]{:S(2)}) copy-start(f32[4,144]{1,0:T(4,128)} %mul.521) | copy-start | bytes 6916
  644.1 105.4 %reduce-scatter.17.cloned.1.call-start = ((), (), s32[]{:S(2)}) async-start(), calls=%async_computation.22 | async-start | bytes 1310720 | tf_op jit(solution)/shard_map/reduce_scatter | solution.py:313
  695.7 98.7 %all-gather.32.cloned.1.call-start = ((), (), s32[]{:S(2)}) async-start(), calls=%async_computation.23 | async-start | bytes 1310720 | tf_op jit(solution)/shard_map/all_gather | solution.py:337
  752.6 19.7 %copy-start.42 = (f32[4,144]{1,0:T(4,128)S(1)}, f32[4,144]{1,0:T(4,128)}, u32[]{:S(2)}) copy-start(f32[4,144]{1,0:T(4,128)} %mul.521) | copy-start | bytes 6916
  752.6 163.0 %reduce-scatter.31.cloned.1.call-start = ((), (), s32[]{:S(2)}) async-start(), calls=%async_computation.30 | async-start | bytes 1179648
  772.3 20.3 %copy-start.6 = (bf16[256,2048]{1,0:T(8,128)(2,1)S(1)}, bf16[256,2048]{1,0:T(8,128)(2,1)}, u32[]{:S(2)}) copy-start(bf16[256,2048]{1,0:T(8,128)(2,1)} %copy-done.5) | copy-start | bytes 3145732
  772.3 20.3 %copy-start.40 = (f32[256,4]{0,1:T(4,128)S(1)}, f32[256,4]{0,1:T(4,128)}, u32[]{:S(2)}) copy-start(f32[256,4]{0,1:T(4,128)} %copy-done.38) | copy-start | bytes 12292
  772.3 20.3 %copy-start.52 = (f32[256]{0:T(256)S(1)}, f32[256]{0:T(256)}, u32[]{:S(2)}) copy-start(f32[256]{0:T(256)} %copy-done.50) | copy-start | bytes 3076
  772.3 20.3 %copy-start.56 = (f32[256]{0:T(256)S(1)}, f32[256]{0:T(256)}, u32[]{:S(2)}) copy-start(f32[256]{0:T(256)} %copy-done.53) | copy-start | bytes 3076
  772.3 20.3 %copy-start.59 = (s32[256,1]{0,1:T(1,128)S(1)}, s32[256,1]{0,1:T(1,128)}, u32[]{:S(2)}) copy-start(s32[256,1]{0,1:T(1,128)} %copy-done.57) | copy-start | bytes 3076
  772.4 20.3 %copy-start.62 = (s32[256,1]{0,1:T(1,128)S(1)}, s32[256,1]{0,1:T(1,128)}, u32[]{:S(2)}) copy-start(s32[256,1]{0,1:T(1,128)} %copy-done.60) | copy-start | bytes 3076
  772.4 20.3 %copy-start.72 = (f32[256]{0:T(256)S(1)}, f32[256]{0:T(256)}, u32[]{:S(2)}) copy-start(f32[256]{0:T(256)} %copy-done.71) | copy-start | bytes 3076
  772.4 20.3 %copy-start.74 = (f32[256]{0:T(256)S(1)}, f32[256]{0:T(256)}, u32[]{:S(2)}) copy-start(f32[256]{0:T(256)} %copy-done.73) | copy-start | bytes 3076
  772.4 20.3 %copy-start.80 = (f32[256]{0:T(256)S(1)}, f32[256]{0:T(256)}, u32[]{:S(2)}) copy-start(f32[256]{0:T(256)} %copy-done.79) | copy-start | bytes 3076
  794.2 135.0 %reduce-scatter.19.cloned.1.call-start = ((), (), s32[]{:S(2)}) async-start(), calls=%async_computation.24 | async-start | bytes 1310720 | tf_op jit(solution)/shard_map/reduce_scatter | solution.py:366
  809.1 850.8 %reduce-scatter.29.cloned.1.call-start = ((), (), s32[]{:S(2)}) async-start(), calls=%async_computation.29 | async-start | bytes 155713536 | tf_op jit(solution)/shard_map/reduce_scatter | solution.py:393
  898.5 816.9 %reduce-scatter.27.cloned.1.call-start = ((), (), s32[]{:S(2)}) async-start(), calls=%async_computation.28 | async-start | bytes 4718592 | tf_op jit(solution)/shard_map/reduce_scatter | solution.py:400
  902.7 868.1 %reduce-scatter.25.cloned.1.call-start = ((), (), s32[]{:S(2)}) async-start(), calls=%async_computation.27 | async-start | bytes 4718592 | tf_op jit(solution)/shard_map/reduce_scatter | solution.py:399
  907.0 919.2 %reduce-scatter.23.cloned.1.call-start = ((), (), s32[]{:S(2)}) async-start(), calls=%async_computation.26 | async-start | bytes 4718592 | tf_op jit(solution)/shard_map/reduce_scatter | solution.py:398
  911.2 970.3 %reduce-scatter.21.cloned.1.call-start = ((), (), s32[]{:S(2)}) async-start(), calls=%async_computation.25 | async-start | bytes 4718592 | tf_op jit(solution)/shard_map/reduce_scatter | solution.py:397
  (64 other events, 344.3 us)
Sparse Core Ops, SparseCore 0:
  9.6 30.6 all-gather.11
  42.1 27.6 all-gather.15
  71.7 27.8 all-gather.17
  101.3 27.8 all-gather.13
  131.0 27.8 all-gather.19
  162.6 27.1 reduce-scatter.12
  191.4 26.5 all-gather.29
  220.2 27.4 all-gather.21
  250.3 115.9 all-gather.25
  368.8 116.4 all-gather.23
  487.4 116.4 all-gather.27
  644.2 48.0 reduce-scatter.14
  695.8 27.0 reduce-scatter.16
  752.7 26.6 all-gather.31
  794.3 34.8 reduce-scatter.30
  831.9 27.1 reduce-scatter.18
  898.7 761.2 reduce-scatter.28
  1664.1 51.3 reduce-scatter.26
  1719.4 51.3 reduce-scatter.24
  1774.9 51.2 reduce-scatter.22
  1830.2 51.3 reduce-scatter.20
where the time goes:
time: 1890 us
  waiting for transfers between devices  1370 us (72%)
  matrix products  202 us (11%)
  other arithmetic  135 us (7%)
  local copies, waits for them, and re-layouts  82.5 us (4%)
  blocking collectives  76.3 us (4%)
    reduce_scatter x1, waiting for transfers between devices, per_device(): lax.psum_scatter(jnp.stack([gate_term, up_term, down_term], 1), 'wide', s...  705 us
    all_gather x1, waiting for transfers between devices, per_device(): lax.all_gather(weight_set[7], 'wide', axis=0, tiled=True)  105 us
    all_gather x1, waiting for transfers between devices, per_device(): lax.all_gather(weight_set[5], 'wide', axis=0, tiled=True)  105 us
    all_gather x1, waiting for transfers between devices, per_device(): lax.all_gather(weight_set[6], 'wide', axis=0, tiled=True)  95 us
    another operation x1, other arithmetic, per_device(): jnp.stack([gate_term, up_term, down_term], 1)  89.4 us
    reduce_scatter x1, waiting for transfers between devices, per_device(): lax.psum_scatter(grad_key_w, 'wide', scatter_dimension=0, tiled=True)  55.5 us
    reduce_scatter x1, waiting for transfers between devices, per_device(): lax.psum_scatter(grad_query_w, 'wide', scatter_dimension=0, tiled=True)  55.3 us
    reduce_scatter x1, waiting for transfers between devices, per_device(): lax.psum_scatter(grad_value_w, 'wide', scatter_dimension=0, tiled=True)  55.3 us
  transfers between devices with their start and end apart: 21, of which 16 were waited for; matrix products, arithmetic and copies ran while one was open for 19% of the time, Pallas kernels for 0%

commit v1 on v0

v1 whole, which is shorter than its diff:
```python
import jax
import jax.numpy as jnp
from jax import lax
from jax.sharding import PartitionSpec as P

HEAD_DIM = 128
EXPERTS = 4
SEGS = 13
CAP = 144
SLOTS = EXPERTS * CAP
NORM_EPS = 1e-05
NEG_FILL = -1e30
ROPE_BASE = 10000.0
BF = jnp.bfloat16
F32 = jnp.float32


def mm(left, right, dims):
    return lax.dot_general(left, right, (dims, ((), ())), preferred_element_type=F32)


def rows_cols(left, right):
    return mm(left, right, ((1,), (0,)))


def rows_rows(left, right):
    return mm(left, right, ((1,), (1,)))


def cols_cols(left, right):
    return mm(left, right, ((0,), (0,)))


def tree_layout(segment_row, parent_row):
    seg_ids = jnp.arange(SEGS, dtype=jnp.int32)
    member = segment_row[:, None] == seg_ids[None, :]
    parent_of = (parent_row[:, None] == seg_ids[None, :]) & (seg_ids[:, None] != 0)
    itself = seg_ids[:, None] == seg_ids[None, :]
    reach = itself
    for _ in range(3):
        reach = itself | jnp.any(parent_of[:, :, None] & reach[None, :, :], axis=1)
    counts = member.astype(jnp.int32)
    lengths = jnp.sum(counts, 0)
    starts = jnp.sum(jnp.where(seg_ids[None, :] < seg_ids[:, None], lengths[None, :], 0), 1)
    before = jnp.sum(jnp.where(reach, lengths[None, :], 0), 1) - lengths
    row_at = jnp.arange(segment_row.shape[0], dtype=jnp.int32)
    places = jnp.sum(counts * (before - starts)[None, :], 1) + row_at
    member_low = member.astype(BF)
    lineage = rows_cols(member_low, reach.astype(BF)).astype(BF)
    shared = rows_rows(lineage, member_low) > 0.5
    seen = shared & (row_at[None, :] <= row_at[:, None])
    return seen, places.astype(F32)


def route(expert_row, slot_rank):
    expert_range = jnp.arange(EXPERTS, dtype=jnp.int32)
    hot_first = (expert_row[:, 0:1] == expert_range[None, :]).astype(F32)
    hot_second = (expert_row[:, 1:2] == expert_range[None, :]).astype(F32)
    earlier = (slot_rank[None, :] < slot_rank[:, None]).astype(BF)
    count_first = rows_cols(earlier, hot_first.astype(BF))
    count_second = rows_cols(earlier, hot_second.astype(BF))
    ahead_first = jnp.sum(count_first * hot_first, 1)
    ahead_second = jnp.sum((count_second + jnp.sum(hot_first, 0)[None, :]) * hot_second, 1)
    slot_index = jnp.stack([ahead_first, ahead_second], 1).astype(jnp.int32)
    kept = slot_index < CAP
    flat_slot = jnp.where(kept, expert_row * CAP + slot_index, SLOTS)
    slot_range = jnp.arange(SLOTS, dtype=jnp.int32)
    pick_first = flat_slot[:, 0:1] == slot_range[None, :]
    pick_second = flat_slot[:, 1:2] == slot_range[None, :]
    return hot_first, hot_second, kept.astype(F32), pick_first, pick_second


def rotate(vectors, cosines, sines):
    half_dim = HEAD_DIM // 2
    first_half = vectors[..., :half_dim]
    second_half = vectors[..., half_dim:]
    return jnp.concatenate(
        [
            first_half * cosines - second_half * sines,
            second_half * cosines + first_half * sines,
        ],
        -1,
    )


def gate_pair(logits, hot_first, hot_second):
    chances = jax.nn.softmax(logits, axis=-1)
    first_share = jnp.sum(chances * hot_first, 1)
    second_share = jnp.sum(chances * hot_second, 1)
    pair_total = first_share + second_share
    return (first_share / pair_total, second_share / pair_total)


def two_parts(column):
    high = column.astype(BF)
    return high, (column - high.astype(F32)).astype(BF)


def per_device(
    tokens, gain_attn, w_query, w_key, w_value, w_out, gain_ffn, w_router,
    w_gate, w_up, w_down, segment, parents, expert_ids, slot_order, cotangent,
):
    narrow_count = lax.axis_size("narrow")
    wide_count = lax.axis_size("wide")
    narrow_at = lax.axis_index("narrow")
    token_count, part_width = tokens.shape
    full_width = part_width * narrow_count
    hidden_width = w_gate.shape[2]
    rows_each = w_gate.shape[0]
    blocks = wide_count // 8
    quads = [
        [8 * block + 2 * chip + core for chip in range(4)]
        for block in range(blocks)
        for core in range(2)
    ]
    mates = [
        [8 * block + 2 * chip + core for block in range(blocks) for core in range(2)]
        for chip in range(4)
    ]

    def quad_swap(array):
        return lax.all_to_all(array, "wide", 0, 0, axis_index_groups=quads, tiled=True)

    def own_rows(weight):
        moved = quad_swap(jnp.transpose(weight, (1, 0, 2)))
        joined = lax.all_gather(moved, "wide", axis=0, axis_index_groups=mates, tiled=True)
        return joined.reshape(full_width, hidden_width)

    def mixed_features(rows):
        count = rows.shape[0]
        return rows.reshape(count, blocks, 4, 2, rows_each).transpose(0, 1, 3, 2, 4).reshape(
            count, full_width
        )

    def plain_features(rows):
        count = rows.shape[0]
        return rows.reshape(count, blocks, 2, 4, rows_each).transpose(0, 1, 3, 2, 4).reshape(
            count, full_width
        )

    def share_rows(grad):
        parts = grad.astype(BF).reshape(blocks * 2, 4, rows_each, hidden_width)
        summed = lax.psum_scatter(
            parts, "wide", scatter_dimension=0, axis_index_groups=mates, tiled=True
        )[0]
        return jnp.transpose(quad_swap(summed), (1, 0, 2)).astype(F32)

    gate_w, up_w, down_w = own_rows(w_gate), own_rows(w_up), own_rows(w_down)
    attn_w = lax.all_gather(
        jnp.stack([w_query, w_key, w_value, w_out], 1), "wide", axis=0, tiled=True
    )
    query_w, key_w, value_w, out_w = (attn_w[:, i] for i in range(4))
    router_w = lax.all_gather(w_router, "wide", axis=0, tiled=True)
    tokens_full = lax.all_gather(tokens, "narrow", axis=1, tiled=True)
    grad_full = lax.all_gather(cotangent, "narrow", axis=1, tiled=True)
    gains_full = lax.all_gather(jnp.stack([gain_attn, gain_ffn]), "narrow", axis=1, tiled=True)
    gain_first = gains_full[0].astype(F32)
    gain_second = gains_full[1].astype(F32)
    gain_first_loc = gain_attn.astype(F32)
    gain_second_loc = gain_ffn.astype(F32)

    seen, places = tree_layout(segment[0], parents[0])
    hot_first, hot_second, kept, pick_first, pick_second = route(expert_ids, slot_order[0])
    pick_first_low = pick_first.astype(BF)
    pick_second_low = pick_second.astype(BF)
    pick_both_low = (pick_first | pick_second).astype(BF)

    inputs_full = tokens_full.astype(F32)
    scale_first = lax.rsqrt(jnp.mean(inputs_full * inputs_full, -1, keepdims=True) + NORM_EPS)
    normed_first = inputs_full * scale_first
    hidden_first = (normed_first * gain_first).astype(BF)
    heads = part_width // HEAD_DIM
    half_dim = HEAD_DIM // 2
    freqs = ROPE_BASE ** (-2.0 * jnp.arange(half_dim, dtype=F32) / HEAD_DIM)
    angles = places[:, None] * freqs[None, :]
    cosines, sines = jnp.cos(angles), jnp.sin(angles)
    query_raw = rows_cols(hidden_first, query_w)
    key_raw = rows_cols(hidden_first, key_w)
    value_low = rows_cols(hidden_first, value_w).astype(BF)
    score_scale = HEAD_DIM ** (-0.5)

    def head_cols(array, head):
        return array[:, head * HEAD_DIM : (head + 1) * HEAD_DIM]

    saved = []
    outs = []
    for head in range(heads):
        query = rotate(head_cols(query_raw, head), cosines, sines).astype(BF)
        key = rotate(head_cols(key_raw, head), cosines, sines).astype(BF)
        value = head_cols(value_low, head)
        scores = jnp.where(seen, rows_rows(query, key) * score_scale, NEG_FILL)
        exps = jnp.exp(scores - jnp.max(scores, -1, keepdims=True))
        weights = exps / jnp.sum(exps, -1, keepdims=True)
        saved.append((query, key, value, weights))
        outs.append(rows_cols(weights.astype(BF), value).astype(BF))
    attended = jnp.concatenate(outs, 1)
    branch_part = rows_rows(attended, out_w).astype(BF)
    branch_loc = lax.psum_scatter(
        branch_part, "narrow", scatter_dimension=1, tiled=True
    ).astype(F32)
    middle = tokens.astype(F32) + branch_loc
    middle_full = lax.all_gather(middle.astype(BF), "narrow", axis=1, tiled=True).astype(F32)
    scale_second = lax.rsqrt(jnp.mean(middle_full * middle_full, -1, keepdims=True) + NORM_EPS)
    normed_second = middle_full * scale_second
    hidden_second = (normed_second * gain_second).astype(BF)
    logits = rows_cols(hidden_second, router_w)
    share_first, share_second = gate_pair(logits, hot_first, hot_second)
    weight_first = kept[:, 0] * share_first
    weight_second = kept[:, 1] * share_second

    slot_weight = jnp.sum(
        pick_first * weight_first[:, None] + pick_second * weight_second[:, None], 0
    )
    weight_high, weight_low = two_parts(slot_weight)
    pads = jnp.stack([weight_high, weight_low], 1)
    pads = jnp.pad(pads, ((0, 0), (0, 126)))
    sent_hidden = cols_cols(pick_both_low, hidden_second).astype(BF)
    sent_grad = cols_cols(pick_both_low, grad_full).astype(BF)
    sent = jnp.concatenate([sent_hidden, sent_grad, pads], 1)
    got = quad_swap(sent.reshape(EXPERTS, CAP, -1)).reshape(SLOTS, -1)
    slot_hidden = mixed_features(got[:, :full_width])
    slot_grad = mixed_features(got[:, full_width : 2 * full_width])
    slot_gate = got[:, 2 * full_width : 2 * full_width + 2].astype(F32)
    slot_gate = slot_gate[:, 0:1] + slot_gate[:, 1:2]

    gate_pre = rows_cols(slot_hidden, gate_w)
    up_pre = rows_cols(slot_hidden, up_w)
    sigmoid_gate = jax.nn.sigmoid(gate_pre)
    silu_gate = gate_pre * sigmoid_gate
    activated = (silu_gate * up_pre).astype(BF)
    expert_part = rows_rows(activated, down_w)
    act_raw = rows_cols(slot_grad, down_w)
    share_part = jnp.sum(act_raw * activated.astype(F32), 1, keepdims=True)
    grad_act = act_raw * slot_gate
    grad_gate_pre = (
        grad_act * up_pre * sigmoid_gate * (1.0 + gate_pre * (1.0 - sigmoid_gate))
    ).astype(BF)
    grad_up_pre = (grad_act * silu_gate).astype(BF)
    grad_slot = rows_rows(grad_gate_pre, gate_w) + rows_rows(grad_up_pre, up_w)
    stat_part = jnp.sum(slot_hidden.astype(F32) * grad_slot, 1, keepdims=True)
    extras = jnp.concatenate([*two_parts(share_part), *two_parts(stat_part)], 1)
    extras = jnp.pad(extras, ((0, 0), (0, 124)))
    back_parts = []
    expert_plain = plain_features(expert_part.astype(BF))
    slot_plain = plain_features(grad_slot.astype(BF))
    for part in range(narrow_count):
        cols = slice(part * part_width, (part + 1) * part_width)
        back_parts += [expert_plain[:, cols], slot_plain[:, cols], extras]
    back = lax.psum_scatter(
        jnp.concatenate(back_parts, 1), "narrow", scatter_dimension=1, tiled=True
    )
    back = quad_swap(back.reshape(EXPERTS, CAP, -1)).reshape(SLOTS, -1)
    picked_first = rows_cols(pick_first_low, back)
    picked_second = rows_cols(pick_second_low, back)
    output = (
        middle
        + weight_first[:, None] * picked_first[:, :part_width]
        + weight_second[:, None] * picked_second[:, :part_width]
    ).astype(BF)

    grad_weight = (slot_grad.astype(F32) * slot_gate).astype(BF)
    gate_out = share_rows(cols_cols(slot_hidden, grad_gate_pre))
    up_out = share_rows(cols_cols(slot_hidden, grad_up_pre))
    down_out = share_rows(cols_cols(grad_weight, activated))

    tail = 2 * part_width
    share_first_grad = picked_first[:, tail] + picked_first[:, tail + 1]
    share_second_grad = picked_second[:, tail] + picked_second[:, tail + 1]
    both = picked_first + picked_second
    stat_second = both[:, tail + 2] + both[:, tail + 3]
    grad_hidden_loc = both[:, part_width:tail]
    grad_local = cotangent.astype(F32)
    _, pull_gates = jax.vjp(lambda given: gate_pair(given, hot_first, hot_second), logits)
    (grad_logits,) = pull_gates((kept[:, 0] * share_first_grad, kept[:, 1] * share_second_grad))
    grad_logits_low = grad_logits.astype(BF)
    grad_router_rows = rows_rows(grad_logits_low, router_w)
    stat_total = stat_second + jnp.sum(normed_second * gain_second * grad_router_rows, 1)

    def take_cols(full_rows):
        return lax.dynamic_slice_in_dim(full_rows, narrow_at * part_width, part_width, 1)

    grad_hidden_loc = grad_hidden_loc + take_cols(grad_router_rows)
    normed_second_loc = take_cols(normed_second)
    grad_gain_second = jnp.sum(grad_hidden_loc * normed_second_loc, 0)
    grad_middle = grad_local + scale_second * (
        gain_second_loc * grad_hidden_loc - normed_second_loc * stat_total[:, None] / full_width
    )
    grad_router_w = cols_cols(hidden_second, grad_logits_low)
    grad_branch = lax.all_gather(grad_middle.astype(BF), "narrow", axis=1, tiled=True)
    grad_attended = rows_cols(grad_branch, out_w).astype(BF)
    grad_out_w = cols_cols(grad_branch, attended)
    grad_qs, grad_ks, grad_vs = [], [], []
    for head in range(heads):
        query, key, value, weights = saved[head]
        grad_out = head_cols(grad_attended, head)
        grad_weights = rows_rows(grad_out, value)
        inner = jnp.sum(weights * grad_weights, -1, keepdims=True)
        grad_scores = (weights * (grad_weights - inner)).astype(BF)
        grad_q = rows_cols(grad_scores, key) * score_scale
        grad_k = cols_cols(grad_scores, query) * score_scale
        grad_qs.append(rotate(grad_q, cosines, -sines).astype(BF))
        grad_ks.append(rotate(grad_k, cosines, -sines).astype(BF))
        grad_vs.append(cols_cols(weights.astype(BF), grad_out).astype(BF))
    grad_query_raw = jnp.concatenate(grad_qs, 1)
    grad_key_raw = jnp.concatenate(grad_ks, 1)
    grad_value_raw = jnp.concatenate(grad_vs, 1)
    grad_hidden_first = (
        rows_rows(grad_query_raw, query_w)
        + rows_rows(grad_key_raw, key_w)
        + rows_rows(grad_value_raw, value_w)
    )
    stat_first = jnp.sum(normed_first * gain_first * grad_hidden_first, 1, keepdims=True)
    extras = jnp.pad(jnp.concatenate(two_parts(stat_first), 1), ((0, 0), (0, 126)))
    grad_hidden_low = grad_hidden_first.astype(BF)
    first_parts = []
    for part in range(narrow_count):
        first_parts += [grad_hidden_low[:, part * part_width : (part + 1) * part_width], extras]
    first_back = lax.psum_scatter(
        jnp.concatenate(first_parts, 1), "narrow", scatter_dimension=1, tiled=True
    ).astype(F32)
    grad_first_loc = first_back[:, :part_width]
    stat_first = first_back[:, part_width : part_width + 1]
    stat_first = stat_first + first_back[:, part_width + 1 : part_width + 2]
    normed_first_loc = take_cols(normed_first)
    grad_gain_first = jnp.sum(grad_first_loc * normed_first_loc, 0)
    grad_tokens = grad_middle + scale_first * (
        gain_first_loc * grad_first_loc - normed_first_loc * stat_first / full_width
    )
    grad_attn_w = jnp.concatenate(
        [
            cols_cols(hidden_first, grad_query_raw).astype(BF),
            cols_cols(hidden_first, grad_key_raw).astype(BF),
            cols_cols(hidden_first, grad_value_raw).astype(BF),
            grad_out_w.astype(BF),
        ],
        1,
    )
    attn_summed = lax.psum_scatter(
        grad_attn_w, "wide", scatter_dimension=0, tiled=True
    ).astype(F32)
    router_summed = lax.psum_scatter(grad_router_w, "wide", scatter_dimension=0, tiled=True)
    gains_summed = lax.psum(jnp.stack([grad_gain_first, grad_gain_second]), "wide")
    return (
        output,
        grad_tokens,
        gains_summed[0],
        attn_summed[:, :part_width],
        attn_summed[:, part_width : 2 * part_width],
        attn_summed[:, 2 * part_width : 3 * part_width],
        attn_summed[:, 3 * part_width :],
        gains_summed[1],
        router_summed,
        gate_out,
        up_out,
        down_out,
    )


def solution(mesh):
    pair = P("wide", "narrow")
    part = P("narrow")
    rows = P("wide", None)
    cube = P("wide", None, "narrow")
    return jax.shard_map(
        per_device,
        mesh=mesh,
        in_specs=(
            pair, part, pair, pair, pair, pair, part, rows, cube, cube, cube,
            rows, rows, rows, rows, pair,
        ),
        out_specs=(
            pair, pair, part, pair, pair, pair, pair, part, rows, cube, cube, cube,
        ),
        check_vma=False,
    )
```

time: 1890 us -> 889 us (0.47)
  waiting for transfers between devices: 1370 us -> 430 us
  other arithmetic: 135 us -> 41 us
  matrix products: 202 us -> 116 us
  local copies, waits for them, and re-layouts: 82.5 us -> 146 us
  starting transfers between devices: 1.02 us -> 33 us
  blocking collectives: 76.3 us -> 97.3 us
    reduce_scatter x9 -> x5, waiting for transfers between devices: 918 us -> 73 us  [the longest x1 44.4 us: per_device(): lax.psum_scatter(grad_attn_w, 'wide', scatter_dimension=0, tiled=True)]
    all_gather x11 -> x8, waiting for transfers between devices: 453 us -> 70 us  [the longest x1 54.8 us: per_device(): lax.all_gather(jnp.stack([w_query, w_key, w_value, w_out], 1), 'wide', ax...]
    all_to_all x0 -> x7, waiting for transfers between devices: none -> 182 us  [quad_swap(): lax.all_to_all(array, 'wide', 0, 0, axis_index_groups=quads, tiled=True)]
    unnamed x22 -> x19, waiting for transfers between devices: 4.06 us -> 105 us
    another operation x7 -> x6, other arithmetic: 90.1 us -> 3.07 us  [the longest x1 2.29 us: per_device(): jnp.stack([w_query, w_key, w_value, w_out], 1)]
    dot_general x33 -> x54, matrix products: 200 us -> 114 us  [mm(): lax.dot_general(left, right, (dims, ((), ())), preferred_element_type=F32)]
    reshape x6 -> x11, local copies, waits for them, and re-layouts: 1.87 us -> 65.3 us  [the longest x6 36.7 us: plain_features(): rows.reshape(count, blocks, 2, 4, rows_each).transpose(0, 1, 3, 2, 4)]
    unnamed x4 -> x0, blocking collectives: 53.7 us -> none
  transfers between devices with their start and end apart: 21 -> 23, of which waited for: 16 -> 12; matrix products, arithmetic and copies ran while one was open for 19% -> 19% of each run, Pallas kernels for 0% -> 0%
where the time goes in v1:
time: 889 us; the launch traced here: 879 us
  waiting for transfers between devices  430 us (48%)
  local copies, waits for them, and re-layouts  146 us (16%)
  matrix products  116 us (13%)
  blocking collectives  97.3 us (11%)
  other arithmetic  41 us (5%)
  starting transfers between devices  33 us (4%)
  between operations  16.3 us (2%)
    all_to_all x7, waiting for transfers between devices, quad_swap(): lax.all_to_all(array, 'wide', 0, 0, axis_index_groups=quads, tiled=True)  182 us
    dot_general x54, matrix products, mm(): lax.dot_general(left, right, (dims, ((), ())), preferred_element_type=F32)  114 us
    unnamed x19, waiting for transfers between devices  105 us
    unnamed x269, local copies, waits for them, and re-layouts  67.1 us
    all_gather x1, waiting for transfers between devices, per_device(): lax.all_gather(jnp.stack([w_query, w_key, w_value, w_out], 1), 'wide', ax...  54.8 us
    reduce_scatter x1, waiting for transfers between devices, per_device(): lax.psum_scatter(grad_attn_w, 'wide', scatter_dimension=0, tiled=True)  44.4 us
    reshape x6, local copies, waits for them, and re-layouts, plain_features(): rows.reshape(count, blocks, 2, 4, rows_each).transpose(0, 1, 3, 2, 4)  36.7 us
    all_to_all x1, blocking collectives, quad_swap(): lax.all_to_all(array, 'wide', 0, 0, axis_index_groups=quads, tiled=True)  36.6 us
  transfers between devices with their start and end apart: 23, of which 12 were waited for; matrix products, arithmetic and copies ran while one was open for 19% of the time, Pallas kernels for 0%

profile of v1, /device:TPU:0, one launch (start us, length us, event | category | flops | bytes accessed | tf_op | source)
XLA Modules:
  0.0 879.3 jit_solution(5810162544895107725)
XLA Ops:
  10.4 13.7 %all_gather.31 = bf16[2,2048]{1,0:T(2,128)(2,1)S(1)} all-gather(bf16[2,512]{1,0:T(2,128)(2,1)S(1)} %pad_maximum_fusion.35), channel_id=1, replica_groups=mesh['wide'=8,'narrow'=4] {'narrow'}, dimensions={1}, use_global_device_ids=true | all-gather | bytes 10240 | tf_op jit(solution)/shard_map/all_gather | solution.py:156
  25.3 15.0 %all-gather.9.cloned.1.call-done = bf16[256,2048]{1,0:T(8,128)(2,1)} async-done(((bf16[256,512]{1,0:T(8,128)(2,1)}), bf16[256,2048]{1,0:T(8,128)(2,1)}) %all-gather.9.cloned.1.call-update) | async-done | bytes 1048592 | tf_op jit(solution)/shard_map/all_gather | solution.py:154
  41.9 54.8 %all-gather.11.cloned.1.call-done = bf16[2048,4,512]{2,0,1:T(8,128)(2,1)} async-done(((bf16[256,4,512]{2,0,1:T(8,128)(2,1)}), bf16[2048,4,512]{2,0,1:T(8,128)(2,1)}) %all-gather.11.cloned.1.call-update) | async-done | bytes 8388624 | tf_op jit(solution)/shard_map/all_gather | solution.py:149
  111.6 27.2 %reduce-scatter.15.cloned.1.call-done = bf16[256,512]{1,0:T(8,128)(2,1)} async-done(((bf16[256,2048]{1,0:T(8,128)(2,1)}), bf16[256,512]{1,0:T(8,128)(2,1)}) %reduce-scatter.15.cloned.1.call-update) | async-done | bytes 262160 | tf_op jit(solution)/shard_map/reduce_scatter | solution.py:198
  144.3 4.6 all-to-all-start.1
  149.6 32.8 %all-to-all-done.1 = bf16[4,256,1408]{2,1,0:T(8,128)(2,1)} async-done(((bf16[4,256,1408]{2,1,0:T(8,128)(2,1)}), bf16[4,256,1408]{2,1,0:T(8,128)(2,1)}, u32[]{:S(2)}, u32[]{:S(2)}) %all-to-all-start.1) | async-done | bytes 2883616 | tf_op jit(solution)/shard_map/all_to_all | solution.py:122
  184.7 36.6 %all_to_all.40 = bf16[4,256,1408]{2,1,0:T(8,128)(2,1)} all-to-all(bf16[4,256,1408]{2,1,0:T(8,128)(2,1)S(1)} %bitcast.142), channel_id=1, replica_groups={{0,8,16,24},{4,12,20,28},{1,9,17,25},{5,13,21,29},{2,10,18,26},{6,14,22..., dimensions={0} | all-to-all | bytes 5767168 | tf_op jit(solution)/shard_map/all_to_all | solution.py:122
  225.0 4.9 all-to-all-start.3
  229.9 35.3 %all_gather.34 = bf16[2048,4]{0,1:T(4,128)(2,1)S(1)} all-gather(bf16[256,4]{0,1:T(4,128)(2,1)S(1)} %copy-done.105), channel_id=1, replica_groups=mesh['wide'=8,'narrow'=4] {'wide'}, dimensions={0}, use_global_device_ids=true | all-gather | bytes 18432 | tf_op jit(solution)/shard_map/all_gather | solution.py:153
  276.1 5.0 all-to-all-start
  281.9 54.6 %all-to-all-done = bf16[4,144,4224]{2,1,0:T(8,128)(2,1)} async-done(((bf16[4,144,4224]{2,1,0:T(8,128)(2,1)}), bf16[4,144,4224]{2,1,0:T(8,128)(2,1)}, u32[]{:S(2)}, u32[]{:S(2)}) %all-to-all-start) | async-done | bytes 4866080 | tf_op jit(solution)/shard_map/all_to_all | solution.py:122
  336.4 5.3 fusion.253
  341.7 6.6 reshape.348
  348.3 4.3 copy.216
  352.6 5.4 reshape.349
  358.1 6.6 reshape.355
  364.7 4.3 copy.259
  368.9 5.6 reshape.356
  375.8 8.9 %fusion.266 = f32[576,1408]{1,0:T(8,128)} fusion(bf16[576,2048]{1,0:T(8,128)(2,1)} %reshape.349, bf16[2048,1408]{1,0:T(8,128)(2,1)} %bitcast.215), kind=kOutput, calls=%fused_computation.452 | convolution fusion | flops 3321888768 | bytes 11370496 | tf_op jit(solution)/shard_map/dot_general | solution.py:19
  384.7 8.9 %fusion.267 = f32[576,1408]{1,0:T(8,128)} fusion(bf16[576,2048]{1,0:T(8,128)(2,1)} %reshape.349, bf16[2048,1408]{1,0:T(8,128)(2,1)} %bitcast.217), kind=kOutput, calls=%fused_computation.453 | convolution fusion | flops 3321888768 | bytes 11370496 | tf_op jit(solution)/shard_map/dot_general | solution.py:19
  393.6 10.9 %multiply_reduce_fusion.1 = (f32[576]{0:T(1024)S(1)}, bf16[576,1408]{1,0:T(8,128)(2,1)}, bf16[576,1408]{1,0:T(8,128)(2,1)S(1)}, bf16[576,1408]{1,0:T(8,128)(2,1)S(1)}) fusion(f32[576,1408]{1,0:T(8,128)} %fusion.267, f32[576,1408]{1,0:T(8,128)} %fusion.266, f32[576]{0:T(1024)S(1)} %fusion.32, bf16[576,2048]{1,0:T(8,128)(2,1)} %reshape.356, ...), kind=kOutput, calls=%fused_computation.12 | convolution fusion | flops 3337297408 | bytes 19485184 | tf_op jit(solution)/shard_map/dot_general | solution.py:19
  404.5 7.1 fusion.268
  411.6 5.4 multiply_reduce_fusion
  417.2 6.6 reshape.357
  423.8 5.5 copy.258
  429.3 6.4 reshape.358
  435.7 8.4 convolution_convert_fusion.3
  444.1 6.2 reshape.353
  450.3 5.5 copy.260
  455.8 6.6 reshape.354
  475.4 8.4 copy.239
  483.8 102.5 %reduce-scatter.25.cloned.1.call-done = bf16[1152,576]{1,0:T(8,128)(2,1)} async-done(((bf16[4608,576]{1,0:T(8,128)(2,1)}), bf16[1152,576]{1,0:T(8,128)(2,1)}) %reduce-scatter.25.cloned.1.call-update) | async-done | bytes 1327120
  594.9 14.4 %all-to-all-done.4 = bf16[4,144,1152]{2,1,0:T(8,128)(2,1)S(1)} async-done(((bf16[4,144,1152]{2,1,0:T(8,128)(2,1)}), bf16[4,144,1152]{2,1,0:T(8,128)(2,1)S(1)}, u32[]{:S(2)}, u32[]{:S(2)}) %all-to-all-start.4) | async-done | bytes 1327136 | tf_op jit(solution)/shard_map/all_to_all | solution.py:122
  624.8 8.8 %convolution_convert_fusion = bf16[2048,1408]{1,0:T(8,128)(2,1)} fusion(bf16[576,1408]{1,0:T(8,128)(2,1)} %get-tuple-element.92, bf16[576,2048]{1,0:T(8,128)(2,1)} %reshape.356, f32[576]{0:T(1024)} %copy-done.93), kind=kOutput, calls=%fused_computation.3 | convolution fusion | flops 3328311296 | bytes 9750784 | tf_op jit(solution)/shard_map/dot_general | solution.py:19
  633.7 8.6 convolution_convert_fusion.2
  642.4 9.0 %convolution_convert_fusion.1 = bf16[2048,1408]{1,0:T(8,128)(2,1)} fusion(bf16[576,2048]{1,0:T(8,128)(2,1)} %reshape.349, bf16[576,1408]{1,0:T(8,128)(2,1)} %copy-done.113), kind=kOutput, calls=%fused_computation.4 | convolution fusion | flops 3324772352 | bytes 9748480 | tf_op jit(solution)/shard_map/dot_general | solution.py:19
  676.4 4.2 pad_maximum_fusion
  680.6 4.8 all-to-all-start.7
  686.8 31.4 %all-to-all-done.7 = bf16[4,256,1408]{2,1,0:T(8,128)(2,1)} async-done(((bf16[4,256,1408]{2,1,0:T(8,128)(2,1)}), bf16[4,256,1408]{2,1,0:T(8,128)(2,1)}, u32[]{:S(2)}, u32[]{:S(2)}) %all-to-all-start.7) | async-done | bytes 2883616 | tf_op jit(solution)/shard_map/all_to_all | solution.py:122
  718.2 4.6 all-to-all-start.5
  722.9 37.0 %all-to-all-done.5 = bf16[4,256,1408]{2,1,0:T(8,128)(2,1)} async-done(((bf16[4,256,1408]{2,1,0:T(8,128)(2,1)}), bf16[4,256,1408]{2,1,0:T(8,128)(2,1)}, u32[]{:S(2)}, u32[]{:S(2)}) %all-to-all-start.5) | async-done | bytes 2883616 | tf_op jit(solution)/shard_map/all_to_all | solution.py:122
  759.9 4.8 all-to-all-start.6
  770.6 6.2 copy.236
  779.0 6.2 copy.234
  785.3 12.2 %all-to-all-done.6 = bf16[4,256,1408]{2,1,0:T(8,128)(2,1)} async-done(((bf16[4,256,1408]{2,1,0:T(8,128)(2,1)}), bf16[4,256,1408]{2,1,0:T(8,128)(2,1)}, u32[]{:S(2)}, u32[]{:S(2)}) %all-to-all-start.6) | async-done | bytes 2883616 | tf_op jit(solution)/shard_map/all_to_all | solution.py:122
  799.7 7.2 copy.235
  810.5 11.8 %psum.7 = f32[2,512]{1,0:T(2,128)S(1)} all-reduce(f32[2,512]{1,0:T(2,128)S(1)} %pad_maximum_fusion.33), channel_id=1, replica_groups=mesh['wide'=8,'narrow'=4] {'wide'}, use_global_device_ids=true, to_apply=%region_39.40 | all-reduce | flops 1024 | bytes 8192 | tf_op jit(solution)/shard_map/psum | solution.py:342
  822.9 44.4 %reduce-scatter.17.cloned.1.call-done = bf16[256,2048]{0,1:T(8,128)(2,1)} async-done(((bf16[2048,2048]{0,1:T(8,128)(2,1)}), bf16[256,2048]{0,1:T(8,128)(2,1)}) %reduce-scatter.17.cloned.1.call-update) | async-done | bytes 1048592 | tf_op jit(solution)/shard_map/reduce_scatter | solution.py:338
  (453 shorter events, 127.8 us)
Async XLA Ops:
  7.2 16.9 %copy-start.106 = (s32[1,256]{1,0:T(1,128)S(1)}, s32[1,256]{1,0:T(1,128)}, u32[]{:S(2)}) copy-start(s32[1,256]{1,0:T(1,128)} %param.27) | copy-start | bytes 3076
  7.2 17.0 %copy-start.107 = (s32[1,13]{1,0:T(1,128)S(1)}, s32[1,13]{1,0:T(1,128)}, u32[]{:S(2)}) copy-start(s32[1,13]{1,0:T(1,128)} %param.28) | copy-start | bytes 160
  7.2 33.1 %all-gather.9.cloned.1.call-start = ((), (), s32[]{:S(2)}) async-start(), calls=%async_computation.16 | async-start | bytes 1310720 | tf_op jit(solution)/shard_map/all_gather | solution.py:154
  8.0 88.7 %all-gather.11.cloned.1.call-start = ((), (), s32[]{:S(2)}) async-start(), calls=%async_computation.17 | async-start | bytes 9437184 | tf_op jit(solution)/shard_map/all_gather | solution.py:149
  10.3 128.5 %reduce-scatter.15.cloned.1.call-start = ((), (), s32[]{:S(2)}) async-start(), calls=%async_computation.18 | async-start | bytes 1310720 | tf_op jit(solution)/shard_map/reduce_scatter | solution.py:198
  96.7 7.1 copy-start.5
  100.2 6.3 copy-start.31
  100.2 6.2 copy-start.33
  100.2 7.8 copy-start.39
  100.2 7.8 copy-start.41
  109.8 29.1 %copy-start.17 = (bf16[256,512]{1,0:T(8,128)(2,1)S(1)}, bf16[256,512]{1,0:T(8,128)(2,1)}, u32[]{:S(2)}) copy-start(bf16[256,512]{1,0:T(8,128)(2,1)} %param.16) | copy-start | bytes 786436
  111.6 153.9 %all-gather.13.cloned.1.call-start = ((), (), s32[]{:S(2)}) async-start(), calls=%async_computation.19 | async-start | bytes 1310720 | tf_op jit(solution)/shard_map/all_gather | solution.py:202
  144.3 38.1 %all-to-all-start.1 = ((bf16[4,256,1408]{2,1,0:T(8,128)(2,1)}), bf16[4,256,1408]{2,1,0:T(8,128)(2,1)}, u32[]{:S(2)}, u32[]{:S(2)}) async-start(bf16[4,256,1408]{2,1,0:T(8,128)(2,1)} %bitcast.141), calls=%async_computation.2 | async-start | bytes 5767168 | tf_op jit(solution)/shard_map/all_to_all | solution.py:122
  148.9 121.5 %all-gather.15.cloned.1.call-start = ((), (), s32[]{:S(2)}) async-start(), calls=%async_computation.20 | async-start | bytes 1310720 | tf_op jit(solution)/shard_map/all_gather | solution.py:155
  149.5 226.3 %all-gather.17.cloned.1.call-start = ((), (), s32[]{:S(2)}) async-start(), calls=%async_computation.21 | async-start | bytes 8650752 | tf_op jit(solution)/shard_map/all_gather | solution.py:126
  182.4 202.2 %all-gather.19.cloned.1.call-start = ((), (), s32[]{:S(2)}) async-start(), calls=%async_computation.22 | async-start | bytes 8650752 | tf_op jit(solution)/shard_map/all_gather | solution.py:126
  225.0 40.1 %copy-start.92 = (s32[256,2]{0,1:T(2,128)S(1)}, s32[256,2]{0,1:T(2,128)}, u32[]{:S(2)}) copy-start(s32[256,2]{0,1:T(2,128)} %param.29) | copy-start | bytes 6148
  225.0 40.2 %copy-start.109 = (s32[1,256]{1,0:T(1,128)S(1)}, s32[1,256]{1,0:T(1,128)}, u32[]{:S(2)}) copy-start(s32[1,256]{1,0:T(1,128)} %param.30) | copy-start | bytes 3076
  225.0 51.1 %all-to-all-start.3 = ((bf16[4,256,1408]{2,1,0:T(8,128)(2,1)}), bf16[4,256,1408]{2,1,0:T(8,128)(2,1)}, u32[]{:S(2)}, u32[]{:S(2)}) async-start(bf16[4,256,1408]{2,1,0:T(8,128)(2,1)} %bitcast.140), calls=%async_computation.4 | async-start | bytes 5767168 | tf_op jit(solution)/shard_map/all_to_all | solution.py:122
  267.0 5.5 copy-start.75
  276.1 60.4 %all-to-all-start = ((bf16[4,144,4224]{2,1,0:T(8,128)(2,1)}), bf16[4,144,4224]{2,1,0:T(8,128)(2,1)}, u32[]{:S(2)}, u32[]{:S(2)}) async-start(bf16[4,144,4224]{2,1,0:T(8,128)(2,1)} %bitcast.137), calls=%async_computation.1 | async-start | bytes 9732096 | tf_op jit(solution)/shard_map/all_to_all | solution.py:122
  281.1 112.5 %all-gather.21.cloned.1.call-start = ((), (), s32[]{:S(2)}) async-start(), calls=%async_computation.23 | async-start | bytes 8650752 | tf_op jit(solution)/shard_map/all_gather | solution.py:126
  281.8 304.4 %reduce-scatter.25.cloned.1.call-start = ((), (), s32[]{:S(2)}) async-start(), calls=%async_computation.29 | async-start | bytes 7372800
  375.8 17.8 %copy-start.93 = (f32[576]{0:T(1024)}, f32[576]{0:T(1024)S(1)}, u32[]{:S(2)}) copy-start(f32[576]{0:T(1024)S(1)} %fusion.32) | copy-start | bytes 6916
  404.5 7.1 copy-start.112
  404.5 7.1 copy-start.113
  404.5 7.2 copy-start.16
  404.5 7.2 copy-start.108
  462.4 6.6 copy-start.2
  462.4 8.2 copy-start.3
  588.8 20.5 %all-to-all-start.4 = ((bf16[4,144,1152]{2,1,0:T(8,128)(2,1)}), bf16[4,144,1152]{2,1,0:T(8,128)(2,1)S(1)}, u32[]{:S(2)}, u32[]{:S(2)}) async-start(bf16[4,144,1152]{2,1,0:T(8,128)(2,1)} %bitcast.150), calls=%async_computation.5 | async-start | bytes 2654208 | tf_op jit(solution)/shard_map/all_to_all | solution.py:122
  592.4 61.4 %all-gather.23.cloned.1.call-start = ((), (), s32[]{:S(2)}) async-start(), calls=%async_computation.24 | async-start | bytes 1310720 | tf_op jit(solution)/shard_map/all_gather | solution.py:289
  624.8 55.8 %reduce-scatter.23.cloned.1.call-start = ((), (), s32[]{:S(2)}) async-start(), calls=%async_computation.28 | async-start | bytes 8650752 | tf_op jit(solution)/shard_map/reduce_scatter | solution.py:143
  633.7 53.1 %reduce-scatter.19.cloned.1.call-start = ((), (), s32[]{:S(2)}) async-start(), calls=%async_computation.26 | async-start | bytes 8650752 | tf_op jit(solution)/shard_map/reduce_scatter | solution.py:143
  642.3 80.5 %reduce-scatter.21.cloned.1.call-start = ((), (), s32[]{:S(2)}) async-start(), calls=%async_computation.27 | async-start | bytes 8650752 | tf_op jit(solution)/shard_map/reduce_scatter | solution.py:143
  651.4 115.3 %reduce-scatter.29.cloned.1.call-start = ((), (), s32[]{:S(2)}) async-start(), calls=%async_computation.31 | async-start | bytes 1179648
  653.8 153.1 %reduce-scatter.27.cloned.1.call-start = ((), (), s32[]{:S(2)}) async-start(), calls=%async_computation.30 | async-start | bytes 1638400
  653.8 11.5 %slice-start = ((s8[8388608]{0:T(1024)(128)(4,1)}), s8[4194304]{0:T(1024)(128)(4,1)S(1)}, s32[]{:S(2)}) async-start(s8[8388608]{0:T(1024)(128)(4,1)} %bitcast.152), calls=%async_computation.32 | async-start | bytes 8388608
  656.9 10.0 %copy-start.51 = (bf16[256,128]{0,1:T(8,128)(2,1)}, bf16[256,128]{0,1:T(8,128)(2,1)S(1)}, u32[]{:S(2)}) copy-start(bf16[256,128]{0,1:T(8,128)(2,1)S(1)} %convolution_convert_fusion.14) | copy-start | bytes 196612
  657.2 9.8 %copy-start.53 = (bf16[256,128]{0,1:T(8,128)(2,1)}, bf16[256,128]{0,1:T(8,128)(2,1)S(1)}, u32[]{:S(2)}) copy-start(bf16[256,128]{0,1:T(8,128)(2,1)S(1)} %convolution_convert_fusion.13) | copy-start | bytes 196612
  657.6 9.4 %copy-start.55 = (bf16[256,128]{0,1:T(8,128)(2,1)}, bf16[256,128]{0,1:T(8,128)(2,1)S(1)}, u32[]{:S(2)}) copy-start(bf16[256,128]{0,1:T(8,128)(2,1)S(1)} %convolution_convert_fusion.12) | copy-start | bytes 196612
  657.8 9.2 %copy-start.57 = (bf16[256,128]{0,1:T(8,128)(2,1)}, bf16[256,128]{0,1:T(8,128)(2,1)S(1)}, u32[]{:S(2)}) copy-start(bf16[256,128]{0,1:T(8,128)(2,1)S(1)} %convolution_convert_fusion.11) | copy-start | bytes 196612
  658.1 7.3 slice-start.1
  671.3 196.0 %reduce-scatter.17.cloned.1.call-start = ((), (), s32[]{:S(2)}) async-start(), calls=%async_computation.25 | async-start | bytes 9437184 | tf_op jit(solution)/shard_map/reduce_scatter | solution.py:338
  680.6 37.6 %all-to-all-start.7 = ((bf16[4,256,1408]{2,1,0:T(8,128)(2,1)}), bf16[4,256,1408]{2,1,0:T(8,128)(2,1)}, u32[]{:S(2)}, u32[]{:S(2)}) async-start(bf16[4,256,1408]{2,1,0:T(8,128)(2,1)} %bitcast.156), calls=%async_computation.12 | async-start | bytes 5767168 | tf_op jit(solution)/shard_map/all_to_all | solution.py:122
  718.2 41.7 %all-to-all-start.5 = ((bf16[4,256,1408]{2,1,0:T(8,128)(2,1)}), bf16[4,256,1408]{2,1,0:T(8,128)(2,1)}, u32[]{:S(2)}, u32[]{:S(2)}) async-start(bf16[4,256,1408]{2,1,0:T(8,128)(2,1)} %bitcast.155), calls=%async_computation.8 | async-start | bytes 5767168 | tf_op jit(solution)/shard_map/all_to_all | solution.py:122
  759.9 37.6 %all-to-all-start.6 = ((bf16[4,256,1408]{2,1,0:T(8,128)(2,1)}), bf16[4,256,1408]{2,1,0:T(8,128)(2,1)}, u32[]{:S(2)}, u32[]{:S(2)}) async-start(bf16[4,256,1408]{2,1,0:T(8,128)(2,1)} %bitcast.154), calls=%async_computation.10 | async-start | bytes 5767168 | tf_op jit(solution)/shard_map/all_to_all | solution.py:122
  799.6 8.6 copy-start.19
  (91 other events, 209.9 us)
Sparse Core Ops, SparseCore 0:
  9.6 30.6 all-gather.8
  42.8 53.8 all-gather.10
  111.7 27.1 reduce-scatter.14
  140.9 26.5 all-gather.12
  169.0 27.4 all-gather.14
  198.0 15.4 all-gather.16
  221.4 13.3 all-gather.18
  283.5 15.3 all-gather.20
  483.9 102.2 reduce-scatter.24
  624.9 27.5 all-gather.22
  655.5 13.4 reduce-scatter.22
  671.7 15.0 reduce-scatter.18
  689.7 15.0 reduce-scatter.20
  707.9 49.9 reduce-scatter.28
  760.0 33.7 reduce-scatter.26
  797.1 70.0 reduce-scatter.16

commit v2 on v1

--- a/solution.py
+++ b/solution.py
@@ -1,6 +1,8 @@
 import jax
 import jax.numpy as jnp
 from jax import lax
+from jax.experimental import pallas as pl
+from jax.experimental.pallas import tpu as pltpu
 from jax.sharding import PartitionSpec as P
 
 HEAD_DIM = 128
@@ -94,6 +96,471 @@
 def two_parts(column):
     high = column.astype(BF)
     return high, (column - high.astype(F32)).astype(BF)
+
+
+MESH = pl.DeviceIdType.MESH
+NEAR = 3
+
+
+def low_dot(left, right):
+    return jnp.dot(left, right, preferred_element_type=F32)
+
+
+def places_of(n):
+    return [lax.rem(n + step, 4) for step in (1, 2, 3)], [lax.rem(n + 4 - step, 4) for step in (1, 2, 3)]
+
+
+def plane_of(chip):
+    x, y = lax.rem(chip, 2), chip // 2
+    return [2 * y + 1 - x, 2 * (1 - y) + x, 2 * (1 - y) + 1 - x]
+
+
+def greet(narrow_peers, plane_peers, chip, core, mate):
+    barrier = pltpu.get_barrier_semaphore()
+    count = 0
+    for peer in narrow_peers:
+        pl.semaphore_signal(barrier, inc=1, device_id={"narrow": peer}, device_id_type=MESH)
+        count += 1
+    for peer in plane_peers:
+        pl.semaphore_signal(
+            barrier, inc=1, device_id={"wide": 2 * peer + core}, device_id_type=MESH
+        )
+        count += 1
+    if mate:
+        pl.semaphore_signal(
+            barrier, inc=1, device_id={"wide": 2 * chip + 1 - core}, device_id_type=MESH
+        )
+        count += 1
+    pl.semaphore_wait(barrier, count)
+
+
+class Links:
+    def __init__(self, sent, landed, local):
+        self.sent, self.landed, self.local = sent, landed, local
+        self.used, self.local_used = 0, 0
+        self.waits = []
+
+    def slot(self):
+        self.used += 1
+        return self.used - 1
+
+    def send(self, source, target, device, slot, when=None):
+        copy = pltpu.make_async_remote_copy(
+            src_ref=source,
+            dst_ref=target,
+            send_sem=self.sent.at[slot],
+            recv_sem=self.landed.at[slot],
+            device_id=device,
+            device_id_type=MESH,
+        )
+        if when is None:
+            copy.start()
+        else:
+            pl.when(when)(copy.start)
+        self.waits.append((copy, when))
+
+    def land(self, target, device, slot, when=None):
+        copy = pltpu.make_async_remote_copy(
+            src_ref=target,
+            dst_ref=target,
+            send_sem=self.sent.at[slot],
+            recv_sem=self.landed.at[slot],
+            device_id=device,
+            device_id_type=MESH,
+        )
+        if when is None:
+            copy.wait_recv()
+        else:
+            pl.when(when)(copy.wait_recv)
+
+    def move(self, source, target):
+        copy = pltpu.make_async_copy(source, target, self.local.at[self.local_used])
+        self.local_used += 1
+        copy.start()
+        self.waits.append((copy, "local"))
+        return copy
+
+    def finish(self):
+        for copy, when in self.waits:
+            if when == "local":
+                copy.wait()
+            elif when is None:
+                copy.wait_send()
+            else:
+                pl.when(when)(copy.wait_send)
+
+
+class Chain:
+    def __init__(self, links, n, block):
+        self.links, self.n, self.block = links, n, block
+        self.slots = [(links.slot(), links.slot()) for _ in range(3)]
+
+    def start(self, step):
+        n, links = self.n, self.links
+        right, left = self.slots[step]
+        block = self.block(lax.rem(n + 4 - step, 4))
+        links.send(
+            block, block, {"narrow": lax.rem(n + 1, 4)}, right,
+            (n < 3) & (n >= step),
+        )
+        block = self.block(lax.rem(n + step, 4))
+        links.send(
+            block, block, {"narrow": lax.rem(n + 3, 4)}, left,
+            (n > 0) & (n + step <= 3),
+        )
+
+    def land(self, step):
+        n, links = self.n, self.links
+        right, left = self.slots[step]
+        links.land(
+            self.block(lax.rem(n + 7 - step, 4)), {"narrow": lax.rem(n + 3, 4)}, right,
+            n >= step + 1,
+        )
+        links.land(
+            self.block(lax.rem(n + 1 + step, 4)), {"narrow": lax.rem(n + 1, 4)}, left,
+            n + 1 + step <= 3,
+        )
+
+
+FRONT_SLOTS = 72
+
+
+def front_body(
+    tok_ref, cot_ref, gains_ref, wq_ref, wk_ref, wv_ref, wo_ref, router_ref, moved_ref,
+    rows_ref, cols_ref, freq_ref,
+    qkvw_out, outw_out, expert_out, x_out, dy_out, gate_out, middle_out, hidden_out,
+    tokens_out, qkv_out, prob_out, att_out, stat_out, rope_out, pick_out,
+    pack, tok_pack, qkvw, outw, cot_send, y_send, br_send, br_recv, stat_send, stat_recv,
+    gate_send, sent, landed, local,
+):
+    n = lax.axis_index("narrow")
+    w = lax.axis_index("wide")
+    chip, core = w // 2, lax.rem(w, 2)
+    to_z, from_z = places_of(n)
+    plane = plane_of(chip)
+    links = Links(sent, landed, local)
+    mate = {"wide": 2 * chip + 1 - core}
+
+    def at_plane(peer):
+        return {"wide": 2 * peer + core}
+
+    token_count, part_width = tok_ref.shape
+    greet(to_z, plane, chip, core, True)
+
+    tok_pack[0:token_count, :] = tok_ref[...]
+    tok_pack[token_count : token_count + 2, :] = gains_ref[...]
+    tok_slots = [links.slot() for _ in range(NEAR)]
+    for step in range(NEAR):
+        links.send(tok_pack, tokens_out.at[n], {"narrow": to_z[step]}, tok_slots[step])
+    pack[:, 0:512] = wq_ref[...]
+    pack[:, 512:1024] = wk_ref[...]
+    pack[:, 1024:1536] = wv_ref[...]
+    pack[:, 1536:1664] = router_ref[...]
+    in_slots = [links.slot() for _ in range(NEAR)]
+    for step in range(NEAR):
+        links.send(pack, qkvw.at[w], at_plane(plane[step]), in_slots[step])
+    in_mate = [links.slot() for _ in range(4)]
+    links.send(pack, qkvw.at[w], mate, in_mate[3])
+    out_slots = [links.slot() for _ in range(NEAR)]
+    for step in range(NEAR):
+        links.send(wo_ref, outw.at[w], at_plane(plane[step]), out_slots[step])
+    out_mate = [links.slot() for _ in range(4)]
+    links.send(wo_ref, outw.at[w], mate, out_mate[3])
+    tokens_out[n] = tok_pack[...]
+    qkvw[w] = pack[...]
+    outw[w] = wo_ref[...]
+
+    wide_shape = (token_count, token_count)
+    row_at = lax.broadcasted_iota(jnp.int32, wide_shape, 0)
+    col_at = lax.broadcasted_iota(jnp.int32, wide_shape, 1)
+    seg_row, rank_row = rows_ref[0:1, :], rows_ref[2:3, :]
+    seg_col, par_col, rank_col = cols_ref[:, 0:1], cols_ref[:, 1:2], cols_ref[:, 2:3]
+    seen = ((seg_row == seg_col) | (seg_row == par_col) | (seg_row == 0)) & (col_at <= row_at)
+    spots = jnp.sum(jnp.where(seen, 1.0, 0.0), 1, keepdims=True) - 1.0
+    angles = spots * freq_ref[...]
+    cosines = jnp.cos(angles)
+    lane_at = lax.broadcasted_iota(jnp.int32, angles.shape, 1)
+    sines = jnp.sin(angles) * jnp.where(lane_at < HEAD_DIM // 2, -1.0, 1.0)
+    rope_out[0] = cosines
+    rope_out[1] = sines
+    kind = lax.broadcasted_iota(jnp.int32, (8, token_count), 0)
+    first_row, second_row = rows_ref[3:4, :], rows_ref[4:5, :]
+    hot_first = jnp.where(kind == first_row, 1.0, 0.0)
+    hot_second = jnp.where(kind == second_row, 1.0, 0.0)
+    earlier = jnp.where(rank_col < rank_row, 1.0, 0.0).astype(BF)
+    count_first = low_dot(hot_first.astype(BF), earlier)
+    count_second = low_dot(hot_second.astype(BF), earlier)
+    count_second = count_second + jnp.sum(hot_first, 1, keepdims=True)
+    slot_first = jnp.sum(count_first * hot_first, 0, keepdims=True)
+    slot_second = jnp.sum(count_second * hot_second, 0, keepdims=True)
+    kept_first = jnp.where(slot_first < CAP, 1.0, 0.0)
+    kept_second = jnp.where(slot_second < CAP, 1.0, 0.0)
+    flat_first = jnp.where(slot_first < CAP, first_row * CAP + slot_first.astype(jnp.int32), SLOTS)
+    flat_second = jnp.where(
+        slot_second < CAP, second_row * CAP + slot_second.astype(jnp.int32), SLOTS
+    )
+    slot_at = lax.broadcasted_iota(jnp.int32, (SLOTS, token_count), 0)
+    pick_first = jnp.where(slot_at == flat_first, 1.0, 0.0)
+    pick_second = jnp.where(slot_at == flat_second, 1.0, 0.0)
+    pick_out[0] = pick_first.astype(BF)
+    pick_out[1] = pick_second.astype(BF)
+    pick_both = (pick_first + pick_second).astype(BF)
+
+    def column_block(array):
+        return lambda m: array.at[:, pl.ds(pl.multiple_of(m * part_width, part_width), part_width)]
+
+    def slot_block(array, owner):
+        return array.at[
+            pl.ds(pl.multiple_of(owner * CAP, 16), CAP),
+            pl.ds(pl.multiple_of(n * part_width, part_width), part_width),
+        ]
+
+    def dispatch(rows, buffer, array):
+        slots = [links.slot() for _ in range(NEAR)]
+        buffer[...] = low_dot(pick_both, rows).astype(BF)
+        for step in range(NEAR):
+            links.send(
+                buffer.at[pl.ds(pl.multiple_of(plane[step] * CAP, 16), CAP), :],
+                slot_block(array, chip), at_plane(plane[step]), slots[step],
+            )
+        own = links.move(
+            buffer.at[pl.ds(pl.multiple_of(chip * CAP, 16), CAP), :], slot_block(array, chip)
+        )
+        return slots, own
+
+    def arrive(array, state):
+        slots, own = state
+        for step in range(NEAR):
+            links.land(slot_block(array, plane[step]), at_plane(plane[step]), slots[step])
+        own.wait()
+        links.waits = [item for item in links.waits if item[0] is not own]
+
+    dy_state = dispatch(cot_ref[...], cot_send, dy_out)
+    dy_chain = Chain(links, n, column_block(dy_out))
+
+    for step in range(NEAR):
+        links.land(tokens_out.at[from_z[step]], {"narrow": from_z[step]}, tok_slots[step])
+    total = jnp.zeros((token_count, 1), F32)
+    for m in range(4):
+        part = tokens_out[m, 0:token_count, :].astype(F32)
+        total = total + jnp.sum(part * part, 1, keepdims=True)
+    scale_first = lax.rsqrt(total * (1.0 / (4 * part_width)) + NORM_EPS)
+    for m in range(4):
+        part = tokens_out[m, 0:token_count, :].astype(F32)
+        gain = tokens_out[m, token_count : token_count + 1, :].astype(F32)
+        hidden_out[:, m * part_width : (m + 1) * part_width] = (part * scale_first * gain).astype(BF)
+
+    arrive(dy_out, dy_state)
+    dy_chain.start(0)
+
+    for step in range(NEAR):
+        owner = 2 * plane[step] + core
+        links.land(qkvw.at[owner], at_plane(plane[step]), in_slots[step])
+        links.send(qkvw.at[owner], qkvw.at[owner], mate, in_mate[step])
+    for step in range(NEAR):
+        links.land(qkvw.at[2 * plane[step] + 1 - core], mate, in_mate[step])
+    links.land(qkvw.at[2 * chip + 1 - core], mate, in_mate[3])
+    saved_in = links.move(qkvw, qkvw_out)
+
+    expert_slots = [[links.slot() for _ in range(NEAR)] for _ in range(3)]
+    expert_mate = [[links.slot() for _ in range(4)] for _ in range(3)]
+    for kind_at in range(3):
+        for step in range(NEAR):
+            links.send(
+                moved_ref.at[kind_at, plane[step]], expert_out.at[kind_at, chip, core],
+                at_plane(plane[step]), expert_slots[kind_at][step],
+            )
+        links.send(
+            moved_ref.at[kind_at, chip], expert_out.at[kind_at, chip, core], mate,
+            expert_mate[kind_at][3],
+        )
+        links.move(moved_ref.at[kind_at, chip], expert_out.at[kind_at, chip, core])
+
+    def pass_on(kind_at):
+        for step in range(NEAR):
+            block = expert_out.at[kind_at, plane[step], core]
+            links.land(block, at_plane(plane[step]), expert_slots[kind_at][step])
+            links.send(block, block, mate, expert_mate[kind_at][step])
+
+    def all_there(kind_at):
+        for step in range(NEAR):
+            links.land(
+                expert_out.at[kind_at, plane[step], 1 - core], mate, expert_mate[kind_at][step]
+            )
+        links.land(expert_out.at[kind_at, chip, 1 - core], mate, expert_mate[kind_at][3])
+
+    dy_chain.land(0)
+    dy_chain.start(1)
+
+    hidden = hidden_out[...]
+    score_scale = HEAD_DIM ** (-0.5)
+    raws = []
+    for part in range(3):
+        weight = qkvw[:, :, part * 512 : (part + 1) * 512].reshape(4 * part_width, part_width)
+        raws.append(low_dot(hidden, weight))
+    for head in range(part_width // HEAD_DIM):
+        cols = slice(head * HEAD_DIM, (head + 1) * HEAD_DIM)
+        turned = []
+        for part in range(2):
+            raw = raws[part][:, cols]
+            turned.append(
+                (raw * cosines + pltpu.roll(raw, HEAD_DIM // 2, 1) * sines).astype(BF)
+            )
+            qkv_out[part, :, cols] = turned[part]
+        value = raws[2][:, cols].astype(BF)
+        qkv_out[2, :, cols] = value
+        scores = rows_rows(turned[0], turned[1]) * score_scale
+        scores = jnp.where(seen, scores, NEG_FILL)
+        exps = jnp.exp(scores - jnp.max(scores, 1, keepdims=True))
+        weights = exps / jnp.sum(exps, 1, keepdims=True)
+        prob_out[head] = weights
+        att_out[:, cols] = low_dot(weights.astype(BF), value).astype(BF)
+
+    dy_chain.land(1)
+    dy_chain.start(2)
+
+    for step in range(NEAR):
+        owner = 2 * plane[step] + core
+        links.land(outw.at[owner], at_plane(plane[step]), out_slots[step])
+        links.send(outw.at[owner], outw.at[owner], mate, out_mate[step])
+    for step in range(NEAR):
+        links.land(outw.at[2 * plane[step] + 1 - core], mate, out_mate[step])
+    links.land(outw.at[2 * chip + 1 - core], mate, out_mate[3])
+    links.move(outw, outw_out)
+
+    attended = att_out[...]
+
+    def branch(m):
+        weight = outw[pl.ds(2 * m, 2)].reshape(part_width, part_width)
+        return rows_rows(attended, weight)
+
+    br_slots = [links.slot() for _ in range(NEAR)]
+    for step in range(NEAR):
+        br_send[step] = branch(to_z[step]).astype(BF)
+        links.send(br_send.at[step], br_recv.at[step], {"narrow": to_z[step]}, br_slots[step])
+    middle = tok_ref[...].astype(F32) + branch(n)
+    for step in range(NEAR):
+        links.land(br_recv.at[step], {"narrow": from_z[step]}, br_slots[step])
+        middle = middle + br_recv[step].astype(F32)
+    middle_out[...] = middle
+    x_state = dispatch(middle.astype(BF), y_send, x_out)
+    x_chain = Chain(links, n, column_block(x_out))
+
+    gain_second = gains_ref[1:2, :].astype(F32)
+    router = qkvw[pl.ds(2 * n, 2), :, 1536:1664].reshape(part_width, 128)
+    logit_part = mm(router, (middle * gain_second).astype(BF), ((0,), (1,)))[0:8, :]
+    square = middle * middle
+    square_high = square.astype(BF)
+    square_low = (square - square_high.astype(F32)).astype(BF)
+    ones = jnp.ones((8, part_width), BF)
+    square_sum = rows_rows(ones, square_high) + rows_rows(ones, square_low)
+    stat = jnp.where(kind == 4, square_sum, logit_part)
+    stat_send[...] = stat
+    stat_slots = [links.slot() for _ in range(NEAR)]
+    for step in range(NEAR):
+        links.send(stat_send, stat_recv.at[step], {"narrow": to_z[step]}, stat_slots[step])
+
+    arrive(x_out, x_state)
+    x_chain.start(0)
+    for step in range(NEAR):
+        links.land(stat_recv.at[step], {"narrow": from_z[step]}, stat_slots[step])
+        stat = stat + stat_recv[step]
+    stat_out[...] = stat
+    scale_row = lax.rsqrt(stat[4:5, :] * (1.0 / (4 * part_width)) + NORM_EPS)
+    logits = jnp.where(kind < EXPERTS, stat * scale_row, NEG_FILL)
+    chances = jnp.exp(logits - jnp.max(logits, 0, keepdims=True))
+    chances = chances / jnp.sum(chances, 0, keepdims=True)
+    share_first = jnp.sum(chances * hot_first, 0, keepdims=True)
+    share_second = jnp.sum(chances * hot_second, 0, keepdims=True)
+    both = share_first + share_second
+    weighted = pick_first * (share_first / both) + pick_second * (share_second / both)
+    slot_gate = jnp.sum(weighted, 1, keepdims=True)
+    gate_send[...] = jnp.broadcast_to(slot_gate, (SLOTS, 128))
+
+    def gate_rows(array, owner):
+        return array.at[pl.ds(pl.multiple_of(owner * CAP, 16), CAP), :]
+
+    gate_slots = [links.slot() for _ in range(NEAR)]
+    for step in range(NEAR):
+        links.send(
+            gate_rows(gate_send, plane[step]), gate_rows(gate_out, chip),
+            at_plane(plane[step]), gate_slots[step],
+        )
+    links.move(gate_rows(gate_send, chip), gate_rows(gate_out, chip))
+
+    pass_on(0)
+    x_chain.land(0)
+    x_chain.start(1)
+    x_chain.land(1)
+    x_chain.start(2)
+    pass_on(1)
+    x_chain.land(2)
+    dy_chain.land(2)
+    for step in range(NEAR):
+        links.land(gate_rows(gate_out, plane[step]), at_plane(plane[step]), gate_slots[step])
+    pass_on(2)
+    for kind_at in range(3):
+        all_there(kind_at)
+    links.finish()
+
+
+def front_call(tokens, cotangent, gains, weights, router, moved, rows, cols, freqs):
+    token_count, part_width = tokens.shape
+    full = 4 * part_width
+    hidden_width = moved.shape[3]
+    rows_each = moved.shape[2]
+    heads = part_width // HEAD_DIM
+    vmem = pl.BlockSpec(memory_space=pltpu.VMEM)
+    hbm = pl.BlockSpec(memory_space=pl.ANY)
+
+    def arr(shape, dtype):
+        return jax.ShapeDtypeStruct(shape, dtype)
+
+    return pl.pallas_call(
+        front_body,
+        out_shape=(
+            arr((8, rows_each, 1664), BF),
+            arr((8, rows_each, part_width), BF),
+            arr((3, 4, 2, rows_each, hidden_width), BF),
+            arr((SLOTS, full), BF),
+            arr((SLOTS, full), BF),
+            arr((SLOTS, 128), F32),
+            arr((token_count, part_width), F32),
+            arr((token_count, full), BF),
+            arr((4, token_count + 16, part_width), BF),
+            arr((3, token_count, part_width), BF),
+            arr((heads, token_count, token_count), F32),
+            arr((token_count, part_width), BF),
+            arr((8, token_count), F32),
+            arr((2, token_count, HEAD_DIM), F32),
+            arr((2, SLOTS, token_count), BF),
+        ),
+        in_specs=[vmem] * 8 + [hbm] + [vmem] * 3,
+        out_specs=(hbm, hbm, hbm) + (vmem,) * 12,
+        scratch_shapes=[
+            pltpu.VMEM((rows_each, 1664), BF),
+            pltpu.VMEM((token_count + 16, part_width), BF),
+            pltpu.VMEM((8, rows_each, 1664), BF),
+            pltpu.VMEM((8, rows_each, part_width), BF),
+            pltpu.VMEM((SLOTS, part_width), BF),
+            pltpu.VMEM((SLOTS, part_width), BF),
+            pltpu.VMEM((NEAR, token_count, part_width), BF),
+            pltpu.VMEM((NEAR, token_count, part_width), BF),
+            pltpu.VMEM((8, token_count), F32),
+            pltpu.VMEM((NEAR, 8, token_count), F32),
+            pltpu.VMEM((SLOTS, 128), F32),
+            pltpu.SemaphoreType.DMA((FRONT_SLOTS,)),
+            pltpu.SemaphoreType.DMA((FRONT_SLOTS,)),
+            pltpu.SemaphoreType.DMA((16,)),
+        ],
+        compiler_params=pltpu.CompilerParams(
+            collective_id=0, has_side_effects=True, vmem_limit_bytes=60 * 1024 * 1024
+        ),
+        cost_estimate=pl.CostEstimate(
+            flops=6_000_000_000, bytes_accessed=60_000_000, transcendentals=400_000
+        ),
+        name="front",
+    )(tokens, cotangent, gains, *weights, router, moved, rows, cols, freqs)
 
 
 def per_device(
@@ -124,104 +591,143 @@
     def own_rows(weight):
         moved = quad_swap(jnp.transpose(weight, (1, 0, 2)))
         joined = lax.all_gather(moved, "wide", axis=0, axis_index_groups=mates, tiled=True)
+        joined = joined.reshape(blocks, 2, 4, rows_each, hidden_width).transpose(0, 2, 1, 3, 4)
         return joined.reshape(full_width, hidden_width)
 
-    def mixed_features(rows):
-        count = rows.shape[0]
-        return rows.reshape(count, blocks, 4, 2, rows_each).transpose(0, 1, 3, 2, 4).reshape(
-            count, full_width
-        )
-
-    def plain_features(rows):
-        count = rows.shape[0]
-        return rows.reshape(count, blocks, 2, 4, rows_each).transpose(0, 1, 3, 2, 4).reshape(
-            count, full_width
-        )
-
     def share_rows(grad):
-        parts = grad.astype(BF).reshape(blocks * 2, 4, rows_each, hidden_width)
+        parts = grad.astype(BF).reshape(blocks, 4, 2, rows_each, hidden_width)
+        parts = parts.transpose(0, 2, 1, 3, 4).reshape(blocks * 2, 4, rows_each, hidden_width)
         summed = lax.psum_scatter(
             parts, "wide", scatter_dimension=0, axis_index_groups=mates, tiled=True
         )[0]
         return jnp.transpose(quad_swap(summed), (1, 0, 2)).astype(F32)
 
-    gate_w, up_w, down_w = own_rows(w_gate), own_rows(w_up), own_rows(w_down)
-    attn_w = lax.all_gather(
-        jnp.stack([w_query, w_key, w_value, w_out], 1), "wide", axis=0, tiled=True
-    )
-    query_w, key_w, value_w, out_w = (attn_w[:, i] for i in range(4))
-    router_w = lax.all_gather(w_router, "wide", axis=0, tiled=True)
-    tokens_full = lax.all_gather(tokens, "narrow", axis=1, tiled=True)
-    grad_full = lax.all_gather(cotangent, "narrow", axis=1, tiled=True)
-    gains_full = lax.all_gather(jnp.stack([gain_attn, gain_ffn]), "narrow", axis=1, tiled=True)
-    gain_first = gains_full[0].astype(F32)
-    gain_second = gains_full[1].astype(F32)
-    gain_first_loc = gain_attn.astype(F32)
-    gain_second_loc = gain_ffn.astype(F32)
-
-    seen, places = tree_layout(segment[0], parents[0])
-    hot_first, hot_second, kept, pick_first, pick_second = route(expert_ids, slot_order[0])
-    pick_first_low = pick_first.astype(BF)
-    pick_second_low = pick_second.astype(BF)
-    pick_both_low = (pick_first | pick_second).astype(BF)
-
-    inputs_full = tokens_full.astype(F32)
-    scale_first = lax.rsqrt(jnp.mean(inputs_full * inputs_full, -1, keepdims=True) + NORM_EPS)
-    normed_first = inputs_full * scale_first
-    hidden_first = (normed_first * gain_first).astype(BF)
+    def head_cols(array, head):
+        return array[:, head * HEAD_DIM : (head + 1) * HEAD_DIM]
+
     heads = part_width // HEAD_DIM
     half_dim = HEAD_DIM // 2
     freqs = ROPE_BASE ** (-2.0 * jnp.arange(half_dim, dtype=F32) / HEAD_DIM)
-    angles = places[:, None] * freqs[None, :]
-    cosines, sines = jnp.cos(angles), jnp.sin(angles)
-    query_raw = rows_cols(hidden_first, query_w)
-    key_raw = rows_cols(hidden_first, key_w)
-    value_low = rows_cols(hidden_first, value_w).astype(BF)
     score_scale = HEAD_DIM ** (-0.5)
-
-    def head_cols(array, head):
-        return array[:, head * HEAD_DIM : (head + 1) * HEAD_DIM]
-
-    saved = []
-    outs = []
-    for head in range(heads):
-        query = rotate(head_cols(query_raw, head), cosines, sines).astype(BF)
-        key = rotate(head_cols(key_raw, head), cosines, sines).astype(BF)
-        value = head_cols(value_low, head)
-        scores = jnp.where(seen, rows_rows(query, key) * score_scale, NEG_FILL)
-        exps = jnp.exp(scores - jnp.max(scores, -1, keepdims=True))
-        weights = exps / jnp.sum(exps, -1, keepdims=True)
-        saved.append((query, key, value, weights))
-        outs.append(rows_cols(weights.astype(BF), value).astype(BF))
-    attended = jnp.concatenate(outs, 1)
-    branch_part = rows_rows(attended, out_w).astype(BF)
-    branch_loc = lax.psum_scatter(
-        branch_part, "narrow", scatter_dimension=1, tiled=True
-    ).astype(F32)
-    middle = tokens.astype(F32) + branch_loc
-    middle_full = lax.all_gather(middle.astype(BF), "narrow", axis=1, tiled=True).astype(F32)
-    scale_second = lax.rsqrt(jnp.mean(middle_full * middle_full, -1, keepdims=True) + NORM_EPS)
-    normed_second = middle_full * scale_second
-    hidden_second = (normed_second * gain_second).astype(BF)
-    logits = rows_cols(hidden_second, router_w)
-    share_first, share_second = gate_pair(logits, hot_first, hot_second)
-    weight_first = kept[:, 0] * share_first
-    weight_second = kept[:, 1] * share_second
-
-    slot_weight = jnp.sum(
-        pick_first * weight_first[:, None] + pick_second * weight_second[:, None], 0
-    )
-    weight_high, weight_low = two_parts(slot_weight)
-    pads = jnp.stack([weight_high, weight_low], 1)
-    pads = jnp.pad(pads, ((0, 0), (0, 126)))
-    sent_hidden = cols_cols(pick_both_low, hidden_second).astype(BF)
-    sent_grad = cols_cols(pick_both_low, grad_full).astype(BF)
-    sent = jnp.concatenate([sent_hidden, sent_grad, pads], 1)
-    got = quad_swap(sent.reshape(EXPERTS, CAP, -1)).reshape(SLOTS, -1)
-    slot_hidden = mixed_features(got[:, :full_width])
-    slot_grad = mixed_features(got[:, full_width : 2 * full_width])
-    slot_gate = got[:, 2 * full_width : 2 * full_width + 2].astype(F32)
-    slot_gate = slot_gate[:, 0:1] + slot_gate[:, 1:2]
+    gains = jnp.stack([gain_attn, gain_ffn])
+    gain_first_loc = gain_attn.astype(F32)
+    gain_second_loc = gain_ffn.astype(F32)
+    hot_first, hot_second, kept, pick_first, pick_second = route(expert_ids, slot_order[0])
+
+    if wide_count == 8 and narrow_count == 4:
+        seg = segment[0]
+        seg_ids = jnp.arange(SEGS, dtype=jnp.int32)
+        above = jnp.sum(jnp.where(seg[:, None] == seg_ids[None, :], parents[0][None, :], 0), 1)
+        table = jnp.stack([seg, above, slot_order[0], expert_ids[:, 0], expert_ids[:, 1]] + [seg] * 3)
+        moved = jnp.stack([jnp.transpose(item, (1, 0, 2)) for item in (w_gate, w_up, w_down)])
+        (
+            in_w, out_w8, expert_w, slot_mid, slot_grad, slot_gate, middle, hidden_first,
+            token_parts, qkv, probs, attended, stat, rope, picks,
+        ) = front_call(
+            tokens, cotangent, gains, (w_query, w_key, w_value, w_out),
+            jnp.pad(w_router, ((0, 0), (0, 124))), moved, table, table.T,
+            jnp.tile(freqs, 2)[None, :],
+        )
+        in_w = in_w.reshape(full_width, 1664)
+        query_w, key_w, value_w = (in_w[:, i * 512 : (i + 1) * 512] for i in range(3))
+        router_w = in_w[:, 1536 : 1536 + EXPERTS]
+        out_w = out_w8.reshape(full_width, part_width)
+        gate_w, up_w, down_w = (expert_w[i].reshape(full_width, hidden_width) for i in range(3))
+        slot_gate = slot_gate[:, 0:1]
+        token_rows = token_parts[:, :token_count]
+        tokens_full = jnp.concatenate([token_rows[i] for i in range(4)], 1)
+        gains_full = jnp.concatenate([token_parts[i, token_count : token_count + 2] for i in range(4)], 1)
+        cosines, sines = rope[0][:, :half_dim], rope[1][:, half_dim:]
+        inputs_full = tokens_full.astype(F32)
+        scale_first = lax.rsqrt(jnp.mean(inputs_full * inputs_full, -1, keepdims=True) + NORM_EPS)
+        normed_first = inputs_full * scale_first
+        gain_first = gains_full[0].astype(F32)
+        gain_second = gains_full[1].astype(F32)
+        saved = [
+            tuple(qkv[i, :, h * HEAD_DIM : (h + 1) * HEAD_DIM] for i in range(3)) + (probs[h],)
+            for h in range(heads)
+        ]
+        scale_second = lax.rsqrt(stat[4] / full_width + NORM_EPS)[:, None]
+        logits = stat[:EXPERTS].T * scale_second
+        slot_mid = slot_mid.astype(F32)
+        slot_scale = lax.rsqrt(jnp.mean(slot_mid * slot_mid, -1, keepdims=True) + NORM_EPS)
+        slot_hidden = (slot_mid * slot_scale * gain_second).astype(BF)
+        pick_first_low, pick_second_low = picks[0].T, picks[1].T
+        pick_both_low = pick_first_low + pick_second_low
+        share_first, share_second = gate_pair(logits, hot_first, hot_second)
+        weight_first = kept[:, 0] * share_first
+        weight_second = kept[:, 1] * share_second
+        middle_full = lax.all_gather(middle.astype(BF), "narrow", axis=1, tiled=True).astype(F32)
+        normed_second = middle_full * scale_second
+        hidden_second = (normed_second * gain_second).astype(BF)
+    else:
+        gate_w, up_w, down_w = own_rows(w_gate), own_rows(w_up), own_rows(w_down)
+        attn_w = lax.all_gather(
+            jnp.stack([w_query, w_key, w_value, w_out], 1), "wide", axis=0, tiled=True
+        )
+        query_w, key_w, value_w, out_w = (attn_w[:, i] for i in range(4))
+        router_w = lax.all_gather(w_router, "wide", axis=0, tiled=True)
+        tokens_full = lax.all_gather(tokens, "narrow", axis=1, tiled=True)
+        grad_full = lax.all_gather(cotangent, "narrow", axis=1, tiled=True)
+        gains_full = lax.all_gather(gains, "narrow", axis=1, tiled=True)
+        gain_first = gains_full[0].astype(F32)
+        gain_second = gains_full[1].astype(F32)
+
+        seen, places = tree_layout(segment[0], parents[0])
+        pick_first_low = pick_first.astype(BF)
+        pick_second_low = pick_second.astype(BF)
+        pick_both_low = (pick_first | pick_second).astype(BF)
+
+        inputs_full = tokens_full.astype(F32)
+        scale_first = lax.rsqrt(jnp.mean(inputs_full * inputs_full, -1, keepdims=True) + NORM_EPS)
+        normed_first = inputs_full * scale_first
+        hidden_first = (normed_first * gain_first).astype(BF)
+        angles = places[:, None] * freqs[None, :]
+        cosines, sines = jnp.cos(angles), jnp.sin(angles)
+        query_raw = rows_cols(hidden_first, query_w)
+        key_raw = rows_cols(hidden_first, key_w)
+        value_low = rows_cols(hidden_first, value_w).astype(BF)
+
+        saved = []
+        outs = []
+        for head in range(heads):
+            query = rotate(head_cols(query_raw, head), cosines, sines).astype(BF)
+            key = rotate(head_cols(key_raw, head), cosines, sines).astype(BF)
+            value = head_cols(value_low, head)
+            scores = jnp.where(seen, rows_rows(query, key) * score_scale, NEG_FILL)
+            exps = jnp.exp(scores - jnp.max(scores, -1, keepdims=True))
+            weights = exps / jnp.sum(exps, -1, keepdims=True)
+            saved.append((query, key, value, weights))
+            outs.append(rows_cols(weights.astype(BF), value).astype(BF))
+        attended = jnp.concatenate(outs, 1)
+        branch_part = rows_rows(attended, out_w).astype(BF)
+        branch_loc = lax.psum_scatter(
+            branch_part, "narrow", scatter_dimension=1, tiled=True
+        ).astype(F32)
+        middle = tokens.astype(F32) + branch_loc
+        middle_full = lax.all_gather(middle.astype(BF), "narrow", axis=1, tiled=True).astype(F32)
+        scale_second = lax.rsqrt(jnp.mean(middle_full * middle_full, -1, keepdims=True) + NORM_EPS)
+        normed_second = middle_full * scale_second
+        hidden_second = (normed_second * gain_second).astype(BF)
+        logits = rows_cols(hidden_second, router_w)
+        share_first, share_second = gate_pair(logits, hot_first, hot_second)
+        weight_first = kept[:, 0] * share_first
+        weight_second = kept[:, 1] * share_second
+
+        slot_weight = jnp.sum(
+            pick_first * weight_first[:, None] + pick_second * weight_second[:, None], 0
+        )
+        weight_high, weight_low = two_parts(slot_weight)
+        pads = jnp.stack([weight_high, weight_low], 1)
+        pads = jnp.pad(pads, ((0, 0), (0, 126)))
+        sent_hidden = cols_cols(pick_both_low, hidden_second).astype(BF)
+        sent_grad = cols_cols(pick_both_low, grad_full).astype(BF)
+        sent = jnp.concatenate([sent_hidden, sent_grad, pads], 1)
+        got = quad_swap(sent.reshape(EXPERTS, CAP, -1)).reshape(SLOTS, -1)
+        slot_hidden = got[:, :full_width]
+        slot_grad = got[:, full_width : 2 * full_width]
+        slot_gate = got[:, 2 * full_width : 2 * full_width + 2].astype(F32)
+        slot_gate = slot_gate[:, 0:1] + slot_gate[:, 1:2]
 
     gate_pre = rows_cols(slot_hidden, gate_w)
     up_pre = rows_cols(slot_hidden, up_w)
@@ -241,8 +747,8 @@
     extras = jnp.concatenate([*two_parts(share_part), *two_parts(stat_part)], 1)
     extras = jnp.pad(extras, ((0, 0), (0, 124)))
     back_parts = []
-    expert_plain = plain_features(expert_part.astype(BF))
-    slot_plain = plain_features(grad_slot.astype(BF))
+    expert_plain = expert_part.astype(BF)
+    slot_plain = grad_slot.astype(BF)
     for part in range(narrow_count):
         cols = slice(part * part_width, (part + 1) * part_width)
         back_parts += [expert_plain[:, cols], slot_plain[:, cols], extras]

time: 889 us -> 736 us (0.83)
  Pallas kernels: 0 us -> 221 us
  waiting for transfers between devices: 430 us -> 251 us
  blocking collectives: 97.3 us -> 12.1 us
  local copies, waits for them, and re-layouts: 146 us -> 95.3 us
  matrix products: 116 us -> 85.9 us
  starting transfers between devices: 33 us -> 17.2 us
  other arithmetic: 41 us -> 27.2 us
    pallas_call x0 -> x1, Pallas kernels: none -> 221 us  [front_call(): pl.pallas_call(front_body, out_shape=(arr((8, rows_each, 1664), BF), arr(...]
    all_gather x6 -> x0, waiting for transfers between devices: 69.9 us -> none  [the longest x1 54.8 us: per_device(): lax.all_gather(jnp.stack([w_query, w_key, w_value, w_out], 1), 'wide', ax...]
    all_to_all x7 -> x4, waiting for transfers between devices: 182 us -> 115 us  [quad_swap(): lax.all_to_all(array, 'wide', 0, 0, axis_index_groups=quads, tiled=True)]
    reshape x11 -> x3, local copies, waits for them, and re-layouts: 65.3 us -> 9.3 us  [share_rows(): parts = grad.astype(BF).reshape(blocks, 4, 2, rows_each, hidden_width)]
    all_gather x2 -> x0, blocking collectives: 48.9 us -> none  [the longest x1 35.3 us: per_device(): router_w = lax.all_gather(w_router, 'wide', axis=0, tiled=True)]
    reduce_scatter x1, waiting for transfers between devices: 44.4 us -> 4.79 us  [per_device(): lax.psum_scatter(grad_attn_w, 'wide', scatter_dimension=0, tiled=True)]
    all_to_all x1 -> x0, blocking collectives: 36.6 us -> none  [quad_swap(): lax.all_to_all(array, 'wide', 0, 0, axis_index_groups=quads, tiled=True)]
    dot_general x54 -> x38, matrix products: 114 us -> 84.3 us  [mm(): lax.dot_general(left, right, (dims, ((), ())), preferred_element_type=F32)]
  transfers between devices with their start and end apart: 23 -> 13, of which waited for: 12 -> 7; matrix products, arithmetic and copies ran while one was open for 19% -> 15% of each run, Pallas kernels for 0% -> 0%
where the time goes in v2:
time: 736 us; the launch traced here: 727 us
  waiting for transfers between devices  251 us (34%)
  Pallas kernels  221 us (30%)
  local copies, waits for them, and re-layouts  95.3 us (13%)
  matrix products  85.9 us (12%)
  other arithmetic  27.2 us (4%)
  starting transfers between devices  17.2 us (2%)
  between operations  16.6 us (2%)
  blocking collectives  12.1 us (2%)
    pallas_call x1, Pallas kernels, front_call(): pl.pallas_call(front_body, out_shape=(arr((8, rows_each, 1664), BF), arr(...  221 us
    all_to_all x4, waiting for transfers between devices, quad_swap(): lax.all_to_all(array, 'wide', 0, 0, axis_index_groups=quads, tiled=True)  115 us
    unnamed x12, waiting for transfers between devices  104 us
    dot_general x38, matrix products, mm(): lax.dot_general(left, right, (dims, ((), ())), preferred_element_type=F32)  84.3 us
    unnamed x98, local copies, waits for them, and re-layouts  63.1 us
    all_gather x1, waiting for transfers between devices, per_device(): lax.all_gather(middle.astype(BF), 'narrow', axis=1, tiled=True).astype(F32)  27.5 us
    all_to_all x4, starting transfers between devices, quad_swap(): lax.all_to_all(array, 'wide', 0, 0, axis_index_groups=quads, tiled=True)  16.9 us
  transfers between devices with their start and end apart: 13, of which 7 were waited for; matrix products, arithmetic and copies ran while one was open for 15% of the time, Pallas kernels for 0%

profile of v2, /device:TPU:0, one launch (start us, length us, event | category | flops | bytes accessed | tf_op | source)
XLA Modules:
  0.0 727.0 jit_solution(14881590254994312035)
XLA Ops:
  14.1 2.3 copy.261
  18.3 4.1 pad_maximum_fusion.moved_ref
  22.4 221.3 %front.1 = (bf16[8,256,1664]{2,1,0:T(8,128)(2,1)}, bf16[8,256,512]{2,1,0:T(8,128)(2,1)}, bf16[3,4,2,256,1408]{4,3,2,1,0:T(8,128)(2,1)}, bf16[576,2048]{1,0:T(8,1...) custom-call(bf16[256,512]{1,0:T(8,128)(2,1)} %tok_ref.1, ...), custom_call_target="tpu_custom_call" | custom-call | flops 6000000000 | bytes 60000000 | tf_op jit(solution)/shard_map/front/pallas_call | solution.py:519
  244.9 2.2 fusion
  247.9 7.2 fusion.98
  255.2 3.9 fusion.95
  259.1 5.6 fusion.93
  264.6 8.2 %multiply_reduce_fusion.1 = (f32[576]{0:T(1024)S(1)}, bf16[576,1408]{1,0:T(8,128)(2,1)}, bf16[576,1408]{1,0:T(8,128)(2,1)S(1)}, bf16[576,1408]{1,0:T(8,128)(2,1)}) fusion(f32[576,1408]{1,0:T(8,128)} %fusion.93, f32[576,1408]{1,0:T(8,128)S(1)} %fusion.95, f32[576]{0:T(1024)S(1)} %slice_reduce_fusion, bf16[576,2048]{1,0:T(8,128)(2,1)S(1)} %copy-done.29, ...), kind=kOutput, calls=%fused_computation.18 | convolution fusion | flops 3337297408 | bytes 19485184 | tf_op jit(solution)/shard_map/dot_general | solution.py:21
  272.9 3.8 fusion.106
  276.8 6.0 multiply_reduce_fusion
  282.8 6.9 convolution_convert_fusion.3
  290.0 2.1 slice_dynamic-update-slice_fusion.7
  300.9 8.4 %copy.242 = bf16[576,4608]{0,1:T(8,128)(2,1)} copy(bf16[576,4608]{1,0:T(8,128)(2,1)} %pad_dynamic-update-slice_fusion.3) | data formatting | bytes 10616832
  309.3 103.6 %reduce-scatter.22.cloned.1.call-done = bf16[1152,576]{1,0:T(8,128)(2,1)} async-done(((bf16[4608,576]{1,0:T(8,128)(2,1)}), bf16[1152,576]{1,0:T(8,128)(2,1)}) %reduce-scatter.22.cloned.1.call-update) | async-done | bytes 1327120
  413.0 2.6 copy.243
  415.5 3.7 all-to-all-start
  419.9 16.1 %all-to-all-done = bf16[4,144,1152]{2,1,0:T(8,128)(2,1)S(1)} async-done(((bf16[4,144,1152]{2,1,0:T(8,128)(2,1)}), bf16[4,144,1152]{2,1,0:T(8,128)(2,1)S(1)}, u32[]{:S(2)}, u32[]{:S(2)}) %all-to-all-start) | async-done | bytes 1327136 | tf_op jit(solution)/shard_map/all_to_all | solution.py:589
  436.8 2.1 fusion.105
  440.3 2.3 fusion.102
  442.9 27.5 %all-gather.3.cloned.1.call-done = bf16[256,2048]{1,0:T(8,128)(2,1)} async-done(((bf16[256,512]{1,0:T(8,128)(2,1)}), bf16[256,2048]{1,0:T(8,128)(2,1)}) %all-gather.3.cloned.1.call-update) | async-done | bytes 1048592 | tf_op jit(solution)/shard_map/all_gather | solution.py:660
  470.4 3.5 convert_multiply_fusion.4
  474.2 2.2 fusion.97
  476.5 7.2 convolution_convert_fusion
  483.7 3.0 copy.258
  488.4 6.9 convolution_convert_fusion.1
  495.2 3.3 copy.259
  498.6 7.2 convolution_convert_fusion.2
  505.8 3.0 copy.260
  512.6 3.6 convolution_convert_fusion.8
  525.2 2.3 fusion.8
  528.9 2.4 convolution_add_fusion.2
  531.4 4.6 multiply_reduce_fusion.2
  544.9 2.5 copy.244
  550.5 4.1 pad_maximum_fusion.1
  554.7 3.7 all-to-all-start.3
  558.4 37.5 %all-to-all-done.3 = bf16[4,256,1408]{2,1,0:T(8,128)(2,1)S(1)} async-done(((bf16[4,256,1408]{2,1,0:T(8,128)(2,1)}), bf16[4,256,1408]{2,1,0:T(8,128)(2,1)S(1)}, u32[]{:S(2)}, u32[]{:S(2)}) %all-to-all-start.3) | async-done | bytes 2883616 | tf_op jit(solution)/shard_map/all_to_all | solution.py:589
  596.0 4.6 all-to-all-start.2
  600.6 32.8 %all-to-all-done.2 = bf16[4,256,1408]{2,1,0:T(8,128)(2,1)} async-done(((bf16[4,256,1408]{2,1,0:T(8,128)(2,1)}), bf16[4,256,1408]{2,1,0:T(8,128)(2,1)}, u32[]{:S(2)}, u32[]{:S(2)}) %all-to-all-start.2) | async-done | bytes 2883616 | tf_op jit(solution)/shard_map/all_to_all | solution.py:589
  633.4 4.9 all-to-all-start.1
  640.4 6.7 copy.229
  647.1 2.3 convert_bitcast_fusion.1
  649.4 6.2 copy.228
  655.7 28.8 %all-to-all-done.1 = bf16[4,256,1408]{2,1,0:T(8,128)(2,1)} async-done(((bf16[4,256,1408]{2,1,0:T(8,128)(2,1)}), bf16[4,256,1408]{2,1,0:T(8,128)(2,1)}, u32[]{:S(2)}, u32[]{:S(2)}) %all-to-all-start.1) | async-done | bytes 2883616 | tf_op jit(solution)/shard_map/all_to_all | solution.py:589
  684.5 2.2 convert_bitcast_fusion.2
  686.7 6.5 copy.227
  694.6 2.0 multiply_reduce_fusion.5
  696.6 12.1 %psum.7 = f32[2,512]{1,0:T(2,128)S(1)} all-reduce(f32[2,512]{1,0:T(2,128)S(1)} %pad_maximum_fusion.8), channel_id=1, replica_groups=mesh['wide'=8,'narrow'=4] {'wide'}, use_global_device_ids=true, to_apply=%region_23.24 | all-reduce | flops 1024 | bytes 8192 | tf_op jit(solution)/shard_map/psum | solution.py:848
  709.3 4.8 reduce-scatter.14.cloned.1.call-done
  (200 shorter events, 59.4 us)
Async XLA Ops:
  8.0 404.9 %reduce-scatter.22.cloned.1.call-start = ((), (), s32[]{:S(2)}) async-start(), calls=%async_computation.17 | async-start | bytes 7372800
  13.2 3.1 copy-start.25
  14.0 3.6 copy-start.4
  14.1 3.6 copy-start.5
  247.9 7.3 copy-start.6
  259.0 5.6 copy-start.29
  272.9 3.9 copy-start.30
  290.0 3.6 copy-start.8
  309.3 109.9 %copy-start.24 = (f32[8,256]{1,0:T(8,128)S(1)}, f32[8,256]{1,0:T(8,128)}, u32[]{:S(2)}) copy-start(f32[8,256]{1,0:T(8,128)} %get-tuple-element.28) | copy-start | bytes 24580
  309.3 110.1 %copy-start.28 = (s32[1,256]{1,0:T(1,128)S(1)}, s32[1,256]{1,0:T(1,128)}, u32[]{:S(2)}) copy-start(s32[1,256]{1,0:T(1,128)} %param.30) | copy-start | bytes 3076
  309.3 126.7 %copy-start.15 = (bf16[2,576,256]{2,1,0:T(8,128)(2,1)S(1)}, bf16[2,576,256]{2,1,0:T(8,128)(2,1)}, u32[]{:S(2)}) copy-start(bf16[2,576,256]{2,1,0:T(8,128)(2,1)} %get-tuple-element.29) | copy-start | bytes 1769476
  415.5 20.5 %all-to-all-start = ((bf16[4,144,1152]{2,1,0:T(8,128)(2,1)}), bf16[4,144,1152]{2,1,0:T(8,128)(2,1)S(1)}, u32[]{:S(2)}, u32[]{:S(2)}) async-start(bf16[4,144,1152]{2,1,0:T(8,128)(2,1)} %bitcast.31), calls=%async_computation | async-start | bytes 2654208 | tf_op jit(solution)/shard_map/all_to_all | solution.py:589
  419.2 51.2 %all-gather.3.cloned.1.call-start = ((), (), s32[]{:S(2)}) async-start(), calls=%async_computation.11 | async-start | bytes 1310720 | tf_op jit(solution)/shard_map/all_gather | solution.py:660
  438.9 3.9 copy-start.26
  442.7 69.9 %all-gather.5.cloned.1.call-start = ((), (), s32[]{:S(2)}) async-start(), calls=%async_computation.12 | async-start | bytes 1310720 | tf_op jit(solution)/shard_map/all_gather | solution.py:795
  470.4 3.6 copy-start.3
  476.4 78.2 %reduce-scatter.20.cloned.1.call-start = ((), (), s32[]{:S(2)}) async-start(), calls=%async_computation.16 | async-start | bytes 8650752 | tf_op jit(solution)/shard_map/reduce_scatter | solution.py:600
  486.7 1.7 copy-start.7
  486.7 71.7 %reduce-scatter.18.cloned.1.call-start = ((), (), s32[]{:S(2)}) async-start(), calls=%async_computation.15 | async-start | bytes 8650752 | tf_op jit(solution)/shard_map/reduce_scatter | solution.py:600
  498.6 102.0 %reduce-scatter.16.cloned.1.call-start = ((), (), s32[]{:S(2)}) async-start(), calls=%async_computation.14 | async-start | bytes 8650752 | tf_op jit(solution)/shard_map/reduce_scatter | solution.py:600
  508.8 1.9 copy-start.16
  508.8 2.0 copy-start.2
  508.9 129.5 %reduce-scatter.26.cloned.1.call-start = ((), (), s32[]{:S(2)}) async-start(), calls=%async_computation.19 | async-start | bytes 1179648
  510.4 5.8 copy-start.12
  512.5 3.8 copy-start.1
  512.5 7.1 copy-start.14
  512.5 180.7 %reduce-scatter.24.cloned.1.call-start = ((), (), s32[]{:S(2)}) async-start(), calls=%async_computation.18 | async-start | bytes 1638400
  528.9 2.5 copy-start.13
  528.9 2.5 copy-start.18
  528.9 2.5 copy-start.19
  528.9 2.5 copy-start.20
  528.9 2.5 copy-start.22
  536.0 1.1 copy-start.11
  537.8 9.7 %copy-start = (bf16[256,2048]{1,0:T(8,128)(2,1)S(1)}, bf16[256,2048]{1,0:T(8,128)(2,1)}, u32[]{:S(2)}) copy-start(bf16[256,2048]{1,0:T(8,128)(2,1)} %get-tuple-element.40) | copy-start | bytes 3145732
  537.8 9.7 %copy-start.21 = (bf16[256,128]{0,1:T(8,128)(2,1)S(1)}, bf16[256,128]{0,1:T(8,128)(2,1)}, u32[]{:S(2)}) copy-start(bf16[256,128]{0,1:T(8,128)(2,1)} %convolution_convert_fusion.10) | copy-start | bytes 196612
  537.8 9.7 %copy-start.23 = (bf16[256,128]{0,1:T(8,128)(2,1)S(1)}, bf16[256,128]{0,1:T(8,128)(2,1)}, u32[]{:S(2)}) copy-start(bf16[256,128]{0,1:T(8,128)(2,1)} %convolution_convert_fusion.9) | copy-start | bytes 196612
  547.4 166.7 %reduce-scatter.14.cloned.1.call-start = ((), (), s32[]{:S(2)}) async-start(), calls=%async_computation.13 | async-start | bytes 9437184 | tf_op jit(solution)/shard_map/reduce_scatter | solution.py:844
  548.2 1.5 copy-start.10
  548.2 1.5 copy-start.17
  554.7 41.3 %all-to-all-start.3 = ((bf16[4,256,1408]{2,1,0:T(8,128)(2,1)}), bf16[4,256,1408]{2,1,0:T(8,128)(2,1)S(1)}, u32[]{:S(2)}, u32[]{:S(2)}) async-start(bf16[4,256,1408]{2,1,0:T(8,128)(2,1)} %bitcast.250), calls=%async_computation.7 | async-start | bytes 5767168 | tf_op jit(solution)/shard_map/all_to_all | solution.py:589
  596.0 37.4 %all-to-all-start.2 = ((bf16[4,256,1408]{2,1,0:T(8,128)(2,1)}), bf16[4,256,1408]{2,1,0:T(8,128)(2,1)}, u32[]{:S(2)}, u32[]{:S(2)}) async-start(bf16[4,256,1408]{2,1,0:T(8,128)(2,1)} %bitcast.251), calls=%async_computation.5 | async-start | bytes 5767168 | tf_op jit(solution)/shard_map/all_to_all | solution.py:589
  633.4 4.9 copy-start.27
  633.4 51.1 %all-to-all-start.1 = ((bf16[4,256,1408]{2,1,0:T(8,128)(2,1)}), bf16[4,256,1408]{2,1,0:T(8,128)(2,1)}, u32[]{:S(2)}, u32[]{:S(2)}) async-start(bf16[4,256,1408]{2,1,0:T(8,128)(2,1)} %bitcast.249), calls=%async_computation.3 | async-start | bytes 5767168 | tf_op jit(solution)/shard_map/all_to_all | solution.py:589
  686.7 7.9 %copy-start.9 = (f32[256,512]{1,0:T(8,128)S(1)}, f32[256,512]{1,0:T(8,128)}, u32[]{:S(2)}) copy-start(f32[256,512]{1,0:T(8,128)} %get-tuple-element.110) | copy-start | bytes 1572868
Sparse Core Ops, SparseCore 0:
  309.4 103.5 reduce-scatter.21
  442.8 27.5 all-gather.2
  476.6 27.4 all-gather.4
Sparse Core Ops, SparseCore 1:
  486.8 13.2 reduce-scatter.19
  502.9 15.0 reduce-scatter.17
  520.7 15.0 reduce-scatter.15
  539.3 53.7 reduce-scatter.25
  595.5 33.9 reduce-scatter.23
  633.3 80.8 reduce-scatter.13

commit v3 on v2

--- a/solution.py
+++ b/solution.py
@@ -563,7 +563,579 @@
     )(tokens, cotangent, gains, *weights, router, moved, rows, cols, freqs)
 
 
-def per_device(
+MID_SLOTS = 48
+
+
+def column_tiles(width):
+    tiles, start = [], 0
+    while start < width:
+        size = min(256, width - start)
+        tiles.append((start, size))
+        start += size
+    return tiles
+
+
+def mid_body(
+    x_ref, dy_ref, gate_ref, tokens_ref, w_ref,
+    back_mid_out, back_exp_out, extra_out, grads_out,
+    weights, hidden, graded, hidden_cat, graded_cat, act_cat, gate_cat, up_cat,
+    rs_send, rs_recv, ext_send, ext_recv, sent, landed, local,
+):
+    n = lax.axis_index("narrow")
+    w = lax.axis_index("wide")
+    chip, core = w // 2, lax.rem(w, 2)
+    to_z, from_z = places_of(n)
+    links = Links(sent, landed, local)
+    mate = {"wide": 2 * chip + 1 - core}
+    slots, full = x_ref.shape
+    part_width = full // 4
+    rows_each = full // 8
+    hidden_width = weights.shape[2]
+    tiles = column_tiles(hidden_width)
+
+    loads = [
+        [
+            links.move(w_ref.at[kind, c, k], weights.at[kind, pl.ds((2 * c + k) * rows_each, rows_each), :])
+            for c in range(4)
+            for k in range(2)
+        ]
+        for kind in range(3)
+    ]
+    links.waits = []
+    greet(to_z, [], chip, core, True)
+
+    total = jnp.zeros((slots, 1), F32)
+    for m in range(4):
+        part = x_ref[:, m * part_width : (m + 1) * part_width].astype(F32)
+        total = total + jnp.sum(part * part, 1, keepdims=True)
+    scale = lax.rsqrt(total * (1.0 / full) + NORM_EPS)
+    slot_gate = gate_ref[:, 0:1]
+    for m in range(4):
+        cols = slice(m * part_width, (m + 1) * part_width)
+        gain = tokens_ref[m, 257:258, :].astype(F32)
+        hidden[:, cols] = (x_ref[:, cols].astype(F32) * scale * gain).astype(BF)
+        graded[:, cols] = (dy_ref[:, cols].astype(F32) * slot_gate).astype(BF)
+
+    def to_mate(source, target):
+        slot = links.slot()
+        links.send(source, target.at[core], mate, slot)
+        return lambda: links.land(target.at[1 - core], mate, slot)
+
+    def parity_exchange(source, target):
+        lands = []
+        for c in range(4):
+            cols = pl.ds(c * rows_each, rows_each)
+            theirs = pl.ds(pl.multiple_of((2 * c + 1 - core) * rows_each, rows_each), rows_each)
+            ours = pl.ds(pl.multiple_of((2 * c + core) * rows_each, rows_each), rows_each)
+            slot = links.slot()
+            links.send(source.at[:, theirs], target.at[core, :, cols], mate, slot)
+            target[core, :, c * rows_each : (c + 1) * rows_each] = source[:, ours]
+            lands.append((target.at[1 - core, :, cols], slot))
+        return lambda: [links.land(block, mate, slot) for block, slot in lands]
+
+    hidden_there = parity_exchange(hidden, hidden_cat)
+    graded_there = parity_exchange(graded, graded_cat)
+
+    for kind in range(3):
+        for load in loads[kind]:
+            load.wait()
+    share = jnp.zeros((slots, 1), F32)
+    for start, size in tiles:
+        cols = slice(start, start + size)
+        gate_pre = low_dot(hidden[...], weights[0, :, cols])
+        up_pre = low_dot(hidden[...], weights[1, :, cols])
+        act_raw = low_dot(dy_ref[...], weights[2, :, cols])
+        sigmoid = 1.0 / (1.0 + jnp.exp(-gate_pre))
+        silu = gate_pre * sigmoid
+        activated = (silu * up_pre).astype(BF)
+        share = share + jnp.sum(act_raw * activated.astype(F32), 1, keepdims=True)
+        grad_act = act_raw * slot_gate
+        act_cat[core, :, cols] = activated
+        gate_cat[core, :, cols] = (
+            grad_act * up_pre * (sigmoid * (1.0 + gate_pre * (1.0 - sigmoid)))
+        ).astype(BF)
+        up_cat[core, :, cols] = (grad_act * silu).astype(BF)
+
+    grad_gate, grad_up = gate_cat[core], up_cat[core]
+    stat = jnp.zeros((slots, 1), F32)
+    mid_slots = [links.slot() for _ in range(NEAR)]
+    for step in range(NEAR + 1):
+        owner = to_z[step] if step < NEAR else n
+        rows = pl.ds(pl.multiple_of(owner * part_width, part_width), part_width)
+        block = rows_rows(grad_gate, weights[0, rows, :]) + rows_rows(grad_up, weights[1, rows, :])
+        cols = pl.ds(pl.multiple_of(owner * part_width, part_width), part_width)
+        stat = stat + jnp.sum(hidden[:, cols].astype(F32) * block, 1, keepdims=True)
+        if step < NEAR:
+            rs_send[0, step] = block.astype(BF)
+            links.send(
+                rs_send.at[0, step], rs_recv.at[0, step], {"narrow": owner}, mid_slots[step]
+            )
+        else:
+            own_mid = block
+    lane_at = lax.broadcasted_iota(jnp.int32, (slots, 128), 1)
+    columns = jnp.where(lane_at == 0, share, jnp.where(lane_at == 1, stat, 0.0))
+    high = columns.astype(BF)
+    rest = (columns - high.astype(F32)).astype(BF)
+    pick = jnp.where(
+        lax.broadcasted_iota(jnp.int32, (8, 128), 0) == lax.broadcasted_iota(jnp.int32, (8, 128), 1),
+        1.0, 0.0,
+    ).astype(BF)
+    extra = rows_rows(pick, high) + rows_rows(pick, rest)
+    ext_send[...] = extra
+    ext_slots = [links.slot() for _ in range(NEAR)]
+    for step in range(NEAR):
+        links.send(ext_send, ext_recv.at[step], {"narrow": to_z[step]}, ext_slots[step])
+    acts_there = [to_mate(item.at[core], item) for item in (act_cat, gate_cat, up_cat)]
+
+    activated = act_cat[core]
+    exp_slots = [links.slot() for _ in range(NEAR)]
+    for step in range(NEAR + 1):
+        owner = to_z[step] if step < NEAR else n
+        rows = pl.ds(pl.multiple_of(owner * part_width, part_width), part_width)
+        block = rows_rows(activated, weights[2, rows, :])
+        if step < NEAR:
+            rs_send[1, step] = block.astype(BF)
+            links.send(
+                rs_send.at[1, step], rs_recv.at[1, step], {"narrow": owner}, exp_slots[step]
+            )
+        else:
+            own_exp = block
+
+    hidden_there()
+    graded_there()
+    for there in acts_there:
+        there()
+    pairs = ((hidden_cat, gate_cat), (hidden_cat, up_cat), (graded_cat, act_cat))
+    for kind, (left, right) in enumerate(pairs):
+        left_rows = left[...].reshape(2 * slots, full // 2)
+        for start, size in tiles:
+            cols = slice(start, start + size)
+            right_rows = right[:, :, cols].reshape(2 * slots, size)
+            weights[kind, 0 : full // 2, cols] = cols_cols(left_rows, right_rows).astype(BF)
+        links.move(weights.at[kind, pl.ds(0, full // 2), :], grads_out.at[kind])
+
+    for step in range(NEAR):
+        links.land(ext_recv.at[step], {"narrow": from_z[step]}, ext_slots[step])
+        extra = extra + ext_recv[step]
+    high = extra.astype(BF)
+    rest = (extra - high.astype(F32)).astype(BF)
+    place = lax.broadcasted_iota(jnp.int32, (8, 128), 0) * 2
+    lanes = lax.broadcasted_iota(jnp.int32, (8, 128), 1)
+    spread_high = jnp.where(place == lanes, 1.0, 0.0).astype(BF)
+    spread_low = jnp.where(place + 1 == lanes, 1.0, 0.0).astype(BF)
+    columns = mm(high, spread_high, ((0,), (0,))) + mm(rest, spread_low, ((0,), (0,)))
+    extra_out[...] = jnp.where(lane_at == 4, 1.0, columns).astype(BF)
+    for which, target in ((0, back_mid_out), (1, back_exp_out)):
+        block = own_mid if which == 0 else own_exp
+        for step in range(NEAR):
+            links.land(
+                rs_recv.at[which, step], {"narrow": from_z[step]},
+                (mid_slots, exp_slots)[which][step],
+            )
+            block = block + rs_recv[which, step].astype(F32)
+        target[...] = block.astype(BF)
+    links.finish()
+
+
+def mid_call(slot_mid, slot_grad, slot_gate, token_parts, expert_w):
+    slots, full = slot_mid.shape
+    part_width = full // 4
+    rows_each, hidden_width = expert_w.shape[3:]
+    vmem = pl.BlockSpec(memory_space=pltpu.VMEM)
+    hbm = pl.BlockSpec(memory_space=pl.ANY)
+
+    def arr(shape, dtype):
+        return jax.ShapeDtypeStruct(shape, dtype)
+
+    return pl.pallas_call(
+        mid_body,
+        out_shape=(
+            arr((slots, part_width), BF),
+            arr((slots, part_width), BF),
+            arr((slots, 128), BF),
+            arr((3, full // 2, hidden_width), BF),
+        ),
+        in_specs=[vmem] * 4 + [hbm],
+        out_specs=(vmem, vmem, vmem, hbm),
+        scratch_shapes=[
+            pltpu.VMEM((3, full, hidden_width), BF),
+            pltpu.VMEM((slots, full), BF),
+            pltpu.VMEM((slots, full), BF),
+            pltpu.VMEM((2, slots, full // 2), BF),
+            pltpu.VMEM((2, slots, full // 2), BF),
+            pltpu.VMEM((2, slots, hidden_width), BF),
+            pltpu.VMEM((2, slots, hidden_width), BF),
+            pltpu.VMEM((2, slots, hidden_width), BF),
+            pltpu.VMEM((2, NEAR, slots, part_width), BF),
+            pltpu.VMEM((2, NEAR, slots, part_width), BF),
+            pltpu.VMEM((8, slots), F32),
+            pltpu.VMEM((NEAR, 8, slots), F32),
+            pltpu.SemaphoreType.DMA((MID_SLOTS,)),
+            pltpu.SemaphoreType.DMA((MID_SLOTS,)),
+            pltpu.SemaphoreType.DMA((32,)),
+        ],
+        compiler_params=pltpu.CompilerParams(
+            collective_id=1, has_side_effects=True, vmem_limit_bytes=62 * 1024 * 1024
+        ),
+        cost_estimate=pl.CostEstimate(
+            flops=30_000_000_000, bytes_accessed=40_000_000, transcendentals=800_000
+        ),
+        name="mid",
+    )(slot_mid, slot_grad, slot_gate, token_parts, expert_w)
+
+
+TAIL_SLOTS = 72
+
+
+def tail_body(
+    mid_ref, exp_ref, ext_ref, moved_ref, picks_ref, stat_ref, cols_ref, middle_ref, cot_ref,
+    tok_ref, tokens_ref, qkv_ref, prob_ref, att_ref, rope_ref, hidden_ref, qkvw_ref, outw_ref,
+    output_out, grad_tokens_out, grad_q_out, grad_k_out, grad_v_out, grad_o_out, small_out,
+    router_out, expert_out,
+    qkvw, outw, ret_mid, ret_exp, ret_ext, branch, hidden_cat, branch_cat, att_cat, proj_cat,
+    proj_send, proj_recv, first_send, first_recv, col_send, col_recv, small_mate, small_sum,
+    small_recv, last_mate, last_sum, last_recv, sent, landed, local,
+):
+    n = lax.axis_index("narrow")
+    w = lax.axis_index("wide")
+    chip, core = w // 2, lax.rem(w, 2)
+    to_z, from_z = places_of(n)
+    plane = plane_of(chip)
+    links = Links(sent, landed, local)
+    mate = {"wide": 2 * chip + 1 - core}
+    token_count, part_width = tok_ref.shape
+    full = 4 * part_width
+    rows_each = full // 8
+    heads = part_width // HEAD_DIM
+    half = full // 2
+
+    def at_plane(peer):
+        return {"wide": 2 * peer + core}
+
+    def cap_rows(array, owner):
+        return array.at[pl.ds(pl.multiple_of(owner * CAP, 16), CAP), :]
+
+    loads = [links.move(qkvw_ref, qkvw), links.move(outw_ref, outw)]
+    links.waits = []
+    greet(to_z, plane, chip, core, True)
+
+    back_slots = []
+    for source, target in ((mid_ref, ret_mid), (ext_ref, ret_ext), (exp_ref, ret_exp)):
+        slots = [links.slot() for _ in range(NEAR)]
+        for step in range(NEAR):
+            links.send(
+                cap_rows(source, plane[step]), cap_rows(target, chip), at_plane(plane[step]),
+                slots[step],
+            )
+        own = links.move(cap_rows(source, chip), cap_rows(target, chip))
+        links.waits.pop()
+        back_slots.append((target, slots, own))
+
+    def returned(which):
+        target, slots, own = back_slots[which]
+        for step in range(NEAR):
+            links.land(cap_rows(target, plane[step]), at_plane(plane[step]), slots[step])
+        own.wait()
+        return target[...]
+
+    expert_slots = {}
+    for kind in (2, 0, 1):
+        expert_slots[kind] = [links.slot() for _ in range(NEAR)]
+        for step in range(NEAR):
+            block = pl.ds(pl.multiple_of(plane[step] * rows_each, rows_each), rows_each)
+            links.send(
+                moved_ref.at[kind, block, :], expert_out.at[kind, chip], at_plane(plane[step]),
+                expert_slots[kind][step],
+            )
+        block = pl.ds(pl.multiple_of(chip * rows_each, rows_each), rows_each)
+        links.move(moved_ref.at[kind, block, :], expert_out.at[kind, chip])
+
+    def to_mate(source, target):
+        slot = links.slot()
+        links.send(source, target.at[core], mate, slot)
+        return lambda: links.land(target.at[1 - core], mate, slot)
+
+    def parity_exchange(source, target):
+        lands = []
+        for c in range(4):
+            cols = pl.ds(c * rows_each, rows_each)
+            theirs = pl.ds(pl.multiple_of((2 * c + 1 - core) * rows_each, rows_each), rows_each)
+            ours = pl.ds(pl.multiple_of((2 * c + core) * rows_each, rows_each), rows_each)
+            slot = links.slot()
+            links.send(source.at[:, theirs], target.at[core, :, cols], mate, slot)
+            target[core, :, c * rows_each : (c + 1) * rows_each] = source[:, ours]
+            lands.append((target.at[1 - core, :, cols], slot))
+        return lambda: [links.land(block, mate, slot) for block, slot in lands]
+
+    hidden_there = parity_exchange(hidden_ref, hidden_cat)
+    att_cat[core] = att_ref[...]
+    att_there = to_mate(att_ref, att_cat)
+
+    stat = jnp.concatenate([stat_ref[...], jnp.zeros((120, token_count), F32)], 0).T
+    lane_at = lax.broadcasted_iota(jnp.int32, (token_count, 128), 1)
+    scale_second = lax.rsqrt(stat[:, 4:5] * (1.0 / full) + NORM_EPS)
+    logits = stat * scale_second
+    hot_first = lane_at == cols_ref[:, 3:4]
+    hot_second = lane_at == cols_ref[:, 4:5]
+    logit_first = jnp.sum(jnp.where(hot_first, logits, 0.0), 1, keepdims=True)
+    logit_second = jnp.sum(jnp.where(hot_second, logits, 0.0), 1, keepdims=True)
+    apart = logit_first - logit_second
+    share_first = 1.0 / (1.0 + jnp.exp(-apart))
+    share_second = 1.0 / (1.0 + jnp.exp(apart))
+    normed = middle_ref[...] * scale_second
+    gain_second = tokens_ref[n, token_count + 1 : token_count + 2, :].astype(F32)
+    hidden_second = (normed * gain_second).astype(BF)
+    for load in loads:
+        load.wait()
+    router = qkvw[pl.ds(2 * n, 2), :, 1536:1664].reshape(part_width, 128)
+
+    rows_mid = returned(0)
+    rows_ext = returned(1)
+    ext_first = cols_cols(picks_ref[0], rows_ext)
+    ext_second = cols_cols(picks_ref[1], rows_ext)
+    ext_both = ext_first + ext_second
+    grad_share = ext_first[:, 0:1] + ext_first[:, 1:2] - ext_second[:, 0:1] - ext_second[:, 1:2]
+    delta = (grad_share * share_first * share_second).astype(BF).astype(F32)
+    grad_logits = jnp.where(hot_first, delta, jnp.where(hot_second, -delta, 0.0)).astype(BF)
+    stat_total = ext_both[:, 2:3] + ext_both[:, 3:4] + delta * apart
+    grad_hidden = cols_cols(picks_ref[0] + picks_ref[1], rows_mid) + rows_rows(grad_logits, router)
+    grad_middle = cot_ref[...].astype(F32) + scale_second * (
+        gain_second * grad_hidden - normed * (stat_total * (1.0 / full))
+    )
+    own_cols = pl.ds(pl.multiple_of(n * part_width, part_width), part_width)
+    branch[:, own_cols] = grad_middle.astype(BF)
+    branch_slots = [links.slot() for _ in range(NEAR)]
+    for step in range(NEAR):
+        links.send(
+            branch.at[:, own_cols], branch.at[:, own_cols], {"narrow": to_z[step]},
+            branch_slots[step],
+        )
+
+    router_part = cols_cols(grad_logits, hidden_second)[0:8, :]
+    gain_part = jnp.sum(grad_hidden * normed, 0, keepdims=True)
+    kind_at = lax.broadcasted_iota(jnp.int32, (8, part_width), 0)
+    small = jnp.where(kind_at == 4, gain_part, router_part)
+    small_mate[core] = small
+    small_there = to_mate(small_mate.at[core], small_mate)
+
+    rows_exp = returned(2)
+    output_out[...] = (
+        middle_ref[...]
+        + share_first * cols_cols(picks_ref[0], rows_exp)
+        + share_second * cols_cols(picks_ref[1], rows_exp)
+    ).astype(BF)
+
+    small_there()
+    small = small_mate[0] + small_mate[1]
+    small_sum[...] = small
+    small_slots = [links.slot() for _ in range(NEAR)]
+    for step in range(NEAR):
+        links.send(small_sum, small_recv.at[step], at_plane(plane[step]), small_slots[step])
+
+    for step in range(NEAR):
+        cols = pl.ds(pl.multiple_of(from_z[step] * part_width, part_width), part_width)
+        links.land(branch.at[:, cols], {"narrow": from_z[step]}, branch_slots[step])
+    branch_there = parity_exchange(branch, branch_cat)
+    grad_att = low_dot(branch[...], outw[...].reshape(full, part_width)).astype(BF)
+    cosines, sines = rope_ref[0], rope_ref[1]
+    score_scale = HEAD_DIM ** (-0.5)
+    stat_first = jnp.zeros((token_count, 1), F32)
+    for head in range(heads):
+        cols = slice(head * HEAD_DIM, (head + 1) * HEAD_DIM)
+        query, key, value = (qkv_ref[i, :, cols] for i in range(3))
+        grad_out = grad_att[:, cols]
+        weights = prob_ref[head]
+        grad_weights = rows_rows(grad_out, value)
+        inner = jnp.sum(weights * grad_weights, 1, keepdims=True)
+        grad_scores = (weights * (grad_weights - inner)).astype(BF)
+        grad_query = low_dot(grad_scores, key) * score_scale
+        grad_key = cols_cols(grad_scores, query) * score_scale
+        grad_value = cols_cols(weights.astype(BF), grad_out)
+        products = (
+            grad_query * query.astype(F32)
+            + grad_key * key.astype(F32)
+            + grad_value * value.astype(F32)
+        )
+        stat_first = stat_first + jnp.sum(products, 1, keepdims=True)
+        for part, grad in ((0, grad_query), (1, grad_key)):
+            turned = grad * cosines - pltpu.roll(grad, HEAD_DIM // 2, 1) * sines
+            proj_cat[core, :, part * 512 + head * 128 : part * 512 + (head + 1) * 128] = (
+                turned.astype(BF)
+            )
+        proj_cat[core, :, 1024 + head * 128 : 1024 + (head + 1) * 128] = grad_value.astype(BF)
+    proj_there = to_mate(proj_cat.at[core], proj_cat)
+    high = stat_first.astype(BF)
+    rest = (stat_first - high.astype(F32)).astype(BF)
+    col_send[...] = jnp.where(
+        lane_at == 0, high.astype(F32), jnp.where(lane_at == 1, rest.astype(F32), 0.0)
+    ).astype(BF)
+    col_slots = [links.slot() for _ in range(NEAR)]
+    for step in range(NEAR):
+        links.send(col_send, col_recv.at[step], {"narrow": to_z[step]}, col_slots[step])
+    grads = proj_cat[core]
+
+    def first_block(m):
+        weight = qkvw[pl.ds(2 * m, 2), :, 0:1536].reshape(part_width, 1536)
+        return rows_rows(grads, weight)
+
+    first_slots = [links.slot() for _ in range(NEAR)]
+    for step in range(NEAR):
+        first_send[step] = first_block(to_z[step]).astype(BF)
+        links.send(
+            first_send.at[step], first_recv.at[step], {"narrow": to_z[step]}, first_slots[step]
+        )
+
+    branch_there()
+    att_there()
+    proj_send[:, 1536:2048] = cols_cols(
+        branch_cat[...].reshape(2 * token_count, half), att_cat[...].reshape(2 * token_count, part_width)
+    ).astype(BF)
+    hidden_there()
+    proj_there()
+    hidden_rows = hidden_cat[...].reshape(2 * token_count, half)
+    for part in range(3):
+        cols = slice(part * 512, (part + 1) * 512)
+        proj_send[:, cols] = cols_cols(
+            hidden_rows, proj_cat[:, :, cols].reshape(2 * token_count, part_width)
+        ).astype(BF)
+
+    def proj_rows(owner):
+        return pl.ds(pl.multiple_of(owner * rows_each, rows_each), rows_each)
+
+    proj_slots = [links.slot() for _ in range(NEAR)]
+    for step in range(NEAR):
+        links.send(
+            proj_send.at[proj_rows(plane[step]), :], proj_recv.at[step], at_plane(plane[step]),
+            proj_slots[step],
+        )
+
+    grad_first = first_block(n)
+    stat_first = high.astype(F32) + rest.astype(F32)
+    total = jnp.zeros((token_count, 1), F32)
+    for m in range(4):
+        part = tokens_ref[m, 0:token_count, :].astype(F32)
+        total = total + jnp.sum(part * part, 1, keepdims=True)
+    scale_first = lax.rsqrt(total * (1.0 / full) + NORM_EPS)
+    normed_first = tok_ref[...].astype(F32) * scale_first
+    gain_first = tokens_ref[n, token_count : token_count + 1, :].astype(F32)
+    for step in range(NEAR):
+        links.land(col_recv.at[step], {"narrow": from_z[step]}, col_slots[step])
+        stat_first = stat_first + (
+            col_recv[step, :, 0:1].astype(F32) + col_recv[step, :, 1:2].astype(F32)
+        )
+    for step in range(NEAR):
+        links.land(first_recv.at[step], {"narrow": from_z[step]}, first_slots[step])
+        grad_first = grad_first + first_recv[step].astype(F32)
+    grad_tokens_out[...] = grad_middle + scale_first * (
+        gain_first * grad_first - normed_first * (stat_first * (1.0 / full))
+    )
+    gain_part = jnp.sum(grad_first * normed_first, 0, keepdims=True)
+    last_mate[core] = jnp.broadcast_to(gain_part, (8, part_width))
+    last_there = to_mate(last_mate.at[core], last_mate)
+
+    for step in range(NEAR):
+        links.land(small_recv.at[step], at_plane(plane[step]), small_slots[step])
+        small = small + small_recv[step]
+    last_there()
+    last = last_mate[0] + last_mate[1]
+    last_sum[...] = last
+    last_slots = [links.slot() for _ in range(NEAR)]
+    for step in range(NEAR):
+        links.send(last_sum, last_recv.at[step], at_plane(plane[step]), last_slots[step])
+    router_out[:, own_cols] = small
+    router_slots = [links.slot() for _ in range(NEAR)]
+    for step in range(NEAR):
+        links.send(
+            router_out.at[:, own_cols], router_out.at[:, own_cols], {"narrow": to_z[step]},
+            router_slots[step],
+        )
+    for step in range(NEAR):
+        links.land(last_recv.at[step], at_plane(plane[step]), last_slots[step])
+        last = last + last_recv[step]
+    small_out[...] = jnp.where(kind_at == 5, last, small)
+    for step in range(NEAR):
+        cols = pl.ds(pl.multiple_of(from_z[step] * part_width, part_width), part_width)
+        links.land(router_out.at[:, cols], {"narrow": from_z[step]}, router_slots[step])
+
+    summed = proj_send[proj_rows(chip), :].astype(F32)
+    for step in range(NEAR):
+        links.land(proj_recv.at[step], at_plane(plane[step]), proj_slots[step])
+        summed = summed + proj_recv[step].astype(F32)
+    for part, target in enumerate((grad_q_out, grad_k_out, grad_v_out, grad_o_out)):
+        target[...] = summed[:, part * 512 : (part + 1) * 512]
+    for kind in (2, 0, 1):
+        for step in range(NEAR):
+            links.land(
+                expert_out.at[kind, plane[step]], at_plane(plane[step]), expert_slots[kind][step]
+            )
+    links.finish()
+
+
+def tail_call(*args):
+    slots, part_width = args[0].shape
+    half, hidden_width = args[3].shape[1:]
+    token_count = args[9].shape[0]
+    full, rows_each = 2 * half, half // 4
+    vmem = pl.BlockSpec(memory_space=pltpu.VMEM)
+    hbm = pl.BlockSpec(memory_space=pl.ANY)
+
+    def arr(shape, dtype):
+        return jax.ShapeDtypeStruct(shape, dtype)
+
+    own = (token_count, part_width)
+    return pl.pallas_call(
+        tail_body,
+        out_shape=(
+            arr(own, BF),
+            arr(own, F32),
+            arr((rows_each, part_width), F32),
+            arr((rows_each, part_width), F32),
+            arr((rows_each, part_width), F32),
+            arr((rows_each, part_width), F32),
+            arr((8, part_width), F32),
+            arr((8, full), F32),
+            arr((3, 4, rows_each, hidden_width), BF),
+        ),
+        in_specs=[vmem] * 3 + [hbm] + [vmem] * 12 + [hbm] * 2,
+        out_specs=(vmem,) * 8 + (hbm,),
+        scratch_shapes=[
+            pltpu.VMEM((8, rows_each, 1664), BF),
+            pltpu.VMEM((8, rows_each, part_width), BF),
+            pltpu.VMEM((slots, part_width), BF),
+            pltpu.VMEM((slots, part_width), BF),
+            pltpu.VMEM((slots, 128), BF),
+            pltpu.VMEM((token_count, full), BF),
+            pltpu.VMEM((2, token_count, half), BF),
+            pltpu.VMEM((2, token_count, half), BF),
+            pltpu.VMEM((2, token_count, part_width), BF),
+            pltpu.VMEM((2, token_count, 1536), BF),
+            pltpu.VMEM((half, full), BF),
+            pltpu.VMEM((NEAR, rows_each, full), BF),
+            pltpu.VMEM((NEAR,) + own, BF),
+            pltpu.VMEM((NEAR,) + own, BF),
+            pltpu.VMEM((token_count, 128), BF),
+            pltpu.VMEM((NEAR, token_count, 128), BF),
+            pltpu.VMEM((2, 8, part_width), F32),
+            pltpu.VMEM((8, part_width), F32),
+            pltpu.VMEM((NEAR, 8, part_width), F32),
+            pltpu.VMEM((2, 8, part_width), F32),
+            pltpu.VMEM((8, part_width), F32),
+            pltpu.VMEM((NEAR, 8, part_width), F32),
+            pltpu.SemaphoreType.DMA((TAIL_SLOTS,)),
+            pltpu.SemaphoreType.DMA((TAIL_SLOTS,)),
+            pltpu.SemaphoreType.DMA((16,)),
+        ],
+        compiler_params=pltpu.CompilerParams(
+            collective_id=2, has_side_effects=True, vmem_limit_bytes=60 * 1024 * 1024
+        ),
+        cost_estimate=pl.CostEstimate(
+            flops=6_000_000_000, bytes_accessed=60_000_000, transcendentals=1_000
+        ),
+        name="tail",
+    )(*args)
+
+
+def plain_device(
     tokens, gain_attn, w_query, w_key, w_value, w_out, gain_ffn, w_router,
     w_gate, w_up, w_down, segment, parents, expert_ids, slot_order, cotangent,
 ):
@@ -614,120 +1186,73 @@
     gain_second_loc = gain_ffn.astype(F32)
     hot_first, hot_second, kept, pick_first, pick_second = route(expert_ids, slot_order[0])
 
-    if wide_count == 8 and narrow_count == 4:
-        seg = segment[0]
-        seg_ids = jnp.arange(SEGS, dtype=jnp.int32)
-        above = jnp.sum(jnp.where(seg[:, None] == seg_ids[None, :], parents[0][None, :], 0), 1)
-        table = jnp.stack([seg, above, slot_order[0], expert_ids[:, 0], expert_ids[:, 1]] + [seg] * 3)
-        moved = jnp.stack([jnp.transpose(item, (1, 0, 2)) for item in (w_gate, w_up, w_down)])
-        (
-            in_w, out_w8, expert_w, slot_mid, slot_grad, slot_gate, middle, hidden_first,
-            token_parts, qkv, probs, attended, stat, rope, picks,
-        ) = front_call(
-            tokens, cotangent, gains, (w_query, w_key, w_value, w_out),
-            jnp.pad(w_router, ((0, 0), (0, 124))), moved, table, table.T,
-            jnp.tile(freqs, 2)[None, :],
-        )
-        in_w = in_w.reshape(full_width, 1664)
-        query_w, key_w, value_w = (in_w[:, i * 512 : (i + 1) * 512] for i in range(3))
-        router_w = in_w[:, 1536 : 1536 + EXPERTS]
-        out_w = out_w8.reshape(full_width, part_width)
-        gate_w, up_w, down_w = (expert_w[i].reshape(full_width, hidden_width) for i in range(3))
-        slot_gate = slot_gate[:, 0:1]
-        token_rows = token_parts[:, :token_count]
-        tokens_full = jnp.concatenate([token_rows[i] for i in range(4)], 1)
-        gains_full = jnp.concatenate([token_parts[i, token_count : token_count + 2] for i in range(4)], 1)
-        cosines, sines = rope[0][:, :half_dim], rope[1][:, half_dim:]
-        inputs_full = tokens_full.astype(F32)
-        scale_first = lax.rsqrt(jnp.mean(inputs_full * inputs_full, -1, keepdims=True) + NORM_EPS)
-        normed_first = inputs_full * scale_first
-        gain_first = gains_full[0].astype(F32)
-        gain_second = gains_full[1].astype(F32)
-        saved = [
-            tuple(qkv[i, :, h * HEAD_DIM : (h + 1) * HEAD_DIM] for i in range(3)) + (probs[h],)
-            for h in range(heads)
-        ]
-        scale_second = lax.rsqrt(stat[4] / full_width + NORM_EPS)[:, None]
-        logits = stat[:EXPERTS].T * scale_second
-        slot_mid = slot_mid.astype(F32)
-        slot_scale = lax.rsqrt(jnp.mean(slot_mid * slot_mid, -1, keepdims=True) + NORM_EPS)
-        slot_hidden = (slot_mid * slot_scale * gain_second).astype(BF)
-        pick_first_low, pick_second_low = picks[0].T, picks[1].T
-        pick_both_low = pick_first_low + pick_second_low
-        share_first, share_second = gate_pair(logits, hot_first, hot_second)
-        weight_first = kept[:, 0] * share_first
-        weight_second = kept[:, 1] * share_second
-        middle_full = lax.all_gather(middle.astype(BF), "narrow", axis=1, tiled=True).astype(F32)
-        normed_second = middle_full * scale_second
-        hidden_second = (normed_second * gain_second).astype(BF)
-    else:
-        gate_w, up_w, down_w = own_rows(w_gate), own_rows(w_up), own_rows(w_down)
-        attn_w = lax.all_gather(
-            jnp.stack([w_query, w_key, w_value, w_out], 1), "wide", axis=0, tiled=True
-        )
-        query_w, key_w, value_w, out_w = (attn_w[:, i] for i in range(4))
-        router_w = lax.all_gather(w_router, "wide", axis=0, tiled=True)
-        tokens_full = lax.all_gather(tokens, "narrow", axis=1, tiled=True)
-        grad_full = lax.all_gather(cotangent, "narrow", axis=1, tiled=True)
-        gains_full = lax.all_gather(gains, "narrow", axis=1, tiled=True)
-        gain_first = gains_full[0].astype(F32)
-        gain_second = gains_full[1].astype(F32)
-
-        seen, places = tree_layout(segment[0], parents[0])
-        pick_first_low = pick_first.astype(BF)
-        pick_second_low = pick_second.astype(BF)
-        pick_both_low = (pick_first | pick_second).astype(BF)
-
-        inputs_full = tokens_full.astype(F32)
-        scale_first = lax.rsqrt(jnp.mean(inputs_full * inputs_full, -1, keepdims=True) + NORM_EPS)
-        normed_first = inputs_full * scale_first
-        hidden_first = (normed_first * gain_first).astype(BF)
-        angles = places[:, None] * freqs[None, :]
-        cosines, sines = jnp.cos(angles), jnp.sin(angles)
-        query_raw = rows_cols(hidden_first, query_w)
-        key_raw = rows_cols(hidden_first, key_w)
-        value_low = rows_cols(hidden_first, value_w).astype(BF)
-
-        saved = []
-        outs = []
-        for head in range(heads):
-            query = rotate(head_cols(query_raw, head), cosines, sines).astype(BF)
-            key = rotate(head_cols(key_raw, head), cosines, sines).astype(BF)
-            value = head_cols(value_low, head)
-            scores = jnp.where(seen, rows_rows(query, key) * score_scale, NEG_FILL)
-            exps = jnp.exp(scores - jnp.max(scores, -1, keepdims=True))
-            weights = exps / jnp.sum(exps, -1, keepdims=True)
-            saved.append((query, key, value, weights))
-            outs.append(rows_cols(weights.astype(BF), value).astype(BF))
-        attended = jnp.concatenate(outs, 1)
-        branch_part = rows_rows(attended, out_w).astype(BF)
-        branch_loc = lax.psum_scatter(
-            branch_part, "narrow", scatter_dimension=1, tiled=True
-        ).astype(F32)
-        middle = tokens.astype(F32) + branch_loc
-        middle_full = lax.all_gather(middle.astype(BF), "narrow", axis=1, tiled=True).astype(F32)
-        scale_second = lax.rsqrt(jnp.mean(middle_full * middle_full, -1, keepdims=True) + NORM_EPS)
-        normed_second = middle_full * scale_second
-        hidden_second = (normed_second * gain_second).astype(BF)
-        logits = rows_cols(hidden_second, router_w)
-        share_first, share_second = gate_pair(logits, hot_first, hot_second)
-        weight_first = kept[:, 0] * share_first
-        weight_second = kept[:, 1] * share_second
-
-        slot_weight = jnp.sum(
-            pick_first * weight_first[:, None] + pick_second * weight_second[:, None], 0
-        )
-        weight_high, weight_low = two_parts(slot_weight)
-        pads = jnp.stack([weight_high, weight_low], 1)
-        pads = jnp.pad(pads, ((0, 0), (0, 126)))
-        sent_hidden = cols_cols(pick_both_low, hidden_second).astype(BF)
-        sent_grad = cols_cols(pick_both_low, grad_full).astype(BF)
-        sent = jnp.concatenate([sent_hidden, sent_grad, pads], 1)
-        got = quad_swap(sent.reshape(EXPERTS, CAP, -1)).reshape(SLOTS, -1)
-        slot_hidden = got[:, :full_width]
-        slot_grad = got[:, full_width : 2 * full_width]
-        slot_gate = got[:, 2 * full_width : 2 * full_width + 2].astype(F32)
-        slot_gate = slot_gate[:, 0:1] + slot_gate[:, 1:2]
+    gate_w, up_w, down_w = own_rows(w_gate), own_rows(w_up), own_rows(w_down)
+    attn_w = lax.all_gather(
+        jnp.stack([w_query, w_key, w_value, w_out], 1), "wide", axis=0, tiled=True
+    )
+    query_w, key_w, value_w, out_w = (attn_w[:, i] for i in range(4))
+    router_w = lax.all_gather(w_router, "wide", axis=0, tiled=True)
+    tokens_full = lax.all_gather(tokens, "narrow", axis=1, tiled=True)
+    grad_full = lax.all_gather(cotangent, "narrow", axis=1, tiled=True)
+    gains_full = lax.all_gather(gains, "narrow", axis=1, tiled=True)
+    gain_first = gains_full[0].astype(F32)
+    gain_second = gains_full[1].astype(F32)
+
+    seen, places = tree_layout(segment[0], parents[0])
+    pick_first_low = pick_first.astype(BF)
+    pick_second_low = pick_second.astype(BF)
+    pick_both_low = (pick_first | pick_second).astype(BF)
+
+    inputs_full = tokens_full.astype(F32)
+    scale_first = lax.rsqrt(jnp.mean(inputs_full * inputs_full, -1, keepdims=True) + NORM_EPS)
+    normed_first = inputs_full * scale_first
+    hidden_first = (normed_first * gain_first).astype(BF)
+    angles = places[:, None] * freqs[None, :]
+    cosines, sines = jnp.cos(angles), jnp.sin(angles)
+    query_raw = rows_cols(hidden_first, query_w)
+    key_raw = rows_cols(hidden_first, key_w)
+    value_low = rows_cols(hidden_first, value_w).astype(BF)
+
+    saved = []
+    outs = []
+    for head in range(heads):
+        query = rotate(head_cols(query_raw, head), cosines, sines).astype(BF)
+        key = rotate(head_cols(key_raw, head), cosines, sines).astype(BF)
+        value = head_cols(value_low, head)
+        scores = jnp.where(seen, rows_rows(query, key) * score_scale, NEG_FILL)
+        exps = jnp.exp(scores - jnp.max(scores, -1, keepdims=True))
+        weights = exps / jnp.sum(exps, -1, keepdims=True)
+        saved.append((query, key, value, weights))
+        outs.append(rows_cols(weights.astype(BF), value).astype(BF))
+    attended = jnp.concatenate(outs, 1)
+    branch_part = rows_rows(attended, out_w).astype(BF)
+    branch_loc = lax.psum_scatter(
+        branch_part, "narrow", scatter_dimension=1, tiled=True
+    ).astype(F32)
+    middle = tokens.astype(F32) + branch_loc
+    middle_full = lax.all_gather(middle.astype(BF), "narrow", axis=1, tiled=True).astype(F32)
+    scale_second = lax.rsqrt(jnp.mean(middle_full * middle_full, -1, keepdims=True) + NORM_EPS)
+    normed_second = middle_full * scale_second
+    hidden_second = (normed_second * gain_second).astype(BF)
+    logits = rows_cols(hidden_second, router_w)
+    share_first, share_second = gate_pair(logits, hot_first, hot_second)
+    weight_first = kept[:, 0] * share_first
+    weight_second = kept[:, 1] * share_second
+
+    slot_weight = jnp.sum(
+        pick_first * weight_first[:, None] + pick_second * weight_second[:, None], 0
+    )
+    weight_high, weight_low = two_parts(slot_weight)
+    pads = jnp.stack([weight_high, weight_low], 1)
+    pads = jnp.pad(pads, ((0, 0), (0, 126)))
+    sent_hidden = cols_cols(pick_both_low, hidden_second).astype(BF)
+    sent_grad = cols_cols(pick_both_low, grad_full).astype(BF)
+    sent = jnp.concatenate([sent_hidden, sent_grad, pads], 1)
+    got = quad_swap(sent.reshape(EXPERTS, CAP, -1)).reshape(SLOTS, -1)
+    slot_hidden = got[:, :full_width]
+    slot_grad = got[:, full_width : 2 * full_width]
+    slot_gate = got[:, 2 * full_width : 2 * full_width + 2].astype(F32)
+    slot_gate = slot_gate[:, 0:1] + slot_gate[:, 1:2]
 
     gate_pre = rows_cols(slot_hidden, gate_w)
     up_pre = rows_cols(slot_hidden, up_w)
@@ -862,6 +1387,53 @@
     )
 
 
+def per_device(
+    tokens, gain_attn, w_query, w_key, w_value, w_out, gain_ffn, w_router,
+    w_gate, w_up, w_down, segment, parents, expert_ids, slot_order, cotangent,
+):
+    if lax.axis_size("wide") != 8 or lax.axis_size("narrow") != 4:
+        return plain_device(
+            tokens, gain_attn, w_query, w_key, w_value, w_out, gain_ffn, w_router,
+            w_gate, w_up, w_down, segment, parents, expert_ids, slot_order, cotangent,
+        )
+    rows_each = w_router.shape[0]
+    freqs = ROPE_BASE ** (-2.0 * jnp.arange(HEAD_DIM // 2, dtype=F32) / HEAD_DIM)
+    seg = segment[0]
+    seg_ids = jnp.arange(SEGS, dtype=jnp.int32)
+    above = jnp.sum(jnp.where(seg[:, None] == seg_ids[None, :], parents[0][None, :], 0), 1)
+    table = jnp.stack(
+        [seg, above, slot_order[0], expert_ids[:, 0], expert_ids[:, 1], seg, seg, seg]
+    )
+    moved = jnp.stack([jnp.transpose(item, (1, 0, 2)) for item in (w_gate, w_up, w_down)])
+    (
+        in_w, out_w, expert_w, slot_mid, slot_grad, slot_gate, middle, hidden_first,
+        token_parts, qkv, probs, attended, stat, rope, picks,
+    ) = front_call(
+        tokens, cotangent, jnp.stack([gain_attn, gain_ffn]), (w_query, w_key, w_value, w_out),
+        jnp.pad(w_router, ((0, 0), (0, 128 - EXPERTS))), moved, table, table.T,
+        jnp.tile(freqs, 2)[None, :],
+    )
+    back_mid, back_exp, back_ext, grads = mid_call(
+        slot_mid, slot_grad, slot_gate, token_parts, expert_w
+    )
+    (
+        output, grad_tokens, grad_q, grad_k, grad_v, grad_o, small, router, experts,
+    ) = tail_call(
+        back_mid, back_exp, back_ext, grads, picks, stat, table.T, middle, cotangent, tokens,
+        token_parts, qkv, probs, attended, rope, hidden_first, in_w, out_w,
+    )
+    gate_out, up_out, down_out = (
+        jnp.transpose(experts[kind], (1, 0, 2)).astype(F32) for kind in range(3)
+    )
+    router = lax.dynamic_slice_in_dim(
+        router[:EXPERTS], lax.axis_index("wide") * rows_each, rows_each, 1
+    ).T
+    return (
+        output, grad_tokens, small[5], grad_q, grad_k, grad_v, grad_o, small[4], router,
+        gate_out, up_out, down_out,
+    )
+
+
 def solution(mesh):
     pair = P("wide", "narrow")
     part = P("narrow")

time: 736 us -> 572 us (0.78)
  Pallas kernels: 221 us -> 514 us
  waiting for transfers between devices: 251 us -> 0 us
  matrix products: 85.9 us -> 0 us
  local copies, waits for them, and re-layouts: 95.3 us -> 36.1 us
  starting transfers between devices: 17.2 us -> 0 us
  between operations: 16.6 us -> 1.04 us
  blocking collectives: 12.1 us -> 0 us
  other arithmetic: 27.2 us -> 15.6 us
    pallas_call x0 -> x2, Pallas kernels: none -> 292 us  [the longest x1 175 us: tail_call(): pl.pallas_call(tail_body, out_shape=(arr(own, BF), arr(own, F32), arr((ro...]
    all_to_all x4 -> x0, waiting for transfers between devices: 115 us -> none  [quad_swap(): lax.all_to_all(array, 'wide', 0, 0, axis_index_groups=quads, tiled=True)]
    unnamed x12 -> x0, waiting for transfers between devices: 104 us -> none
    dot_general x38 -> x0, matrix products: 84.3 us -> none  [mm(): lax.dot_general(left, right, (dims, ((), ())), preferred_element_type=F32)]
    unnamed x98 -> x41, local copies, waits for them, and re-layouts: 63.1 us -> 26.9 us
    all_gather x2 -> x0, waiting for transfers between devices: 27.6 us -> none  [the longest x1 27.5 us: per_device(): lax.all_gather(middle.astype(BF), 'narrow', axis=1, tiled=True).astype(F32)]
    all_to_all x4 -> x0, starting transfers between devices: 16.9 us -> none  [quad_swap(): lax.all_to_all(array, 'wide', 0, 0, axis_index_groups=quads, tiled=True)]
    psum x1 -> x0, blocking collectives: 12.1 us -> none  [per_device(): lax.psum(jnp.stack([grad_gain_first, grad_gain_second]), 'wide')]
  transfers between devices with their start and end apart: 13 -> 0, of which waited for: 7 -> 0; matrix products, arithmetic and copies ran while one was open for 15% -> 0% of each run, Pallas kernels for 0% -> 0%
where the time goes in v3:
time: 572 us; the launch traced here: 567 us
  Pallas kernels  514 us (90%)
  local copies, waits for them, and re-layouts  36.1 us (6%)
  other arithmetic  15.6 us (3%)
    pallas_call x1, Pallas kernels, front_call(): pl.pallas_call(front_body, out_shape=(arr((8, rows_each, 1664), BF), arr(...  221 us
    pallas_call x1, Pallas kernels, tail_call(): pl.pallas_call(tail_body, out_shape=(arr(own, BF), arr(own, F32), arr((ro...  175 us
    pallas_call x1, Pallas kernels, mid_call(): pl.pallas_call(mid_body, out_shape=(arr((slots, part_width), BF), arr((sl...  117 us
    unnamed x41, local copies, waits for them, and re-layouts  26.9 us

profile of v3, /device:TPU:0, one launch (start us, length us, event | category | flops | bytes accessed | tf_op | source)
XLA Modules:
  0.0 566.6 jit_solution(4692169000714868705)
XLA Ops:
  0.6 0.8 slice_bitcast_fusion
  1.4 0.8 select_reduce_fusion
  2.2 0.9 stack.35.rows_ref
  3.0 0.8 copy.69
  3.8 3.6 copy_bitcast_fusion
  7.4 0.0 copy-done.8
  7.4 0.0 copy-done.1
  7.4 0.3 copy.76
  7.8 0.0 copy-start.10
  7.8 0.0 copy-start.11
  7.8 0.0 copy-start.12
  7.8 4.1 pad_maximum_fusion.moved_ref
  11.9 0.0 copy-done.10
  11.9 0.1 copy.65
  12.1 0.6 pad.4.router_ref
  12.7 0.0 copy-done.11
  12.7 0.0 copy-done.12
  12.7 0.6 pad_maximum_fusion.1.gains_ref
  13.3 0.6 broadcast_in_dim_tile.3.freq_ref
  13.9 221.4 %front.1 = (bf16[8,256,1664]{2,1,0:T(8,128)(2,1)}, bf16[8,256,512]{2,1,0:T(8,128)(2,1)}, bf16[3,4,2,256,1408]{4,3,2,1,0:T(8,128)(2,1)}, bf16[576,2048]{1,0:T(8,1...) custom-call(bf16[256,512]{1,0:T(8,128)(2,1)} %tok_ref.3, ...), custom_call_target="tpu_custom_call" | custom-call | flops 6000000000 | bytes 60000000 | tf_op jit(solution)/shard_map/front/pallas_call | solution.py:519
  235.4 117.4 %mid.1 = (bf16[576,512]{1,0:T(8,128)(2,1)}, bf16[576,512]{1,0:T(8,128)(2,1)}, bf16[576,128]{1,0:T(8,128)(2,1)}, bf16[3,1024,1408]{2,1,0:T(8,128)(2,1)}) custom-call(bf16[576,2048]{1,0:T(8,128)(2,1)} %get-tuple-element.40.x_ref, bf16[576,2048]{1,0:T(8,128)(2,1)} %get-tuple-element.41.dy_ref, f32[576,128]{1,0:T(8,128)} %get-tuple-element.42.gate_ref, ...), custom_call_target="tpu_custom_call" | custom-call | flops 30000001024 | bytes 40000000 | tf_op jit(solution)/shard_map/mid/pallas_call | solution.py:750
  352.8 175.0 %tail.1 = (bf16[256,512]{1,0:T(8,128)(2,1)}, f32[256,512]{1,0:T(8,128)}, f32[256,512]{1,0:T(8,128)}, f32[256,512]{1,0:T(8,128)}, f32[256,512]{1,0:T(8,128)}, /*i...) custom-call(bf16[576,512]{1,0:T(8,128)(2,1)} %get-tuple-element.45.mid_ref, ...), custom_call_target="tpu_custom_call" | custom-call | flops 6000000000 | bytes 60000000 | tf_op jit(solution)/shard_map/tail/pallas_call | solution.py:1086
  527.8 10.1 %convert_bitcast_fusion = (f32[256,4,1408]{2,0,1:T(8,128)}, f32[256,4,1408]{2,0,1:T(8,128)}, f32[256,4,1408]{2,0,1:T(8,128)}) fusion(bf16[3,4,256,1408]{3,2,1,0:T(8,128)(2,1)} %get-tuple-element.67), kind=kLoop, calls=%fused_computation.1 | loop fusion | flops 4325376 | bytes 25952256 | tf_op jit(solution)/shard_map/convert_element_type | solution.py:1426
  537.9 9.2 %copy.70 = f32[256,4,1408]{2,1,0:T(4,128)} copy(f32[256,4,1408]{2,0,1:T(8,128)} %get-tuple-element.118) | data formatting | bytes 11534336
  547.1 0.0 copy-done
  547.1 6.2 %copy.71 = f32[256,4,1408]{2,1,0:T(4,128)} copy(f32[256,4,1408]{2,0,1:T(8,128)S(1)} %copy-done) | data formatting | bytes 11534336
  553.4 0.0 slice-done
  553.4 0.0 slice-done.1
  553.4 0.0 copy-start.7
  553.4 0.0 copy-start.6
  553.4 0.0 copy-start.5
  553.4 0.0 copy-start.4
  553.4 0.0 copy-start.3
  553.4 0.0 copy-start.2
  553.5 6.2 %copy.72 = f32[256,4,1408]{2,1,0:T(4,128)} copy(f32[256,4,1408]{2,0,1:T(8,128)S(1)} %bitcast.41) | data formatting | bytes 11534336
  559.7 0.0 copy-done.9
  559.7 0.6 dynamic-slice_bitcast_fusion
  560.3 1.4 fusion
  561.7 0.0 copy-done.7
  561.7 0.7 copy.83
  562.4 0.0 copy-done.6
  562.4 0.8 copy.84
  563.2 0.0 copy-done.5
  563.2 0.8 copy.85
  564.0 0.0 copy-done.4
  564.0 0.8 copy.86
  564.8 0.8 copy.87
  565.6 0.8 copy.88
  (14 shorter events, 0.0 us)
Async XLA Ops:
  3.0 4.4 copy-start.8
  3.8 3.6 copy-start.1
  7.8 4.2 copy-start.10
  7.8 4.9 copy-start.11
  7.8 4.9 copy-start.12
  537.9 9.2 %copy-start = (f32[256,4,1408]{2,0,1:T(8,128)S(1)}, f32[256,4,1408]{2,0,1:T(8,128)}, u32[]{:S(2)}) copy-start(f32[256,4,1408]{2,0,1:T(8,128)} %get-tuple-element.117) | copy-start | bytes 17301508
  537.9 15.5 %slice-start = ((s8[5767168]{0:T(1024)(128)(4,1)}), s8[4194304]{0:T(1024)(128)(4,1)S(1)}, s32[]{:S(2)}) async-start(s8[5767168]{0:T(1024)(128)(4,1)} %bitcast.40), calls=%async_computation | async-start | bytes 8388608
  547.1 6.2 %slice-start.1 = ((s8[5767168]{0:T(1024)(128)(4,1)}), s8[1572864]{0:T(1024)(128)(4,1)S(1)}, s32[]{:S(2)}) async-start(s8[5767168]{0:T(1024)(128)(4,1)} %bitcast.40), calls=%async_computation.1 | async-start | bytes 3145728
  553.4 6.3 %copy-start.9 = (f32[8,2048]{1,0:T(8,128)S(1)}, f32[8,2048]{1,0:T(8,128)}, u32[]{:S(2)}) copy-start(f32[8,2048]{1,0:T(8,128)} %get-tuple-element.66) | copy-start | bytes 196612
  553.4 8.3 %copy-start.7 = (bf16[256,512]{1,0:T(8,128)(2,1)S(1)}, bf16[256,512]{1,0:T(8,128)(2,1)}, u32[]{:S(2)}) copy-start(bf16[256,512]{1,0:T(8,128)(2,1)} %get-tuple-element.137) | copy-start | bytes 786436
  553.4 9.0 %copy-start.6 = (f32[256,512]{1,0:T(8,128)S(1)}, f32[256,512]{1,0:T(8,128)}, u32[]{:S(2)}) copy-start(f32[256,512]{1,0:T(8,128)} %get-tuple-element.138) | copy-start | bytes 1572868
  553.4 9.8 %copy-start.5 = (f32[256,512]{1,0:T(8,128)S(1)}, f32[256,512]{1,0:T(8,128)}, u32[]{:S(2)}) copy-start(f32[256,512]{1,0:T(8,128)} %get-tuple-element.140) | copy-start | bytes 1572868
  553.4 10.6 %copy-start.4 = (f32[256,512]{1,0:T(8,128)S(1)}, f32[256,512]{1,0:T(8,128)}, u32[]{:S(2)}) copy-start(f32[256,512]{1,0:T(8,128)} %get-tuple-element.141) | copy-start | bytes 1572868
  553.4 11.3 %copy-start.3 = (f32[256,512]{1,0:T(8,128)S(1)}, f32[256,512]{1,0:T(8,128)}, u32[]{:S(2)}) copy-start(f32[256,512]{1,0:T(8,128)} %get-tuple-element.142) | copy-start | bytes 1572868
  553.4 12.1 %copy-start.2 = (f32[256,512]{1,0:T(8,128)S(1)}, f32[256,512]{1,0:T(8,128)}, u32[]{:S(2)}) copy-start(f32[256,512]{1,0:T(8,128)} %get-tuple-element.143) | copy-start | bytes 1572868

commit v4 on v3

--- a/solution.py
+++ b/solution.py
@@ -252,24 +252,6 @@
     tok_slots = [links.slot() for _ in range(NEAR)]
     for step in range(NEAR):
         links.send(tok_pack, tokens_out.at[n], {"narrow": to_z[step]}, tok_slots[step])
-    pack[:, 0:512] = wq_ref[...]
-    pack[:, 512:1024] = wk_ref[...]
-    pack[:, 1024:1536] = wv_ref[...]
-    pack[:, 1536:1664] = router_ref[...]
-    in_slots = [links.slot() for _ in range(NEAR)]
-    for step in range(NEAR):
-        links.send(pack, qkvw.at[w], at_plane(plane[step]), in_slots[step])
-    in_mate = [links.slot() for _ in range(4)]
-    links.send(pack, qkvw.at[w], mate, in_mate[3])
-    out_slots = [links.slot() for _ in range(NEAR)]
-    for step in range(NEAR):
-        links.send(wo_ref, outw.at[w], at_plane(plane[step]), out_slots[step])
-    out_mate = [links.slot() for _ in range(4)]
-    links.send(wo_ref, outw.at[w], mate, out_mate[3])
-    tokens_out[n] = tok_pack[...]
-    qkvw[w] = pack[...]
-    outw[w] = wo_ref[...]
-
     wide_shape = (token_count, token_count)
     row_at = lax.broadcasted_iota(jnp.int32, wide_shape, 0)
     col_at = lax.broadcasted_iota(jnp.int32, wide_shape, 1)
@@ -337,6 +319,24 @@
 
     dy_state = dispatch(cot_ref[...], cot_send, dy_out)
     dy_chain = Chain(links, n, column_block(dy_out))
+
+    pack[:, 0:512] = wq_ref[...]
+    pack[:, 512:1024] = wk_ref[...]
+    pack[:, 1024:1536] = wv_ref[...]
+    pack[:, 1536:1664] = router_ref[...]
+    in_slots = [links.slot() for _ in range(NEAR)]
+    for step in range(NEAR):
+        links.send(pack, qkvw.at[w], at_plane(plane[step]), in_slots[step])
+    in_mate = [links.slot() for _ in range(4)]
+    links.send(pack, qkvw.at[w], mate, in_mate[3])
+    out_slots = [links.slot() for _ in range(NEAR)]
+    for step in range(NEAR):
+        links.send(wo_ref, outw.at[w], at_plane(plane[step]), out_slots[step])
+    out_mate = [links.slot() for _ in range(4)]
+    links.send(wo_ref, outw.at[w], mate, out_mate[3])
+    tokens_out[n] = tok_pack[...]
+    qkvw[w] = pack[...]
+    outw[w] = wo_ref[...]
 
     for step in range(NEAR):
         links.land(tokens_out.at[from_z[step]], {"narrow": from_z[step]}, tok_slots[step])
@@ -577,7 +577,7 @@
 
 def mid_body(
     x_ref, dy_ref, gate_ref, tokens_ref, w_ref,
-    back_mid_out, back_exp_out, extra_out, grads_out,
+    back_mid_out, back_exp_out, extra_out, grads_out, expert_out,
     weights, hidden, graded, hidden_cat, graded_cat, act_cat, gate_cat, up_cat,
     rs_send, rs_recv, ext_send, ext_recv, sent, landed, local,
 ):
@@ -585,6 +585,7 @@
     w = lax.axis_index("wide")
     chip, core = w // 2, lax.rem(w, 2)
     to_z, from_z = places_of(n)
+    plane = plane_of(chip)
     links = Links(sent, landed, local)
     mate = {"wide": 2 * chip + 1 - core}
     slots, full = x_ref.shape
@@ -602,7 +603,7 @@
         for kind in range(3)
     ]
     links.waits = []
-    greet(to_z, [], chip, core, True)
+    greet(to_z, plane, chip, core, True)
 
     total = jnp.zeros((slots, 1), F32)
     for m in range(4):
@@ -687,6 +688,43 @@
         links.send(ext_send, ext_recv.at[step], {"narrow": to_z[step]}, ext_slots[step])
     acts_there = [to_mate(item.at[core], item) for item in (act_cat, gate_cat, up_cat)]
 
+    half = full // 2
+    expert_slots = {}
+
+    def weight_grad(left, right, kind, start_row):
+        left_rows = left[...].reshape(2 * slots, half)
+        for start, size in tiles:
+            cols = slice(start, start + size)
+            right_rows = right[:, :, cols].reshape(2 * slots, size)
+            weights[kind, start_row : start_row + half, cols] = cols_cols(
+                left_rows, right_rows
+            ).astype(BF)
+
+    def share_out(index, kind, start_row):
+        expert_slots[index] = [links.slot() for _ in range(NEAR)]
+
+        def block(owner):
+            first = pl.multiple_of(start_row + owner * rows_each, rows_each)
+            return weights.at[kind, pl.ds(first, rows_each), :]
+
+        for step in range(NEAR):
+            links.send(
+                block(plane[step]), expert_out.at[index, chip],
+                {"wide": 2 * plane[step] + core}, expert_slots[index][step],
+            )
+        links.move(block(chip), expert_out.at[index, chip])
+
+    graded_there()
+    for there in acts_there[:1]:
+        there()
+    weight_grad(graded_cat, act_cat, 0, 0)
+    share_out(0, 0, 0)
+    hidden_there()
+    for there in acts_there[1:]:
+        there()
+    weight_grad(hidden_cat, gate_cat, 0, half)
+    share_out(1, 0, half)
+
     activated = act_cat[core]
     exp_slots = [links.slot() for _ in range(NEAR)]
     for step in range(NEAR + 1):
@@ -701,18 +739,8 @@
         else:
             own_exp = block
 
-    hidden_there()
-    graded_there()
-    for there in acts_there:
-        there()
-    pairs = ((hidden_cat, gate_cat), (hidden_cat, up_cat), (graded_cat, act_cat))
-    for kind, (left, right) in enumerate(pairs):
-        left_rows = left[...].reshape(2 * slots, full // 2)
-        for start, size in tiles:
-            cols = slice(start, start + size)
-            right_rows = right[:, :, cols].reshape(2 * slots, size)
-            weights[kind, 0 : full // 2, cols] = cols_cols(left_rows, right_rows).astype(BF)
-        links.move(weights.at[kind, pl.ds(0, full // 2), :], grads_out.at[kind])
+    weight_grad(hidden_cat, up_cat, 1, 0)
+    links.move(weights.at[1, pl.ds(0, half), :], grads_out)
 
     for step in range(NEAR):
         links.land(ext_recv.at[step], {"narrow": from_z[step]}, ext_slots[step])
@@ -734,6 +762,12 @@
             )
             block = block + rs_recv[which, step].astype(F32)
         target[...] = block.astype(BF)
+    for index in range(2):
+        for step in range(NEAR):
+            links.land(
+                expert_out.at[index, plane[step]], {"wide": 2 * plane[step] + core},
+                expert_slots[index][step],
+            )
     links.finish()
 
 
@@ -753,10 +787,11 @@
             arr((slots, part_width), BF),
             arr((slots, part_width), BF),
             arr((slots, 128), BF),
-            arr((3, full // 2, hidden_width), BF),
+            arr((full // 2, hidden_width), BF),
+            arr((2, 4, rows_each, hidden_width), BF),
         ),
         in_specs=[vmem] * 4 + [hbm],
-        out_specs=(vmem, vmem, vmem, hbm),
+        out_specs=(vmem, vmem, vmem, hbm, hbm),
         scratch_shapes=[
             pltpu.VMEM((3, full, hidden_width), BF),
             pltpu.VMEM((slots, full), BF),
@@ -838,17 +873,14 @@
         own.wait()
         return target[...]
 
-    expert_slots = {}
-    for kind in (2, 0, 1):
-        expert_slots[kind] = [links.slot() for _ in range(NEAR)]
-        for step in range(NEAR):
-            block = pl.ds(pl.multiple_of(plane[step] * rows_each, rows_each), rows_each)
-            links.send(
-                moved_ref.at[kind, block, :], expert_out.at[kind, chip], at_plane(plane[step]),
-                expert_slots[kind][step],
-            )
-        block = pl.ds(pl.multiple_of(chip * rows_each, rows_each), rows_each)
-        links.move(moved_ref.at[kind, block, :], expert_out.at[kind, chip])
+    expert_slots = [links.slot() for _ in range(NEAR)]
+    for step in range(NEAR):
+        block = pl.ds(pl.multiple_of(plane[step] * rows_each, rows_each), rows_each)
+        links.send(
+            moved_ref.at[block, :], expert_out.at[chip], at_plane(plane[step]), expert_slots[step]
+        )
+    block = pl.ds(pl.multiple_of(chip * rows_each, rows_each), rows_each)
+    links.move(moved_ref.at[block, :], expert_out.at[chip])
 
     def to_mate(source, target):
         slot = links.slot()
@@ -1063,17 +1095,14 @@
         summed = summed + proj_recv[step].astype(F32)
     for part, target in enumerate((grad_q_out, grad_k_out, grad_v_out, grad_o_out)):
         target[...] = summed[:, part * 512 : (part + 1) * 512]
-    for kind in (2, 0, 1):
-        for step in range(NEAR):
-            links.land(
-                expert_out.at[kind, plane[step]], at_plane(plane[step]), expert_slots[kind][step]
-            )
+    for step in range(NEAR):
+        links.land(expert_out.at[plane[step]], at_plane(plane[step]), expert_slots[step])
     links.finish()
 
 
 def tail_call(*args):
     slots, part_width = args[0].shape
-    half, hidden_width = args[3].shape[1:]
+    half, hidden_width = args[3].shape
     token_count = args[9].shape[0]
     full, rows_each = 2 * half, half // 4
     vmem = pl.BlockSpec(memory_space=pltpu.VMEM)
@@ -1094,7 +1123,7 @@
             arr((rows_each, part_width), F32),
             arr((8, part_width), F32),
             arr((8, full), F32),
-            arr((3, 4, rows_each, hidden_width), BF),
+            arr((4, rows_each, hidden_width), BF),
         ),
         in_specs=[vmem] * 3 + [hbm] + [vmem] * 12 + [hbm] * 2,
         out_specs=(vmem,) * 8 + (hbm,),
@@ -1413,7 +1442,7 @@
         jnp.pad(w_router, ((0, 0), (0, 128 - EXPERTS))), moved, table, table.T,
         jnp.tile(freqs, 2)[None, :],
     )
-    back_mid, back_exp, back_ext, grads = mid_call(
+    back_mid, back_exp, back_ext, grads, early_experts = mid_call(
         slot_mid, slot_grad, slot_gate, token_parts, expert_w
     )
     (
@@ -1423,7 +1452,8 @@
         token_parts, qkv, probs, attended, rope, hidden_first, in_w, out_w,
     )
     gate_out, up_out, down_out = (
-        jnp.transpose(experts[kind], (1, 0, 2)).astype(F32) for kind in range(3)
+        jnp.transpose(item, (1, 0, 2)).astype(F32)
+        for item in (early_experts[1], experts, early_experts[0])
     )
     router = lax.dynamic_slice_in_dim(
         router[:EXPERTS], lax.axis_index("wide") * rows_each, rows_each, 1

time: 572 us -> 491 us (0.86)
  Pallas kernels: 514 us -> 442 us
  other arithmetic: 15.6 us -> 8.64 us
    pallas_call x1, Pallas kernels: 175 us -> 112 us  [tail_call(): pl.pallas_call(tail_body, out_shape=(arr(own, BF), arr(own, F32), arr((ro...]
    pallas_call x1, Pallas kernels: 221 us -> 212 us  [front_call(): pl.pallas_call(front_body, out_shape=(arr((8, rows_each, 1664), BF), arr(...]
    convert_element_type x1 -> x2, other arithmetic: 10.1 us -> 3.12 us  [per_device(): jnp.transpose(item, (1, 0, 2)).astype(F32)]
    unnamed x41 -> x39, local copies, waits for them, and re-layouts: 26.9 us -> 24.1 us
where the time goes in v4:
time: 491 us; the launch traced here: 485 us
  Pallas kernels  442 us (90%)
  local copies, waits for them, and re-layouts  33.3 us (7%)
  other arithmetic  8.64 us (2%)
    pallas_call x1, Pallas kernels, front_call(): pl.pallas_call(front_body, out_shape=(arr((8, rows_each, 1664), BF), arr(...  212 us
    pallas_call x1, Pallas kernels, mid_call(): pl.pallas_call(mid_body, out_shape=(arr((slots, part_width), BF), arr((sl...  117 us
    pallas_call x1, Pallas kernels, tail_call(): pl.pallas_call(tail_body, out_shape=(arr(own, BF), arr(own, F32), arr((ro...  112 us
    unnamed x39, local copies, waits for them, and re-layouts  24.1 us

profile of v4, /device:TPU:0, one launch (start us, length us, event | category | flops | bytes accessed | tf_op | source)
XLA Modules:
  0.0 485.1 jit_solution(13784433037969620600)
XLA Ops:
  0.6 0.8 slice_bitcast_fusion
  1.4 0.8 select_reduce_fusion
  2.2 0.9 stack.35.rows_ref
  3.0 0.0 copy-start.7
  3.0 0.8 copy.69
  3.8 0.0 copy-start
  3.8 3.6 copy_bitcast_fusion
  7.4 0.0 copy-done.7
  7.4 0.0 copy-done
  7.4 0.3 copy.76
  7.8 0.0 copy-start.9
  7.8 0.0 copy-start.10
  7.8 0.0 copy-start.11
  7.8 4.1 pad_maximum_fusion.moved_ref
  11.9 0.0 copy-done.9
  11.9 0.1 copy.65
  12.1 0.6 pad.4.router_ref
  12.7 0.0 copy-done.10
  12.7 0.0 copy-done.11
  12.8 0.6 pad_maximum_fusion.1.gains_ref
  13.4 0.6 broadcast_in_dim_tile.3.freq_ref
  14.0 212.5 %front.1 = (bf16[8,256,1664]{2,1,0:T(8,128)(2,1)}, bf16[8,256,512]{2,1,0:T(8,128)(2,1)}, bf16[3,4,2,256,1408]{4,3,2,1,0:T(8,128)(2,1)}, bf16[576,2048]{1,0:T(8,1...) custom-call(bf16[256,512]{1,0:T(8,128)(2,1)} %tok_ref.3, ...), custom_call_target="tpu_custom_call" | custom-call | flops 6000000000 | bytes 60000000 | tf_op jit(solution)/shard_map/front/pallas_call | solution.py:519
  226.4 117.5 %mid.1 = (bf16[576,512]{1,0:T(8,128)(2,1)}, bf16[576,512]{1,0:T(8,128)(2,1)}, bf16[576,128]{1,0:T(8,128)(2,1)}, bf16[1024,1408]{1,0:T(8,128)(2,1)}, bf16[2,4,256,1408]{3,2,1,0:T(8,128)(2,1)}) custom-call(bf16[576,2048]{1,0:T(8,128)(2,1)} %get-tuple-element.41.x_ref, bf16[576,2048]{1,0:T(8,128)(2,1)} %get-tuple-element.42.dy_ref, ...), custom_call_target="tpu_custom_call" | custom-call | flops 30000001024 | bytes 40000000 | tf_op jit(solution)/shard_map/mid/pallas_call | solution.py:784
  343.9 112.1 %tail.1 = (bf16[256,512]{1,0:T(8,128)(2,1)}, f32[256,512]{1,0:T(8,128)}, f32[256,512]{1,0:T(8,128)}, f32[256,512]{1,0:T(8,128)}, f32[256,512]{1,0:T(8,128)}, /*i...) custom-call(bf16[576,512]{1,0:T(8,128)(2,1)} %get-tuple-element.46.mid_ref, ...), custom_call_target="tpu_custom_call" | custom-call | flops 6000000000 | bytes 60000000 | tf_op jit(solution)/shard_map/tail/pallas_call | solution.py:1115
  456.1 0.0 slice-start
  456.1 2.3 convert_bitcast_fusion.2
  458.4 0.0 slice-start.1
  458.4 6.5 %copy.71 = f32[256,4,1408]{2,1,0:T(4,128)} copy(f32[256,4,1408]{2,0,1:T(8,128)S(1)} %convert_bitcast_fusion.2) | data formatting | bytes 11534336
  464.9 0.0 slice-done
  464.9 0.0 slice-done.1
  464.9 0.8 convert_bitcast_fusion
  465.7 6.2 %copy.70 = f32[256,4,1408]{2,1,0:T(4,128)} copy(f32[256,4,1408]{2,0,1:T(8,128)S(1)} %get-tuple-element.119) | data formatting | bytes 11534336
  471.9 6.2 %copy.72 = f32[256,4,1408]{2,1,0:T(4,128)} copy(f32[256,4,1408]{2,0,1:T(8,128)S(1)} %get-tuple-element.118) | data formatting | bytes 11534336
  478.2 0.0 copy-done.8
  478.2 0.6 dynamic-slice_bitcast_fusion
  478.8 1.4 fusion
  480.2 0.0 copy-done.6
  480.2 0.7 copy.83
  480.9 0.0 copy-done.5
  480.9 0.8 copy.84
  481.7 0.0 copy-done.4
  481.7 0.8 copy.85
  482.5 0.0 copy-done.3
  482.5 0.8 copy.86
  483.3 0.0 copy-done.2
  483.3 0.8 copy.87
  484.1 0.0 copy-done.1
  484.1 0.8 copy.88
  (13 shorter events, 0.0 us)
Async XLA Ops:
  3.0 4.4 copy-start.7
  3.8 3.6 copy-start
  7.8 4.2 copy-start.9
  7.8 5.0 %copy-start.10 = (bf16[512]{0:T(512)(128)(2,1)S(1)}, bf16[512]{0:T(512)(128)(2,1)}, u32[]{:S(2)}) copy-start(bf16[512]{0:T(512)(128)(2,1)} %param.17) | copy-start | bytes 3076
  7.8 5.0 %copy-start.11 = (bf16[512]{0:T(512)(128)(2,1)S(1)}, bf16[512]{0:T(512)(128)(2,1)}, u32[]{:S(2)}) copy-start(bf16[512]{0:T(512)(128)(2,1)} %param.22) | copy-start | bytes 3076
  456.1 8.8 %slice-start = ((s8[5767168]{0:T(1024)(128)(4,1)}), s8[4194304]{0:T(1024)(128)(4,1)S(1)}, s32[]{:S(2)}) async-start(s8[5767168]{0:T(1024)(128)(4,1)} %bitcast.38), calls=%async_computation | async-start | bytes 8388608
  458.4 6.5 %slice-start.1 = ((s8[5767168]{0:T(1024)(128)(4,1)}), s8[1572864]{0:T(1024)(128)(4,1)S(1)}, s32[]{:S(2)}) async-start(s8[5767168]{0:T(1024)(128)(4,1)} %bitcast.38), calls=%async_computation.1 | async-start | bytes 3145728
  471.9 6.3 %copy-start.8 = (f32[8,2048]{1,0:T(8,128)S(1)}, f32[8,2048]{1,0:T(8,128)}, u32[]{:S(2)}) copy-start(f32[8,2048]{1,0:T(8,128)} %get-tuple-element.67) | copy-start | bytes 196612
  471.9 8.3 %copy-start.6 = (bf16[256,512]{1,0:T(8,128)(2,1)S(1)}, bf16[256,512]{1,0:T(8,128)(2,1)}, u32[]{:S(2)}) copy-start(bf16[256,512]{1,0:T(8,128)(2,1)} %get-tuple-element.138) | copy-start | bytes 786436
  471.9 9.0 %copy-start.5 = (f32[256,512]{1,0:T(8,128)S(1)}, f32[256,512]{1,0:T(8,128)}, u32[]{:S(2)}) copy-start(f32[256,512]{1,0:T(8,128)} %get-tuple-element.139) | copy-start | bytes 1572868
  471.9 9.8 %copy-start.4 = (f32[256,512]{1,0:T(8,128)S(1)}, f32[256,512]{1,0:T(8,128)}, u32[]{:S(2)}) copy-start(f32[256,512]{1,0:T(8,128)} %get-tuple-element.141) | copy-start | bytes 1572868
  478.2 4.3 copy-start.3
  478.2 5.1 %copy-start.2 = (f32[256,512]{1,0:T(8,128)S(1)}, f32[256,512]{1,0:T(8,128)}, u32[]{:S(2)}) copy-start(f32[256,512]{1,0:T(8,128)} %get-tuple-element.143) | copy-start | bytes 1572868
  478.2 5.9 %copy-start.1 = (f32[256,512]{1,0:T(8,128)S(1)}, f32[256,512]{1,0:T(8,128)}, u32[]{:S(2)}) copy-start(f32[256,512]{1,0:T(8,128)} %get-tuple-element.144) | copy-start | bytes 1572868
